TPU v7x, 32 devices: a whole 2x2x4 slice. The times are simulated.
32 devices in a mesh: group: 2 (over x), src: 16 (over z, y, core).
Axes of the slice: x: 2, y: 2, z: 4, core: 2. Of those that a mesh axis runs over, the one named last changes fastest.
Arguments:
- rcv_points: float32 [3, 4096], P(None, ('group', 'src')), parts along dimension 1, may hold values from -1 to 1
- rcv_normals: float32 [3, 4096], P(None, ('group', 'src')), parts along dimension 1, may hold values from -4 to 4
- left_modes: float32 [8, 4096], P(None, ('group', 'src')), parts along dimension 1, may hold values from -5 to 5
- vertices: float32 [3, 2048], P(None, ('group', 'src')), parts along dimension 1, may hold values from -1 to 1
- connect: int32 [2, 4096], P(None, ('group', 'src')), parts along dimension 1, may hold values from 0 to 1023, as said below
- right_modes: float32 [8, 4096], P(None, ('group', 'src')), parts along dimension 1, may hold values from -0.125 to 0.125
- mode_weights: float32 [16], P('group'), parts along dimension 0, may hold values from 0.25 to 1
Outputs:
- rcv_grad: float32 [6, 4096], P(None, ('group', 'src')), parts along dimension 1
- vert_grad: float32 [3, 2048], P(None, ('group', 'src')), parts along dimension 1
There are 2 independent parts, one for each index of `group`. A program takes and returns all parts, laid end to end along the dimension named above; each array names one. Nothing has to cross between parts.
Inputs may be any that keep to these rules, and one draw needn't show every extreme that they name: `connect`: a panel's first vertex is one of the 64 vertices held at the same index of src as the panel, and its second vertex is the next vertex number.
All inputs are finite; a program needn't handle non-finite values.
Results may differ from a plain program's by a relative error of at most 0.0003.
Values sent between devices are 32-bit elements; how exact they have to be, the bound alone decides.
No kernel may reach another device: no remote copies, remote signals or barrier semaphores. Data moves between devices by JAX's collectives and lax.ppermute only.
A program may use at most 64 MiB of HBM per device.

v0:
```python
import math

import jax
import jax.numpy as jnp
from jax import lax
from jax.sharding import PartitionSpec as P

core_term = 0.05
inverse_four_pi = 0.25 / math.pi


def shifted(value, axis, steps):
    count = lax.axis_size(axis)
    leading, last = (max(0, -steps), min(count, count - steps))
    return lax.ppermute(value, axis, [(source, source + steps) for source in range(leading, last)])


def lift_points(raw):
    return jnp.stack([raw[0], raw[1], 0.5 + 0.2 * raw[2]])


def place_points(raw):
    return jnp.stack([raw[0], raw[1], 0.2 * raw[2]])


def tile_energy(points, normals, first_end, second_end, coefficient):
    rel_first = points[:, None, :] - first_end[:, :, None]
    rel_second = points[:, None, :] - second_end[:, :, None]
    segment = (second_end - first_end)[:, :, None]
    cross_x = rel_first[1] * rel_second[2] - rel_first[2] * rel_second[1]
    cross_y = rel_first[2] * rel_second[0] - rel_first[0] * rel_second[2]
    cross_z = rel_first[0] * rel_second[1] - rel_first[1] * rel_second[0]
    cross_sq = cross_x * cross_x + cross_y * cross_y + cross_z * cross_z
    dist_first = jnp.sqrt(jnp.sum(rel_first * rel_first, axis=0))
    dist_second = jnp.sqrt(jnp.sum(rel_second * rel_second, axis=0))
    along_term = jnp.sum(segment * (rel_first / dist_first - rel_second / dist_second), axis=0)
    span_sq = jnp.sum(segment * segment, axis=0)
    denominator = cross_sq + core_term * (span_sq + 1.0)
    normal_term = (
        normals[0][None, :] * cross_x
        + normals[1][None, :] * cross_y
        + normals[2][None, :] * cross_z
    )
    influence = inverse_four_pi * normal_term * along_term / denominator
    return jnp.sum(coefficient * influence)


def tile_gradients(points, normals, first_end, second_end, coefficient):
    return jax.grad(tile_energy, argnums=(0, 1, 2, 3))(
        points, normals, first_end, second_end, coefficient
    )


def on_device(rcv_points, rcv_normals, left_modes, vertices, connect, right_modes, mode_weights):
    own_count = vertices.shape[1]
    next_first = shifted(vertices[:, :1], "src", -1)
    extended = jnp.concatenate([vertices, next_first], axis=1)
    places = place_points(extended)
    base_vertex = lax.axis_index("src") * own_count
    local_first = connect[0] - base_vertex
    local_second = local_first + 1
    first_end = places[:, local_first]
    second_end = places[:, local_second]
    points = lift_points(rcv_points)
    chain_scale = jnp.array([1.0, 1.0, 0.2], dtype=jnp.float32)[:, None]
    weighted = right_modes * mode_weights[:, None]
    receiver_count = rcv_points.shape[1] * lax.axis_size("src")
    source_count = connect.shape[1]
    start_totals = (
        jnp.zeros((3, source_count), jnp.float32),
        jnp.zeros((3, source_count), jnp.float32),
        jnp.zeros((6, receiver_count), jnp.float32),
    )
    shard_points = lax.all_gather(points, "src", axis=1, tiled=True)
    shard_normals = lax.all_gather(rcv_normals, "src", axis=1, tiled=True)
    shard_left = lax.all_gather(left_modes, "src", axis=1, tiled=True)
    row_count = shard_points.shape[1]
    width_rows = math.gcd(row_count, 2048)

    def advance(number, inner):
        sum_first, sum_second, receiver_buffer = inner
        local_start = number * width_rows
        block_points = lax.dynamic_slice_in_dim(shard_points, local_start, width_rows, 1)
        block_normals = lax.dynamic_slice_in_dim(shard_normals, local_start, width_rows, 1)
        block_left = lax.dynamic_slice_in_dim(shard_left, local_start, width_rows, 1)
        coefficient = jnp.einsum("mj,mi->ji", weighted, block_left, precision=lax.Precision.HIGHEST)
        grads = tile_gradients(block_points, block_normals, first_end, second_end, coefficient)
        rows_out = jnp.concatenate([grads[0] * chain_scale, grads[1]], axis=0)
        receiver_buffer = lax.dynamic_update_slice_in_dim(receiver_buffer, rows_out, local_start, 1)
        return (sum_first + grads[2], sum_second + grads[3], receiver_buffer)

    sum_first, sum_second, receiver_buffer = lax.fori_loop(
        0, row_count // width_rows, advance, start_totals
    )
    rcv_grad = lax.psum_scatter(receiver_buffer, "src", scatter_dimension=1, tiled=True)
    vertex_partial = jnp.zeros((3, own_count + 1), jnp.float32)
    vertex_partial = (
        vertex_partial.at[:, local_first].add(sum_first).at[:, local_second].add(sum_second)
    )
    incoming = shifted(vertex_partial[:, own_count:], "src", 1)
    own_part = vertex_partial[:, :own_count]
    own_part = jnp.concatenate([own_part[:, :1] + incoming, own_part[:, 1:]], axis=1)
    vert_grad = own_part * chain_scale
    return (rcv_grad, vert_grad)


def solution(mesh):
    in_specs = (
        P(None, ("group", "src")),
        P(None, ("group", "src")),
        P(None, ("group", "src")),
        P(None, ("group", "src")),
        P(None, ("group", "src")),
        P(None, ("group", "src")),
        P("group"),
    )
    out_specs = (P(None, ("group", "src")), P(None, ("group", "src")))
    return jax.shard_map(
        on_device, mesh=mesh, in_specs=in_specs, out_specs=out_specs, check_vma=False
    )
```

profile of v0, /device:TPU:0, one launch (start us, length us, event | category | flops | bytes accessed | tf_op | source)
XLA Modules:
  0.0 154.4 jit_solution(849035136935577808)
XLA Ops:
  7.2 1.3 collective-permute-start
  8.5 0.7 multiply_add_fusion.1
  9.2 0.7 slice.81
  9.9 23.8 %all_gather.10 = f32[3,2048]{1,0:T(4,128)S(1)} all-gather(f32[3,128]{1,0:T(4,128)S(1)} %pad_maximum_fusion.3), channel_id=1, replica_groups=mesh['group'=2,'src'=16] {'src'}, dimensions={1}, use_global_device_ids=true | all-gather | bytes 26112 | tf_op jit(solution)/shard_map/all_gather | solution.py:74
  33.7 17.7 %all_gather.9 = f32[3,2048]{1,0:T(4,128)S(1)} all-gather(f32[3,128]{1,0:T(4,128)} %param.9), channel_id=1, replica_groups=mesh['group'=2,'src'=16] {'src'}, dimensions={1}, use_global_device_ids=true | all-gather | bytes 26112 | tf_op jit(solution)/shard_map/all_gather | solution.py:75
  51.4 19.2 %all_gather.11 = f32[8,2048]{1,0:T(8,128)S(1)} all-gather(f32[8,128]{1,0:T(8,128)} %param.10), channel_id=1, replica_groups=mesh['group'=2,'src'=16] {'src'}, dimensions={1}, use_global_device_ids=true | all-gather | bytes 69632 | tf_op jit(solution)/shard_map/all_gather | solution.py:76
  70.6 0.7 fusion.24
  71.3 0.8 pad_maximum_fusion.1
  72.2 0.6 gather_fusion.1
  72.9 0.7 gather_fusion
  73.7 0.8 fusion.15
  75.3 1.8 %divide_multiply_fusion.1 = (f32[128,2048]{1,0:T(8,128)S(1)}, f32[128,2048]{1,0:T(8,128)S(1)}, f32[128,2048]{1,0:T(8,128)S(1)}, f32[128,2048]{1,0:T(8,128)S(1)},...) fusion(f32[128]{0:T(128)S(1)} %add_multiply_fusion.2, f32[2048]{0:T(1024)S(1)} %bitcast.136, ...), kind=kOutput, calls=%fused_computation.109 | convolution fusion | flops 31196160 | bytes 13726240 | tf_op jit(solution)/shard_map/while/body/eval_jaxpr/mj,mi->ji/dot_general | solution.py:86
  77.1 2.5 %multiply_reduce_fusion = (f32[3,128]{1,0:T(4,128)S(1)}, f32[128,2048]{1,0:T(8,128)S(1)}, f32[128,2048]{1,0:T(8,128)S(1)}, f32[128,2048]{1,0:T(8,128)S(1)}) fusion(f32[128,2048]{1,0:T(8,128)S(1)} %get-tuple-element.62, f32[128,2048]{1,0:T(8,128)S(1)} %get-tuple-element.92, f32[3,128]{1,0:T(4,128)S(1)} %bitcast.127, f32[128,2048]{1,0:T(8,128)S(1)} %get-tuple-element.94, ...), kind=kLoop, calls=%fused_computation.36 | loop fusion | flops 12582528 | bytes 8419328 | tf_op jit(solution)/shard_map/while/body/eval_jaxpr/transpose(jvp())/reduce_sum | solution.py:36
  80.6 2.0 %multiply_bitcast_fusion.5 = (f32[1,128,2048]{2,1,0:T(8,128)}, f32[128,2048]{1,0:T(8,128)}, f32[128,2048]{1,0:T(8,128)S(1)}) fusion(f32[3,128,2048]{2,1,0:T(8,128)S(1)} %get-tuple-element.95, f32[128,2048]{1,0:T(8,128)S(1)} %get-tuple-element.67, f32[128,2048]{1,0:T(8,128)S(1)} %get-tuple-element.54, f32[2048]{0:T(1024)S(1)} %broadcast_multiply_fusion.2, ...), kind=kLoop, calls=%fused_computation.57 | loop fusion | flops 2359296 | bytes 9445376 | tf_op jit(solution)/shard_map/while/body/eval_jaxpr/transpose(jvp())/broadcast_in_dim | solution.py:32
  82.6 2.2 %multiply_bitcast_fusion.3 = (f32[1,128,2048]{2,1,0:T(8,128)S(1)}, f32[128,2048]{1,0:T(8,128)}, f32[1,128,2048]{2,1,0:T(8,128)S(1)}, f32[128,2048]{1,0:T(8,128)}...) fusion(f32[3,128,2048]{2,1,0:T(8,128)S(1)} %get-tuple-element.95, f32[128,2048]{1,0:T(8,128)S(1)} %get-tuple-element.66, ...), kind=kLoop, calls=%fused_computation.55 | loop fusion | flops 5236736 | bytes 11575296 | tf_op jit(solution)/shard_map/while/body/eval_jaxpr/transpose(jvp())/broadcast_in_dim | solution.py:31
  84.9 4.8 %multiply_bitcast_fusion.11 = (f32[1,128,2048]{2,1,0:T(8,128)S(1)}, f32[1,128,2048]{2,1,0:T(8,128)S(1)}, f32[1,128,2048]{2,1,0:T(8,128)S(1)}, f32[1,128,2048]{2,...) fusion(f32[128,2048]{1,0:T(8,128)} %get-tuple-element.56, ...), kind=kLoop, calls=%fused_computation.65 | loop fusion | flops 3145728 | bytes 18874368 | tf_op jit(solution)/shard_map/while/body/eval_jaxpr/transpose(jvp())/broadcast_in_dim | solution.py:32
  89.7 3.4 %fusion.27 = (f32[3,128]{1,0:T(4,128)S(1)}, f32[3,2048]{1,0:T(4,128)S(1)}) fusion(f32[1,128,2048]{2,1,0:T(8,128)} %get-tuple-element.88, f32[1,128,2048]{2,1,0:T(8,128)S(1)} %get-tuple-element.70, f32[1,128,2048]{2,1,0:T(8,128)} %get-tuple-element.89, f32[1,128,2048]{2,1,0:T(8,128)S(1)} %get-tuple-element.58, f32[1,128,2048]{2,1,0:T(8,128)} %get-tuple-element.90, ...), kind=kLoop, calls=%fused_computation.111 | loop fusion | flops 11003520 | bytes 9490944 | tf_op jit(solution)/shard_map/while/body/eval_jaxpr/transpose(jvp())/reduce_sum | solution.py:27
  93.1 1.9 %fusion.26 = (f32[3,128]{1,0:T(4,128)S(1)}, f32[3,2048]{1,0:T(4,128)S(1)}) fusion(f32[1,128,2048]{2,1,0:T(8,128)S(1)} %get-tuple-element.84, f32[1,128,2048]{2,1,0:T(8,128)S(1)} %get-tuple-element.85, f32[1,128,2048]{2,1,0:T(8,128)S(1)} %get-tuple-element.86, f32[1,128,2048]{2,1,0:T(8,128)S(1)} %copy-done, f32[1,128,2048]{2,1,0:T(8,128)S(1)} %get-tuple-element.73, ...), kind=kLoop, calls=%fused_computation.110 | loop fusion | flops 11789952 | bytes 9490944 | tf_op jit(solution)/shard_map/while/body/eval_jaxpr/transpose(jvp())/reduce_sum | solution.py:28
  95.2 1.0 scatter_custom_fusion
  96.2 1.2 scatter_fusion
  98.3 2.2 %collective-permute-start.1 = (f32[3,1]{0,1:T(1,128)S(1)}, f32[3,1]{0,1:T(1,128)S(1)}, u32[]{:S(2)}, u32[]{:S(2)}) collective-permute-start(f32[3,1]{0,1:T(1,128)S(1)} %slice.108), channel_id=1, source_target_pairs={{0,1},{1,2},{2,3},{3,4},{4,5},{5,6},{6,7},{7,8},{8,9},{9,10},{10,1... | collective-permute-start | bytes 44 | tf_op jit(solution)/shard_map/ppermute | solution.py:15
  100.6 0.7 collective-permute-done.1
  101.4 0.7 maximum_multiply_fusion
  102.1 45.5 %reduce-scatter.2.cloned.1.call-done = f32[6,128]{1,0:T(8,128)} async-done(((f32[6,2048]{1,0:T(8,128)}), f32[6,128]{1,0:T(8,128)}) %reduce-scatter.2.cloned.1.call-update) | async-done | bytes 3088 | tf_op jit(solution)/shard_map/reduce_scatter | solution.py:95
  (41 shorter events, 3.2 us)
Async XLA Ops:
  7.2 140.4 %reduce-scatter.2.cloned.1.call-start = ((), (), s32[]{:S(2)}) async-start(), calls=%async_computation.1 | async-start | bytes 69632 | tf_op jit(solution)/shard_map/reduce_scatter | solution.py:95
  7.2 64.1 %collective-permute-start = (f32[3,1]{1,0:T(4,128)}, f32[3,1]{1,0:T(4,128)S(1)}, u32[]{:S(2)}, u32[]{:S(2)}) collective-permute-start(f32[3,1]{1,0:T(4,128)} %bitcast.141), channel_id=1, source_target_pairs={{1,0},{2,1},{3,2},{4,3},{5,4},{6,5},{7,6},{8,7},{9,8},{10,9},{11,1... | collective-permute-start | bytes 44 | tf_op jit(solution)/shard_map/ppermute | solution.py:15
  74.5 0.7 copy-start.2
  74.5 0.7 copy-start.3
  89.7 3.4 %copy-start = (f32[1,128,2048]{2,1,0:T(8,128)S(1)}, f32[1,128,2048]{2,1,0:T(8,128)}, u32[]{:S(2)}) copy-start(f32[1,128,2048]{2,1,0:T(8,128)} %get-tuple-element.87) | copy-start | bytes 3145732
  93.1 4.4 %copy-start.1 = (f32[3]{0:T(128)S(1)}, f32[3]{0:T(128)}, u32[]{:S(2)}) copy-start(f32[3]{0:T(128)} %constant.34.clone) | copy-start | bytes 40
  98.3 3.1 %collective-permute-start.1 = (f32[3,1]{0,1:T(1,128)S(1)}, f32[3,1]{0,1:T(1,128)S(1)}, u32[]{:S(2)}, u32[]{:S(2)}) collective-permute-start(f32[3,1]{0,1:T(1,128)S(1)} %slice.108), channel_id=1, source_target_pairs={{0,1},{1,2},{2,3},{3,4},{4,5},{5,6},{6,7},{7,8},{8,9},{9,10},{10,1... | collective-permute-start | bytes 44 | tf_op jit(solution)/shard_map/ppermute | solution.py:15
Sparse Core Ops, SparseCore 0:
  98.4 49.1 reduce-scatter.1
where the time goes:
time: 155 us; the launch traced here: 154 us
  blocking collectives  60.7 us (39%)
  waiting for transfers between devices  46.2 us (30%)
  other arithmetic  25.1 us (16%)
  between operations  14.3 us (9%)
  starting transfers between devices  3.58 us (2%)
  local copies, waits for them, and re-layouts  2.68 us (2%)
  matrix products  1.85 us (1%)
    reduce_scatter x1, waiting for transfers between devices, on_device(): lax.psum_scatter(receiver_buffer, 'src', scatter_dimension=1, tiled=True)  45.5 us
    all_gather x1, blocking collectives, on_device(): shard_points = lax.all_gather(points, 'src', axis=1, tiled=True)  23.8 us
    all_gather x1, blocking collectives, on_device(): shard_left = lax.all_gather(left_modes, 'src', axis=1, tiled=True)  19.2 us
    all_gather x1, blocking collectives, on_device(): shard_normals = lax.all_gather(rcv_normals, 'src', axis=1, tiled=True)  17.7 us
    broadcast_in_dim x2, other arithmetic, tile_energy(): cross_z = rel_first[0] * rel_second[1] - rel_first[1] * rel_second[0]  6.79 us
    ppermute x2, starting transfers between devices, shifted(): lax.ppermute(value, axis, [(source, source + steps) for source in range(l...  3.54 us
    reduce_sum x1, other arithmetic, tile_energy(): rel_first = points[:, None, :] - first_end[:, :, None]  3.41 us
  transfers between devices with their start and end apart: 3, of which 2 were waited for; matrix products, arithmetic and copies ran while one was open for 2% of the time, Pallas kernels for 0%

commit v1 on v0

v1 whole, which is shorter than its diff:
```python
import functools
import math

import jax
import jax.numpy as jnp
from jax import lax
from jax.experimental import pallas as pl
from jax.experimental.pallas import tpu as pltpu
from jax.sharding import PartitionSpec as P

core_term = 0.05
inverse_four_pi = 0.25 / math.pi

LANES = 128
ROWS = 24
REC_ROWS = 14
SEG_ROWS = 11


def exchange_masks(count):
    masks = []
    step = count // 2
    while step >= 1:
        masks.append(step)
        step //= 2
    return masks


def position_of(mask_value, masks):
    place = 0
    for bit, step in enumerate(masks):
        place = place + (lax.shift_right_logical(mask_value, step.bit_length() - 1) & 1) * (1 << bit)
    return place


def split2(value):
    high = value.astype(jnp.bfloat16)
    low = (value - high.astype(jnp.float32)).astype(jnp.bfloat16)
    return high, low


def dot_nt(left, right):
    return lax.dot_general(
        left, right, (((1,), (1,)), ((), ())), preferred_element_type=jnp.float32
    )


def contract(values, features):
    vh, vl = split2(values)
    fh, fl = split2(features)
    return dot_nt(vh, fh) + (dot_nt(vh, fl) + dot_nt(vl, fh))


def pair_terms(normal_cross, dist_sq, along, span, scale, want_span):
    second_sq = dist_sq - 2.0 * along + span
    inv_first = lax.rsqrt(dist_sq)
    inv_second = lax.rsqrt(second_sq)
    inv_den = 1.0 / (span * dist_sq + (core_term * span + core_term) - along * along)
    other = along - span
    part_first = along * inv_first
    part_second = other * inv_second
    line = part_first - part_second
    scaled = scale * inv_den
    by_normal = scaled * line
    by_line = scaled * normal_cross
    by_den2 = -2.0 * (by_normal * normal_cross) * inv_den
    cube_first = part_first * (inv_first * inv_first)
    cube_second = part_second * (inv_second * inv_second)
    by_dist2 = by_line * (cube_second - cube_first) + by_den2 * span
    by_along = by_line * ((inv_first - inv_second) - cube_second) - by_den2 * along
    if not want_span:
        return by_normal, by_dist2, by_along
    by_span2 = by_line * (2.0 * inv_second + cube_second) + by_den2 * (dist_sq + core_term)
    return by_normal, by_dist2, by_along, by_span2


def kernel(count, own_seg, gathered_ref, rcv_out, vert_out, seg_ref, own_rec, own_segment):
    masks = exchange_masks(count)
    me = lax.axis_index("src")
    lane = lax.broadcasted_iota(jnp.int32, (1, LANES), 1)
    low_half = lane < own_seg

    def block_start(device):
        return pl.multiple_of(position_of(device ^ me, masks) * ROWS, 8)

    tiles = count // 2

    def fill(tile, carry):
        even = gathered_ref[pl.ds(block_start(2 * tile), ROWS), :][REC_ROWS : REC_ROWS + 6]
        odd = gathered_ref[pl.ds(block_start(2 * tile + 1), ROWS), :][REC_ROWS : REC_ROWS + 6]
        first_rows = jnp.where(low_half, even, pltpu.roll(odd, own_seg, 1))
        last_rows = jnp.where(low_half, pltpu.roll(even, own_seg, 1), odd)
        seg_ref[tile, 0:6, :] = first_rows
        seg_ref[tile, 6:12, :] = last_rows
        return carry

    lax.fori_loop(0, tiles, fill, 0)

    def fill_next(tile, carry):
        here = pltpu.roll(seg_ref[tile, 0:3, :], LANES - 1, 1)
        after = pltpu.roll(seg_ref[(tile + 1) % tiles, 0:3, :], LANES - 1, 1)
        seg_ref[tile, 12:15, :] = jnp.where(lane == LANES - 1, after, here)
        seg_ref[tile, 15:16, :] = jnp.zeros((1, LANES), jnp.float32)
        return carry

    lax.fori_loop(0, tiles, fill_next, 0)

    own_block = gathered_ref[0:16, :]
    own_rec[...] = jnp.transpose(own_block)

    own_tile = me // 2
    mine = seg_ref[own_tile]
    mine = jnp.where(me % 2 == 0, mine, pltpu.roll(mine, own_seg, 1))
    before_tile = (me + count - 1) % count
    before = seg_ref[before_tile // 2]
    before = jnp.where(before_tile % 2 == 0, pltpu.roll(before, 1, 1), pltpu.roll(before, own_seg + 1, 1))
    row = lax.broadcasted_iota(jnp.int32, (16, LANES), 0)
    is_weight = (row >= 3) & (row < 11)
    before = jnp.where(is_weight & (me == 0), 0.0, before)
    mine = jnp.where(lane < own_seg, mine, before)
    own_segment[...] = jnp.transpose(mine)
    mine_rows = mine

    rec = own_rec[...]
    px, py, pz = rec[:, 0:1], rec[:, 1:2], rec[:, 2:3]
    nx, ny, nz = rec[:, 3:4], rec[:, 4:5], rec[:, 5:6]
    left = rec[:, 6:14]

    def first_pass(tile, carry):
        seg = seg_ref[tile]
        ax, ay, az = seg[0:1], seg[1:2], seg[2:3]
        weights = seg[3:11]
        sx, sy, sz = seg[12:13] - ax, seg[13:14] - ay, seg[14:15] - az
        span = sx * sx + sy * sy + sz * sz
        scale = inverse_four_pi * lax.dot_general(
            left, weights, (((1,), (0,)), ((), ())), precision=lax.Precision.HIGHEST,
            preferred_element_type=jnp.float32)
        rx, ry, rz = px - ax, py - ay, pz - az
        normal_cross = nx * (sy * rz - sz * ry) + ny * (sz * rx - sx * rz) + nz * (sx * ry - sy * rx)
        dist_sq = rx * rx + ry * ry + rz * rz
        along = sx * rx + sy * ry + sz * rz
        by_normal, by_dist2, by_along = pair_terms(normal_cross, dist_sq, along, span, scale, False)
        tx, ty, tz = sy * az - sz * ay, sz * ax - sx * az, sx * ay - sy * ax
        ones = jnp.ones_like(ax)
        sum_n, sum_a, sum_u = carry
        sum_n = sum_n + contract(by_normal, jnp.concatenate([sx, sy, sz, tx, ty, tz, ones, ones], 0))
        sum_a = sum_a + contract(by_dist2, jnp.concatenate([ones, ax, ay, az, ones, ones, ones, ones], 0))
        sum_u = sum_u + contract(by_along, jnp.concatenate([sx, sy, sz, ones, ones, ones, ones, ones], 0))
        return sum_n, sum_a, sum_u

    zeros = jnp.zeros((LANES, 8), jnp.float32)
    sum_n, sum_a, sum_u = lax.fori_loop(0, tiles, first_pass, (zeros, zeros, zeros))
    totals = jnp.transpose(jnp.concatenate([sum_n, sum_a, sum_u, zeros] + [jnp.zeros((LANES, 96), jnp.float32)], 1))
    gx, gy, gz = totals[0:1], totals[1:2], totals[2:3]
    hx, hy, hz = totals[3:4], totals[4:5], totals[5:6]
    a1, aex, aey, aez = totals[8:9], totals[9:10], totals[10:11], totals[11:12]
    ux, uy, uz = totals[16:17], totals[17:18], totals[18:19]
    qx, qy, qz = own_block[0:1], own_block[1:2], own_block[2:3]
    mx, my, mz = own_block[3:4], own_block[4:5], own_block[5:6]
    rcv_out[0:1, :] = my * gz - mz * gy + a1 * qx - aex + ux
    rcv_out[1:2, :] = mz * gx - mx * gz + a1 * qy - aey + uy
    rcv_out[2:3, :] = 0.2 * (mx * gy - my * gx + a1 * qz - aez + uz)
    rcv_out[3:4, :] = gy * qz - gz * qy - hx
    rcv_out[4:5, :] = gz * qx - gx * qz - hy
    rcv_out[5:6, :] = gx * qy - gy * qx - hz

    used = own_seg + 8
    cols = own_segment[...][0:used]
    ax, ay, az = cols[:, 0:1], cols[:, 1:2], cols[:, 2:3]
    weights = cols[:, 3:11]
    sx, sy, sz = cols[:, 12:13] - ax, cols[:, 13:14] - ay, cols[:, 14:15] - az
    span = sx * sx + sy * sy + sz * sz

    def second_pass(block, carry):
        rec_rows = gathered_ref[pl.ds(pl.multiple_of(block * ROWS, 8), 16), :]
        px, py, pz = rec_rows[0:1], rec_rows[1:2], rec_rows[2:3]
        nx, ny, nz = rec_rows[3:4], rec_rows[4:5], rec_rows[5:6]
        scale = inverse_four_pi * lax.dot_general(
            weights, rec_rows[6:14], (((1,), (0,)), ((), ())), precision=lax.Precision.HIGHEST,
            preferred_element_type=jnp.float32)
        rx, ry, rz = px - ax, py - ay, pz - az
        normal_cross = nx * (sy * rz - sz * ry) + ny * (sz * rx - sx * rz) + nz * (sx * ry - sy * rx)
        dist_sq = rx * rx + ry * ry + rz * rz
        along = sx * rx + sy * ry + sz * rz
        by_normal, by_dist2, by_along, by_span2 = pair_terms(normal_cross, dist_sq, along, span, scale, True)
        tx, ty, tz = py * nz - pz * ny, pz * nx - px * nz, px * ny - py * nx
        ones = jnp.ones_like(px)
        sum_n, sum_a, sum_u, sum_q = carry
        points_rows = jnp.concatenate([ones, px, py, pz, ones, ones, ones, ones], 0)
        sum_n = sum_n + contract(by_normal, jnp.concatenate([nx, ny, nz, tx, ty, tz, ones, ones], 0))
        sum_a = sum_a + contract(by_dist2, points_rows)
        sum_u = sum_u + contract(by_along, points_rows)
        sum_q = sum_q + by_span2
        return sum_n, sum_a, sum_u, sum_q

    zeros = jnp.zeros((used, 8), jnp.float32)
    sum_n, sum_a, sum_u, sum_q = lax.fori_loop(
        0, count, second_pass, (zeros, zeros, zeros, jnp.zeros((used, LANES), jnp.float32)))
    sum_q = jnp.sum(sum_q, axis=1, keepdims=True)
    totals = jnp.concatenate([sum_n, sum_a, sum_u, sum_q, jnp.zeros((used, LANES - 25), jnp.float32)], 1)
    totals = jnp.transpose(jnp.concatenate([totals, jnp.zeros((LANES - used, LANES), jnp.float32)], 0))
    gx, gy, gz = totals[0:1], totals[1:2], totals[2:3]
    hx, hy, hz = totals[3:4], totals[4:5], totals[5:6]
    a1, apx, apy, apz = totals[8:9], totals[9:10], totals[10:11], totals[11:12]
    u1, upx, upy, upz = totals[16:17], totals[17:18], totals[18:19], totals[19:20]
    q2 = totals[24:25]
    ex, ey, ez = mine_rows[0:1], mine_rows[1:2], mine_rows[2:3]
    sx, sy, sz = mine_rows[12:13] - ex, mine_rows[13:14] - ey, mine_rows[14:15] - ez
    by_s = (
        hx - (ey * gz - ez * gy) + upx - ex * u1 + sx * q2,
        hy - (ez * gx - ex * gz) + upy - ey * u1 + sy * q2,
        hz - (ex * gy - ey * gx) + upz - ez * u1 + sz * q2,
    )
    by_r = (
        gy * sz - gz * sy + apx - ex * a1 + sx * u1,
        gz * sx - gx * sz + apy - ey * a1 + sy * u1,
        gx * sy - gy * sx + apz - ez * a1 + sz * u1,
    )
    for axis in range(3):
        by_second = by_s[axis]
        by_first = -(by_s[axis] + by_r[axis])
        carried = jnp.where(
            lane == 0,
            pltpu.roll(jnp.broadcast_to(by_second, (8, LANES)), LANES - own_seg, 1)[0:1],
            pltpu.roll(jnp.broadcast_to(by_second, (8, LANES)), 1, 1)[0:1],
        )
        result = by_first + carried
        if axis == 2:
            result = 0.2 * result
        vert_out[axis : axis + 1, :] = result[:, 0:own_seg]


def on_device(rcv_points, rcv_normals, left_modes, vertices, connect, right_modes, mode_weights):
    count = lax.axis_size("src")
    own_count = vertices.shape[1]
    base_vertex = lax.axis_index("src") * own_count
    local_first = connect[0] - base_vertex
    weighted = right_modes * mode_weights[:, None]
    one_hot = (local_first[:, None] == jnp.arange(own_count, dtype=jnp.int32)[None, :]).astype(jnp.float32)
    folded = jnp.dot(weighted, one_hot, precision=lax.Precision.HIGHEST)
    lift = jnp.array([1.0, 1.0, 0.2], jnp.float32)[:, None]
    base = jnp.array([0.0, 0.0, 0.5], jnp.float32)[:, None]
    segment_rows = jnp.concatenate([vertices * lift, folded, jnp.zeros((1, own_count), jnp.float32)], 0)
    value = jnp.concatenate(
        [
            rcv_points * lift + base,
            rcv_normals,
            left_modes,
            jnp.concatenate([segment_rows[0:6], segment_rows[6:12]], 1),
            jnp.zeros((ROWS - REC_ROWS - 6, LANES), jnp.float32),
        ],
        0,
    )
    for step in exchange_masks(count):
        other = lax.ppermute(value, "src", [(s, s ^ step) for s in range(count)])
        value = jnp.concatenate([value, other], 0)
    return pl.pallas_call(
        functools.partial(kernel, count, own_count),
        out_shape=(
            jax.ShapeDtypeStruct((6, LANES), jnp.float32),
            jax.ShapeDtypeStruct((3, own_count), jnp.float32),
        ),
        in_specs=[pl.BlockSpec(memory_space=pltpu.VMEM)],
        out_specs=(pl.BlockSpec(memory_space=pltpu.VMEM), pl.BlockSpec(memory_space=pltpu.VMEM)),
        scratch_shapes=[
            pltpu.VMEM((count // 2, 16, LANES), jnp.float32),
            pltpu.VMEM((LANES, 16), jnp.float32),
            pltpu.VMEM((LANES, 16), jnp.float32),
        ],
        compiler_params=pltpu.CompilerParams(vmem_limit_bytes=16 << 20),
    )(value)


def solution(mesh):
    split = P(None, ("group", "src"))
    return jax.shard_map(
        on_device, mesh=mesh, in_specs=(split,) * 6 + (P("group"),), out_specs=(split, split), check_vma=False
    )
```

time: 155 us -> 36.8 us (0.24)
  blocking collectives: 60.7 us -> 0 us
  waiting for transfers between devices: 46.2 us -> 7.11 us
  other arithmetic: 25.1 us -> 0.22 us
  Pallas kernels: 0 us -> 15.9 us
  between operations: 14.3 us -> 0.68 us
  starting transfers between devices: 3.58 us -> 8.05 us
  local copies, waits for them, and re-layouts: 2.68 us -> 4.35 us
  matrix products: 1.85 us -> 0.19 us
    all_gather x3 -> x0, blocking collectives: 60.7 us -> none  [the longest x1 23.8 us: on_device(): shard_points = lax.all_gather(points, 'src', axis=1, tiled=True)]
    reduce_scatter x1 -> x0, waiting for transfers between devices: 45.5 us -> none  [on_device(): lax.psum_scatter(receiver_buffer, 'src', scatter_dimension=1, tiled=True)]
    pallas_call x0 -> x1, Pallas kernels: none -> 15.9 us  [on_device(): pl.pallas_call(functools.partial(kernel, count, own_count), out_shape=(ja...]
    reduce_sum x6 -> x0, other arithmetic: 9.18 us -> none  [the longest x1 3.41 us: tile_energy(): rel_first = points[:, None, :] - first_end[:, :, None]]
    broadcast_in_dim x3 -> x0, other arithmetic: 9.04 us -> none  [the longest x2 6.79 us: tile_energy(): cross_z = rel_first[0] * rel_second[1] - rel_first[1] * rel_second[0]]
    ppermute x2 -> x4, waiting for transfers between devices: 0.72 us -> 7.11 us  [on_device(): other = lax.ppermute(value, 'src', [(s, s ^ step) for s in range(count)])]
    ppermute x2 -> x4, starting transfers between devices: 3.54 us -> 8.05 us  [on_device(): other = lax.ppermute(value, 'src', [(s, s ^ step) for s in range(count)])]
    unnamed x8 -> x18, local copies, waits for them, and re-layouts: 0.02 us -> 3.31 us
  transfers between devices with their start and end apart: 3 -> 4, of which waited for: 2 -> 4; matrix products, arithmetic and copies ran while one was open for 2% -> 0% of each run, Pallas kernels for 0% -> 0%
where the time goes in v1:
time: 36.8 us; the launch traced here: 36.5 us
  Pallas kernels  15.9 us (43%)
  starting transfers between devices  8.05 us (22%)
  waiting for transfers between devices  7.11 us (19%)
  local copies, waits for them, and re-layouts  4.35 us (12%)
  between operations  0.68 us (2%)
    pallas_call x1, Pallas kernels, on_device(): pl.pallas_call(functools.partial(kernel, count, own_count), out_shape=(ja...  15.9 us
    ppermute x4, starting transfers between devices, on_device(): other = lax.ppermute(value, 'src', [(s, s ^ step) for s in range(count)])  8.05 us
    ppermute x4, waiting for transfers between devices, on_device(): other = lax.ppermute(value, 'src', [(s, s ^ step) for s in range(count)])  7.11 us
    unnamed x18, local copies, waits for them, and re-layouts  3.31 us
    concatenate x4, local copies, waits for them, and re-layouts, on_device(): value = jnp.concatenate([value, other], 0)  0.81 us
  transfers between devices with their start and end apart: 4, of which 4 were waited for; matrix products, arithmetic and copies ran while one was open for 0% of the time, Pallas kernels for 0%

profile of v1, /device:TPU:0, one launch (start us, length us, event | category | flops | bytes accessed | tf_op | source)
XLA Modules:
  0.0 36.5 jit_solution(1510826976432305969)
XLA Ops:
  0.7 0.7 %copy-done.7 = s32[2,128]{1,0:T(2,128)S(1)} copy-done((s32[2,128]{1,0:T(2,128)S(1)}, s32[2,128]{1,0:T(2,128)}, u32[]{:S(2)}) %copy-start.7) | copy-done | bytes 1048
  1.3 0.6 %copy-done.8 = f32[8]{0:T(128)S(1)} copy-done((f32[8]{0:T(128)S(1)}, f32[8]{0:T(128)}, u32[]{:S(2)}) %copy-start.8) | copy-done | bytes 56
  2.0 0.2 fusion
  2.2 0.6 %copy-done.2 = f32[3]{0:T(128)S(1)} copy-done((f32[3]{0:T(128)S(1)}, f32[3]{0:T(128)}, u32[]{:S(2)}) %copy-start.2) | copy-done | bytes 36
  2.9 0.1 broadcast_multiply_fusion
  3.0 0.6 %copy-done.4 = f32[3,128]{1,0:T(4,128)S(1)} copy-done((f32[3,128]{1,0:T(4,128)S(1)}, f32[3,128]{1,0:T(4,128)}, u32[]{:S(2)}) %copy-start.4) | copy-done | bytes 1560
  3.6 0.1 multiply_add_fusion
  3.7 0.1 fusion.2
  3.7 0.6 %copy-done = f32[8,128]{1,0:T(8,128)S(1)} copy-done((f32[8,128]{1,0:T(8,128)S(1)}, f32[8,128]{1,0:T(8,128)}, u32[]{:S(2)}) %copy-start) | copy-done | bytes 4120
  4.3 0.1 copy-done.1
  4.4 0.2 concatenate.32
  4.6 4.1 %collective-permute-start = (f32[24,128]{1,0:T(8,128)S(1)}, f32[24,128]{1,0:T(8,128)S(1)}, u32[]{:S(2)}, u32[]{:S(2)}) collective-permute-start(f32[24,128]{1,0:T(8,128)S(1)} %concatenate.32), channel_id=1, source_target_pairs={{0,8},{1,9},{2,10},{3,11},{4,12},{5,13},{6,14},{7,15},{8,0},{9,1},... | collective-permute-start | bytes 36872 | tf_op jit(solution)/shard_map/ppermute | solution.py:255
  8.7 1.7 %collective-permute-done = f32[24,128]{1,0:T(8,128)S(1)} collective-permute-done((f32[24,128]{1,0:T(8,128)S(1)}, f32[24,128]{1,0:T(8,128)S(1)}, u32[]{:S(2)}, u32[]{:S(2)}) %collective-permute-start) | collective-permute-done | bytes 12320 | tf_op jit(solution)/shard_map/ppermute | solution.py:255
  10.4 0.2 concatenate.33
  10.6 2.0 %collective-permute-start.1 = (f32[48,128]{1,0:T(8,128)S(1)}, f32[48,128]{1,0:T(8,128)S(1)}, u32[]{:S(2)}, u32[]{:S(2)}) collective-permute-start(f32[48,128]{1,0:T(8,128)S(1)} %concatenate.33), channel_id=1, source_target_pairs={{0,4},{1,5},{2,6},{3,7},{4,0},{5,1},{6,2},{7,3},{8,12},{9,13},{10,... | collective-permute-start | bytes 73736 | tf_op jit(solution)/shard_map/ppermute | solution.py:255
  12.6 1.9 %collective-permute-done.1 = f32[48,128]{1,0:T(8,128)S(1)} collective-permute-done((f32[48,128]{1,0:T(8,128)S(1)}, f32[48,128]{1,0:T(8,128)S(1)}, u32[]{:S(2)}, u32[]{:S(2)}) %collective-permute-start.1) | collective-permute-done | bytes 24608 | tf_op jit(solution)/shard_map/ppermute | solution.py:255
  14.5 0.2 concatenate.34
  14.7 1.9 %collective-permute-start.2 = (f32[96,128]{1,0:T(8,128)S(1)}, f32[96,128]{1,0:T(8,128)S(1)}, u32[]{:S(2)}, u32[]{:S(2)}) collective-permute-start(f32[96,128]{1,0:T(8,128)S(1)} %concatenate.34), channel_id=1, source_target_pairs={{0,2},{1,3},{2,0},{3,1},{4,6},{5,7},{6,4},{7,5},{8,10},{9,11},{10,... | collective-permute-start | bytes 147464 | tf_op jit(solution)/shard_map/ppermute | solution.py:255
  16.6 2.2 %collective-permute-done.2 = f32[96,128]{1,0:T(8,128)S(1)} collective-permute-done((f32[96,128]{1,0:T(8,128)S(1)}, f32[96,128]{1,0:T(8,128)S(1)}, u32[]{:S(2)}, u32[]{:S(2)}) %collective-permute-start.2) | collective-permute-done | bytes 49184 | tf_op jit(solution)/shard_map/ppermute | solution.py:255
  18.8 0.2 concatenate.35
  19.0 0.1 collective-permute-start.3
  19.1 1.3 %collective-permute-done.3 = f32[192,128]{1,0:T(8,128)S(1)} collective-permute-done((f32[192,128]{1,0:T(8,128)S(1)}, f32[192,128]{1,0:T(8,128)S(1)}, u32[]{:S(2)}, u32[]{:S(2)}) %collective-permute-start.3) | collective-permute-done | bytes 98336 | tf_op jit(solution)/shard_map/ppermute | solution.py:255
  20.4 0.2 concatenate.36.gathered_ref
  20.6 15.9 %shard_map.104 = (f32[6,128]{1,0:T(8,128)}, f32[3,64]{1,0:T(4,128)}) custom-call(f32[384,128]{1,0:T(8,128)S(1)} %concatenate.36.gathered_ref), custom_call_target="tpu_custom_call" | custom-call | tf_op jit(solution)/shard_map/pallas_call | solution.py:257
  (15 shorter events, 0.1 us)
Async XLA Ops:
  0.6 0.7 %copy-start.6 = (f32[8,128]{1,0:T(8,128)S(1)}, f32[8,128]{1,0:T(8,128)}, u32[]{:S(2)}) copy-start(f32[8,128]{1,0:T(8,128)} %param.14) | copy-start | bytes 12292
  0.6 0.7 %copy-start.7 = (s32[2,128]{1,0:T(2,128)S(1)}, s32[2,128]{1,0:T(2,128)}, u32[]{:S(2)}) copy-start(s32[2,128]{1,0:T(2,128)} %param.13) | copy-start | bytes 3076
  1.3 0.7 %copy-start.8 = (f32[8]{0:T(128)S(1)}, f32[8]{0:T(128)}, u32[]{:S(2)}) copy-start(f32[8]{0:T(128)} %param.15) | copy-start | bytes 100
  2.2 0.7 %copy-start.2 = (f32[3]{0:T(128)S(1)}, f32[3]{0:T(128)}, u32[]{:S(2)}) copy-start(f32[3]{0:T(128)} %constant.4.clone) | copy-start | bytes 40
  2.2 0.7 %copy-start.3 = (f32[3,64]{1,0:T(4,128)S(1)}, f32[3,64]{1,0:T(4,128)}, u32[]{:S(2)}) copy-start(f32[3,64]{1,0:T(4,128)} %param.12) | copy-start | bytes 2308
  2.9 0.7 %copy-start.4 = (f32[3,128]{1,0:T(4,128)S(1)}, f32[3,128]{1,0:T(4,128)}, u32[]{:S(2)}) copy-start(f32[3,128]{1,0:T(4,128)} %param.9) | copy-start | bytes 4612
  2.9 0.7 %copy-start.5 = (f32[3]{0:T(128)S(1)}, f32[3]{0:T(128)}, u32[]{:S(2)}) copy-start(f32[3]{0:T(128)} %constant.14.clone) | copy-start | bytes 40
  3.7 0.7 %copy-start = (f32[8,128]{1,0:T(8,128)S(1)}, f32[8,128]{1,0:T(8,128)}, u32[]{:S(2)}) copy-start(f32[8,128]{1,0:T(8,128)} %param.11) | copy-start | bytes 12292
  3.7 0.7 %copy-start.1 = (f32[3,128]{1,0:T(4,128)S(1)}, f32[3,128]{1,0:T(4,128)}, u32[]{:S(2)}) copy-start(f32[3,128]{1,0:T(4,128)} %param.10) | copy-start | bytes 4612
  4.6 5.8 %collective-permute-start = (f32[24,128]{1,0:T(8,128)S(1)}, f32[24,128]{1,0:T(8,128)S(1)}, u32[]{:S(2)}, u32[]{:S(2)}) collective-permute-start(f32[24,128]{1,0:T(8,128)S(1)} %concatenate.32), channel_id=1, source_target_pairs={{0,8},{1,9},{2,10},{3,11},{4,12},{5,13},{6,14},{7,15},{8,0},{9,1},... | collective-permute-start | bytes 36872 | tf_op jit(solution)/shard_map/ppermute | solution.py:255
  10.6 3.9 %collective-permute-start.1 = (f32[48,128]{1,0:T(8,128)S(1)}, f32[48,128]{1,0:T(8,128)S(1)}, u32[]{:S(2)}, u32[]{:S(2)}) collective-permute-start(f32[48,128]{1,0:T(8,128)S(1)} %concatenate.33), channel_id=1, source_target_pairs={{0,4},{1,5},{2,6},{3,7},{4,0},{5,1},{6,2},{7,3},{8,12},{9,13},{10,... | collective-permute-start | bytes 73736 | tf_op jit(solution)/shard_map/ppermute | solution.py:255
  14.7 4.2 %collective-permute-start.2 = (f32[96,128]{1,0:T(8,128)S(1)}, f32[96,128]{1,0:T(8,128)S(1)}, u32[]{:S(2)}, u32[]{:S(2)}) collective-permute-start(f32[96,128]{1,0:T(8,128)S(1)} %concatenate.34), channel_id=1, source_target_pairs={{0,2},{1,3},{2,0},{3,1},{4,6},{5,7},{6,4},{7,5},{8,10},{9,11},{10,... | collective-permute-start | bytes 147464 | tf_op jit(solution)/shard_map/ppermute | solution.py:255
  19.0 1.4 %collective-permute-start.3 = (f32[192,128]{1,0:T(8,128)S(1)}, f32[192,128]{1,0:T(8,128)S(1)}, u32[]{:S(2)}, u32[]{:S(2)}) collective-permute-start(f32[192,128]{1,0:T(8,128)S(1)} %concatenate.35), channel_id=1, source_target_pairs={{0,1},{1,0},{2,3},{3,2},{4,5},{5,4},{6,7},{7,6},{8,9},{9,8},{10,11... | collective-permute-start | bytes 294920 | tf_op jit(solution)/shard_map/ppermute | solution.py:255

commit v2 on v0

v2 whole, which is shorter than its diff:
```python
import functools
import math

import jax
import jax.numpy as jnp
from jax import lax
from jax.experimental import pallas as pl
from jax.experimental.pallas import tpu as pltpu
from jax.sharding import PartitionSpec as P

core_term = 0.05
inverse_four_pi = 0.25 / math.pi

LANES = 128
ROWS = 24
CHUNK = 16
VMEM = pl.BlockSpec(memory_space=pltpu.VMEM)


def exchange_masks(count):
    masks = []
    step = count // 2
    while step > 1:
        masks.append(step + 1)
        step //= 2
    return masks + [1]


def mask_at(place, masks):
    value = 0
    for bit, mask in enumerate(masks):
        if place >> bit & 1:
            value ^= mask
    return value


def place_of(value, masks):
    place = 0
    rest = value & 1
    for bit, mask in enumerate(masks[:-1]):
        taken = lax.shift_right_logical(value, mask.bit_length() - 1) & 1
        place = place + taken * (1 << bit)
        rest = rest ^ taken
    return place + rest * (1 << (len(masks) - 1))


def high_low(value):
    high = value.astype(jnp.bfloat16).astype(jnp.float32)
    return high, value - high


def dot_nt(left, right):
    return lax.dot_general(left, right, (((1,), (1,)), ((), ())), preferred_element_type=jnp.float32)


def cross(a, b):
    return (a[1] * b[2] - a[2] * b[1], a[2] * b[0] - a[0] * b[2], a[0] * b[1] - a[1] * b[0])


def pair_terms(point, normal, moment, first, segment, turn, span, span_core, scale, want_span):
    rel = tuple(p - e for p, e in zip(point, first))
    cross_n = (moment[0] * segment[0] + moment[1] * segment[1] + moment[2] * segment[2]) - (
        normal[0] * turn[0] + normal[1] * turn[1] + normal[2] * turn[2]
    )
    dist_sq = rel[0] * rel[0] + rel[1] * rel[1] + rel[2] * rel[2]
    along = segment[0] * rel[0] + segment[1] * rel[1] + segment[2] * rel[2]
    other = along - span
    second_sq = dist_sq - along - other
    inv_first = lax.rsqrt(dist_sq)
    inv_second = lax.rsqrt(second_sq)
    inv_den = 1.0 / ((span * dist_sq + span_core) - along * along)
    part_first = along * inv_first
    part_second = other * inv_second
    line = part_first - part_second
    scaled = scale * inv_den
    by_normal = scaled * line
    by_line = scaled * cross_n
    by_den = (by_normal * cross_n) * inv_den
    by_den2 = by_den + by_den
    cube_first = part_first * (inv_first * inv_first)
    cube_second = part_second * (inv_second * inv_second)
    by_dist2 = by_line * (cube_second - cube_first) - by_den2 * span
    by_along = by_line * ((inv_first - inv_second) - cube_second) + by_den2 * along
    if not want_span:
        return rel, by_normal, by_dist2, by_along
    by_span2 = by_line * ((inv_second + inv_second) + cube_second) - by_den2 * (dist_sq + core_term)
    return rel, by_normal, by_dist2, by_along, by_span2


def segment_terms(first, second):
    segment = tuple(b - a for a, b in zip(first, second))
    span = segment[0] * segment[0] + segment[1] * segment[1] + segment[2] * segment[2]
    return segment, cross(segment, first), span, core_term * span + core_term


def pack_kernel(own_seg, points_ref, normals_ref, left_ref, vertices_ref, connect_ref, right_ref, weights_ref, out_ref):
    base = lax.axis_index("src") * own_seg
    row8 = lax.broadcasted_iota(jnp.int32, (8, LANES), 0)
    weight = jnp.zeros((8, LANES), jnp.float32)
    for mode in range(8):
        weight = jnp.where(row8 == mode, weights_ref[mode], weight)
    weighted = right_ref[...] * (weight * inverse_four_pi)
    high, rest = high_low(weighted)
    middle, low = high_low(rest)
    parts = jnp.concatenate([high, middle, low, jnp.zeros_like(low)], 0).astype(jnp.bfloat16)
    local = connect_ref[0:1, :] - base
    hit = lax.broadcasted_iota(jnp.int32, (LANES, LANES), 0) == local
    folded = dot_nt(parts, hit.astype(jnp.float32).astype(jnp.bfloat16))
    folded = folded[0:8] + (folded[8:16] + folded[16:24])
    out_ref[0:8, :] = left_ref[...]
    out_ref[8:10, :] = points_ref[0:2, :]
    out_ref[10:11, :] = 0.5 + 0.2 * points_ref[2:3, :]
    out_ref[11:14, :] = normals_ref[...]
    out_ref[14:16, :] = jnp.zeros((2, LANES), jnp.float32)
    out_ref[16:24, :] = folded
    out_ref[16:18, own_seg : 2 * own_seg] = vertices_ref[0:2, :]
    out_ref[18:19, own_seg : 2 * own_seg] = 0.2 * vertices_ref[2:3, :]


def pair_kernel(count, own_seg, data_ref, rcv_out, vert_out, seg_ref, rec_ref, scale1_ref, scale2_ref, total_ref):
    masks = exchange_masks(count)
    tiles = count // 2
    me = lax.axis_index("src")
    lane = lax.broadcasted_iota(jnp.int32, (1, LANES), 1)
    low_half = lane < own_seg

    def device_block(device):
        return data_ref[place_of(device ^ me, masks), 16:24, :]

    folded = []
    for tile in range(tiles):
        block_a, block_b = data_ref[tile, 16:24, :], data_ref[tile + tiles, 16:24, :]
        after_a = device_block(((me ^ mask_at(tile, masks)) + 1) & (count - 1))
        after_b = device_block(((me ^ mask_at(tile + tiles, masks)) + 1) & (count - 1))
        folded.append(jnp.where(low_half, block_a, pltpu.roll(block_b, own_seg, 1)))
        first = jnp.where(low_half, pltpu.roll(block_a, own_seg, 1), block_b)
        second = jnp.where(
            lane < own_seg - 1,
            pltpu.roll(block_a, own_seg - 1, 1),
            jnp.where(
                low_half,
                pltpu.roll(after_a, LANES - 1, 1),
                jnp.where(lane < LANES - 1, pltpu.roll(block_b, LANES - 1, 1), pltpu.roll(after_b, own_seg - 1, 1)),
            ),
        )
        for axis in range(3):
            seg_ref[axis, tile : tile + 1, :] = first[axis : axis + 1]
            seg_ref[3 + axis, tile : tile + 1, :] = second[axis : axis + 1]
    first = tuple(seg_ref[axis] for axis in range(3))
    segment, turn, span, span_core = segment_terms(first, tuple(seg_ref[3 + axis] for axis in range(3)))
    for axis in range(3):
        seg_ref[3 + axis] = segment[axis]
        seg_ref[6 + axis] = turn[axis]
    seg_ref[9] = span
    seg_ref[10] = span_core

    point = tuple(data_ref[:, 8 + axis, :] for axis in range(3))
    normal = tuple(data_ref[:, 11 + axis, :] for axis in range(3))
    moment = cross(point, normal)
    for axis in range(3):
        rec_ref[axis] = point[axis]
        rec_ref[3 + axis] = normal[axis]
        rec_ref[6 + axis] = moment[axis]

    def stack_hhll(rows):
        high, low = high_low(rows)
        return jnp.transpose(jnp.concatenate([high, high, low, low], 0)).astype(jnp.bfloat16)

    def stack_hlhl(rows):
        high, low = high_low(rows)
        both = jnp.concatenate([high, low], 0).astype(jnp.bfloat16)
        return jnp.concatenate([both, both], 0)

    left_own = stack_hhll(data_ref[0, 0:8, :])
    seg_own = stack_hhll(data_ref[0, 16:24, :])[0:own_seg]
    scale1_ref[...] = jnp.dot(
        left_own, stack_hlhl(jnp.concatenate(folded, 1)), preferred_element_type=jnp.float32)
    scale2_ref[...] = jnp.dot(
        seg_own, stack_hlhl(jnp.concatenate([data_ref[b, 0:8, :] for b in range(count)], 1)),
        preferred_element_type=jnp.float32)

    own_p = tuple(rec_ref[axis, 0:1, :] for axis in range(3))
    own_n = tuple(rec_ref[3 + axis, 0:1, :] for axis in range(3))
    own_m = tuple(rec_ref[6 + axis, 0:1, :] for axis in range(3))
    pad = jnp.zeros((7, LANES), jnp.float32)
    total_ref[...] = jnp.transpose(jnp.concatenate([*own_p, *own_n, *own_m, pad], 0))

    def gather_totals(sums, start):
        packed = jnp.zeros((CHUNK, 16), jnp.float32)
        column = lax.broadcasted_iota(jnp.int32, (CHUNK, 16), 1)
        for index, value in enumerate(sums):
            packed = jnp.where(column == index, jnp.sum(value, axis=1, keepdims=True), packed)
        total_ref[pl.ds(start, CHUNK), :] = packed

    def first_chunk(chunk, carry):
        start = pl.multiple_of(chunk * CHUNK, CHUNK)
        cols = total_ref[pl.ds(start, CHUNK), :]
        col = [jnp.broadcast_to(cols[:, k : k + 1], (CHUNK, LANES)) for k in range(9)]
        sums = [jnp.zeros((CHUNK, LANES), jnp.float32) for _ in range(9)]
        for tile in range(tiles):
            row = [seg_ref[k, tile : tile + 1, :] for k in range(11)]
            scale = scale1_ref[pl.ds(start, CHUNK), tile * LANES : (tile + 1) * LANES]
            rel, by_normal, by_dist2, by_along = pair_terms(
                col[0:3], col[3:6], col[6:9], row[0:3], row[3:6], row[6:9], row[9], row[10], scale, False)
            for axis in range(3):
                sums[axis] += by_normal * row[3 + axis]
                sums[3 + axis] += by_normal * row[6 + axis]
                sums[6 + axis] += by_dist2 * rel[axis] + by_along * row[3 + axis]
        gather_totals(sums, start)
        return carry

    lax.fori_loop(0, LANES // CHUNK, first_chunk, 0)
    totals = jnp.transpose(total_ref[...])
    sum_s = tuple(totals[axis : axis + 1] for axis in range(3))
    by_point = tuple(
        a + totals[6 + axis : 7 + axis] for axis, a in enumerate(cross(own_n, sum_s)))
    by_norm = tuple(
        a - totals[3 + axis : 4 + axis] for axis, a in enumerate(cross(sum_s, own_p)))
    rcv_out[0:1, :] = by_point[0]
    rcv_out[1:2, :] = by_point[1]
    rcv_out[2:3, :] = 0.2 * by_point[2]
    for axis in range(3):
        rcv_out[3 + axis : 4 + axis, :] = by_norm[axis]

    own_rows = [seg_ref[k, 0:1, :] for k in range(11)]
    total_ref[...] = jnp.transpose(jnp.concatenate(own_rows + [pad[0:5]], 0))

    def second_chunk(chunk, carry):
        start = pl.multiple_of(chunk * CHUNK, CHUNK)
        cols = total_ref[pl.ds(start, CHUNK), :]
        col = [jnp.broadcast_to(cols[:, k : k + 1], (CHUNK, LANES)) for k in range(11)]
        sums = [jnp.zeros((CHUNK, LANES), jnp.float32) for _ in range(11)]
        for block in range(count):
            row = [rec_ref[k, block : block + 1, :] for k in range(9)]
            scale = scale2_ref[pl.ds(start, CHUNK), block * LANES : (block + 1) * LANES]
            rel, by_normal, by_dist2, by_along, by_span2 = pair_terms(
                row[0:3], row[3:6], row[6:9], col[0:3], col[3:6], col[6:9], col[9], col[10], scale, True)
            for axis in range(3):
                sums[axis] += by_normal * row[3 + axis]
                sums[3 + axis] += by_normal * row[6 + axis] + by_along * rel[axis]
                sums[6 + axis] += by_dist2 * rel[axis]
            sums[9] += by_along
            sums[10] += by_span2
        gather_totals(sums, start)
        return carry

    lax.fori_loop(0, own_seg // CHUNK, second_chunk, 0)
    totals = jnp.transpose(total_ref[...])
    sum_n = tuple(totals[axis : axis + 1] for axis in range(3))
    own_e, own_s = own_rows[0:3], own_rows[3:6]
    turned, swept = cross(own_e, sum_n), cross(sum_n, own_s)

    before = device_block((me + count - 1) & (count - 1))
    here = data_ref[0, 16:24, :]
    edge_e = tuple(before[axis : axis + 1, LANES - 1 :] for axis in range(3))
    edge_e2 = tuple(here[axis : axis + 1, own_seg : own_seg + 1] for axis in range(3))
    edge_w = jnp.where(me == 0, 0.0, before[:, own_seg - 1 : own_seg])
    edge_s, edge_t, edge_span, edge_core = segment_terms(edge_e, edge_e2)
    scale = jnp.zeros((count, LANES), jnp.float32)
    for mode in range(8):
        scale += edge_w[mode : mode + 1] * data_ref[:, mode, :]
    point = tuple(rec_ref[axis] for axis in range(3))
    normal = tuple(rec_ref[3 + axis] for axis in range(3))
    moment = tuple(rec_ref[6 + axis] for axis in range(3))
    rel, by_normal, _, by_along, by_span2 = pair_terms(
        point, normal, moment, edge_e, edge_s, edge_t, edge_span, edge_core, scale, True)
    swung = cross(rel, normal)
    for axis in range(3):
        edge = jnp.sum(by_normal * swung[axis] + by_along * rel[axis] + by_span2 * edge_s[axis])
        by_second = totals[3 + axis : 4 + axis] - turned[axis] + own_s[axis] * totals[10:11]
        by_rel = swept[axis] + totals[6 + axis : 7 + axis] + own_s[axis] * totals[9:10]
        result = jnp.where(lane == 0, edge, pltpu.roll(by_second, 1, 1)) - (by_second + by_rel)
        if axis == 2:
            result = 0.2 * result
        vert_out[axis : axis + 1, :] = result[:, 0:own_seg]


def on_device(rcv_points, rcv_normals, left_modes, vertices, connect, right_modes, mode_weights):
    count = lax.axis_size("src")
    own_seg = vertices.shape[1]
    tiles = count // 2
    value = pl.pallas_call(
        functools.partial(pack_kernel, own_seg),
        out_shape=jax.ShapeDtypeStruct((ROWS, LANES), jnp.float32),
        in_specs=[VMEM] * 6 + [pl.BlockSpec(memory_space=pltpu.SMEM)],
        out_specs=VMEM,
    )(rcv_points, rcv_normals, left_modes, vertices, connect, right_modes, mode_weights)[None]
    for mask in exchange_masks(count):
        other = lax.ppermute(value, "src", [(s, s ^ mask) for s in range(count)])
        value = jnp.concatenate([value, other], 0)
    return pl.pallas_call(
        functools.partial(pair_kernel, count, own_seg),
        out_shape=(
            jax.ShapeDtypeStruct((6, LANES), jnp.float32),
            jax.ShapeDtypeStruct((3, own_seg), jnp.float32),
        ),
        in_specs=[VMEM],
        out_specs=(VMEM, VMEM),
        scratch_shapes=[
            pltpu.VMEM((11, tiles, LANES), jnp.float32),
            pltpu.VMEM((9, count, LANES), jnp.float32),
            pltpu.VMEM((LANES, tiles * LANES), jnp.float32),
            pltpu.VMEM((own_seg, count * LANES), jnp.float32),
            pltpu.VMEM((LANES, 16), jnp.float32),
        ],
        compiler_params=pltpu.CompilerParams(vmem_limit_bytes=24 << 20),
    )(value)


def solution(mesh):
    split = P(None, ("group", "src"))
    return jax.shard_map(
        on_device, mesh=mesh, in_specs=(split,) * 6 + (P("group"),), out_specs=(split, split), check_vma=False
    )
```

time: 155 us -> 22.3 us (0.14)
  blocking collectives: 60.7 us -> 0 us
  waiting for transfers between devices: 46.2 us -> 5.21 us
  other arithmetic: 25.1 us -> 0.02 us
  between operations: 14.3 us -> 0.64 us
  Pallas kernels: 0 us -> 7.84 us
  starting transfers between devices: 3.58 us -> 7.62 us
  local copies, waits for them, and re-layouts: 2.68 us -> 0.76 us
  matrix products: 1.85 us -> 0 us
    all_gather x3 -> x0, blocking collectives: 60.7 us -> none  [the longest x1 23.8 us: on_device(): shard_points = lax.all_gather(points, 'src', axis=1, tiled=True)]
    reduce_scatter x1 -> x0, waiting for transfers between devices: 45.5 us -> none  [on_device(): lax.psum_scatter(receiver_buffer, 'src', scatter_dimension=1, tiled=True)]
    reduce_sum x6 -> x0, other arithmetic: 9.18 us -> none  [the longest x1 3.41 us: tile_energy(): rel_first = points[:, None, :] - first_end[:, :, None]]
    broadcast_in_dim x3 -> x0, other arithmetic: 9.04 us -> none  [the longest x2 6.79 us: tile_energy(): cross_z = rel_first[0] * rel_second[1] - rel_first[1] * rel_second[0]]
    pallas_call x0 -> x2, Pallas kernels: none -> 7.84 us  [the longest x1 6.28 us: on_device(): pl.pallas_call(functools.partial(pair_kernel, count, own_seg), out_shape=...]
    ppermute x2 -> x4, waiting for transfers between devices: 0.72 us -> 5.21 us  [on_device(): other = lax.ppermute(value, 'src', [(s, s ^ mask) for s in range(count)])]
    ppermute x2 -> x4, starting transfers between devices: 3.54 us -> 7.62 us  [on_device(): other = lax.ppermute(value, 'src', [(s, s ^ mask) for s in range(count)])]
    scatter-add x2 -> x0, other arithmetic: 2.21 us -> none  [on_device(): vertex_partial.at[:, local_first].add(sum_first).at[:, local_second]]
  transfers between devices with their start and end apart: 3 -> 4, of which waited for: 2 -> 4; matrix products, arithmetic and copies ran while one was open for 2% -> 3% of each run, Pallas kernels for 0% -> 0%
where the time goes in v2:
time: 22.3 us; the launch traced here: 22.1 us
  Pallas kernels  7.84 us (35%)
  starting transfers between devices  7.62 us (34%)
  waiting for transfers between devices  5.21 us (23%)
  local copies, waits for them, and re-layouts  0.76 us (3%)
  between operations  0.64 us (3%)
    ppermute x4, starting transfers between devices, on_device(): other = lax.ppermute(value, 'src', [(s, s ^ mask) for s in range(count)])  7.62 us
    pallas_call x1, Pallas kernels, on_device(): pl.pallas_call(functools.partial(pair_kernel, count, own_seg), out_shape=...  6.28 us
    ppermute x4, waiting for transfers between devices, on_device(): other = lax.ppermute(value, 'src', [(s, s ^ mask) for s in range(count)])  5.21 us
    pallas_call x1, Pallas kernels, on_device(): pl.pallas_call(functools.partial(pack_kernel, own_seg), out_shape=jax.Sha...  1.56 us
    unnamed x6, local copies, waits for them, and re-layouts  0.76 us
  transfers between devices with their start and end apart: 4, of which 4 were waited for; matrix products, arithmetic and copies ran while one was open for 3% of the time, Pallas kernels for 0%

profile of v2, /device:TPU:0, one launch (start us, length us, event | category | flops | bytes accessed | tf_op | source)
XLA Modules:
  0.0 22.1 jit_solution(5415553419792669023)
XLA Ops:
  0.6 1.6 %shard_map.86 = f32[24,128]{1,0:T(8,128)} custom-call(f32[3,128]{1,0:T(4,128)} %points_ref.1, f32[3,128]{1,0:T(4,128)} %normals_ref.1, f32[8,128]{1,0:T(8,128)} %left_ref.1, f32[3,64]{1,0:T(4,128)} %vertices_ref.1, s32[2,128]{1,0:T(2,128)} %connect_ref.1, f32[8,128]{1,0:T(8,128)} %right_ref.1, f32[8]{0:T(128)} %weights_ref.1), custom_call_target="tpu_custom_call" | custom-call | tf_op jit(solution)/shard_map/pallas_call | solution.py:282
  2.2 0.0 copy-start
  2.2 3.5 %collective-permute-start = (f32[1,24,128]{2,1,0:T(8,128)}, f32[1,24,128]{2,1,0:T(8,128)S(1)}, u32[]{:S(2)}, u32[]{:S(2)}) collective-permute-start(f32[1,24,128]{2,1,0:T(8,128)} %bitcast.2), channel_id=1, source_target_pairs={{0,9},{1,8},{2,11},{3,10},{4,13},{5,12},{6,15},{7,14},{8,1},{9,0},... | collective-permute-start | bytes 36872 | tf_op jit(solution)/shard_map/ppermute | solution.py:289
  5.7 0.7 %constant_dynamic-update-slice_fusion.4 = f32[16,24,128]{2,1,0:T(8,128)S(1)} fusion(f32[24,128]{1,0:T(8,128)} %shard_map.86), kind=kLoop, calls=%fused_computation.7 | loop fusion | bytes 24576
  6.4 0.9 %collective-permute-done = f32[1,24,128]{2,1,0:T(8,128)S(1)} collective-permute-done((f32[1,24,128]{2,1,0:T(8,128)}, f32[1,24,128]{2,1,0:T(8,128)S(1)}, u32[]{:S(2)}, u32[]{:S(2)}) %collective-permute-start) | collective-permute-done | bytes 12320 | tf_op jit(solution)/shard_map/ppermute | solution.py:289
  7.3 0.0 copy-done
  7.3 1.9 %collective-permute-start.1 = (f32[2,24,128]{2,1,0:T(8,128)S(1)}, f32[2,24,128]{2,1,0:T(8,128)S(1)}, u32[]{:S(2)}, u32[]{:S(2)}) collective-permute-start(f32[2,24,128]{2,1,0:T(8,128)S(1)} %pad_maximum_fusion.2), channel_id=1, source_target_pairs={{0,5},{1,4},{2,7},{3,6},{4,1},{5,0},{6,3},{7,2},{8,13},{9,12},{10,... | collective-permute-start | bytes 73736 | tf_op jit(solution)/shard_map/ppermute | solution.py:289
  9.2 1.5 %collective-permute-done.1 = f32[2,24,128]{2,1,0:T(8,128)S(1)} collective-permute-done((f32[2,24,128]{2,1,0:T(8,128)S(1)}, f32[2,24,128]{2,1,0:T(8,128)S(1)}, u32[]{:S(2)}, u32[]{:S(2)}) %collective-permute-start.1) | collective-permute-done | bytes 24608 | tf_op jit(solution)/shard_map/ppermute | solution.py:289
  10.7 1.7 %collective-permute-start.2 = (f32[4,24,128]{2,1,0:T(8,128)S(1)}, f32[4,24,128]{2,1,0:T(8,128)S(1)}, u32[]{:S(2)}, u32[]{:S(2)}) collective-permute-start(f32[4,24,128]{2,1,0:T(8,128)S(1)} %pad_maximum_fusion.1), channel_id=1, source_target_pairs={{0,3},{1,2},{2,1},{3,0},{4,7},{5,6},{6,5},{7,4},{8,11},{9,10},{10,... | collective-permute-start | bytes 147464 | tf_op jit(solution)/shard_map/ppermute | solution.py:289
  12.4 1.8 %collective-permute-done.2 = f32[4,24,128]{2,1,0:T(8,128)S(1)} collective-permute-done((f32[4,24,128]{2,1,0:T(8,128)S(1)}, f32[4,24,128]{2,1,0:T(8,128)S(1)}, u32[]{:S(2)}, u32[]{:S(2)}) %collective-permute-start.2) | collective-permute-done | bytes 49184 | tf_op jit(solution)/shard_map/ppermute | solution.py:289
  14.2 0.6 %collective-permute-start.3 = (f32[8,24,128]{2,1,0:T(8,128)S(1)}, f32[8,24,128]{2,1,0:T(8,128)S(1)}, u32[]{:S(2)}, u32[]{:S(2)}) collective-permute-start(f32[8,24,128]{2,1,0:T(8,128)S(1)} %pad_maximum_fusion), channel_id=1, source_target_pairs={{0,1},{1,0},{2,3},{3,2},{4,5},{5,4},{6,7},{7,6},{8,9},{9,8},{10,11... | collective-permute-start | bytes 294920 | tf_op jit(solution)/shard_map/ppermute | solution.py:289
  14.9 0.9 %collective-permute-done.3 = f32[8,24,128]{2,1,0:T(8,128)S(1)} collective-permute-done((f32[8,24,128]{2,1,0:T(8,128)S(1)}, f32[8,24,128]{2,1,0:T(8,128)S(1)}, u32[]{:S(2)}, u32[]{:S(2)}) %collective-permute-start.3) | collective-permute-done | bytes 98336 | tf_op jit(solution)/shard_map/ppermute | solution.py:289
  15.8 6.3 %shard_map.87 = (f32[6,128]{1,0:T(8,128)}, f32[3,64]{1,0:T(4,128)}) custom-call(f32[16,24,128]{2,1,0:T(8,128)S(1)} %constant_dynamic-update-slice_fusion.data_ref), custom_call_target="tpu_custom_call" | custom-call | tf_op jit(solution)/shard_map/pallas_call | solution.py:291
  (7 shorter events, 0.0 us)
Async XLA Ops:
  2.2 5.1 %copy-start = (f32[24,128]{1,0:T(8,128)S(1)}, f32[24,128]{1,0:T(8,128)}, u32[]{:S(2)}) copy-start(f32[24,128]{1,0:T(8,128)} %shard_map.86) | copy-start | bytes 36868
  2.2 5.1 %collective-permute-start = (f32[1,24,128]{2,1,0:T(8,128)}, f32[1,24,128]{2,1,0:T(8,128)S(1)}, u32[]{:S(2)}, u32[]{:S(2)}) collective-permute-start(f32[1,24,128]{2,1,0:T(8,128)} %bitcast.2), channel_id=1, source_target_pairs={{0,9},{1,8},{2,11},{3,10},{4,13},{5,12},{6,15},{7,14},{8,1},{9,0},... | collective-permute-start | bytes 36872 | tf_op jit(solution)/shard_map/ppermute | solution.py:289
  7.3 3.4 %collective-permute-start.1 = (f32[2,24,128]{2,1,0:T(8,128)S(1)}, f32[2,24,128]{2,1,0:T(8,128)S(1)}, u32[]{:S(2)}, u32[]{:S(2)}) collective-permute-start(f32[2,24,128]{2,1,0:T(8,128)S(1)} %pad_maximum_fusion.2), channel_id=1, source_target_pairs={{0,5},{1,4},{2,7},{3,6},{4,1},{5,0},{6,3},{7,2},{8,13},{9,12},{10,... | collective-permute-start | bytes 73736 | tf_op jit(solution)/shard_map/ppermute | solution.py:289
  10.7 3.5 %collective-permute-start.2 = (f32[4,24,128]{2,1,0:T(8,128)S(1)}, f32[4,24,128]{2,1,0:T(8,128)S(1)}, u32[]{:S(2)}, u32[]{:S(2)}) collective-permute-start(f32[4,24,128]{2,1,0:T(8,128)S(1)} %pad_maximum_fusion.1), channel_id=1, source_target_pairs={{0,3},{1,2},{2,1},{3,0},{4,7},{5,6},{6,5},{7,4},{8,11},{9,10},{10,... | collective-permute-start | bytes 147464 | tf_op jit(solution)/shard_map/ppermute | solution.py:289
  14.2 1.6 %collective-permute-start.3 = (f32[8,24,128]{2,1,0:T(8,128)S(1)}, f32[8,24,128]{2,1,0:T(8,128)S(1)}, u32[]{:S(2)}, u32[]{:S(2)}) collective-permute-start(f32[8,24,128]{2,1,0:T(8,128)S(1)} %pad_maximum_fusion), channel_id=1, source_target_pairs={{0,1},{1,0},{2,3},{3,2},{4,5},{5,4},{6,7},{7,6},{8,9},{9,8},{10,11... | collective-permute-start | bytes 294920 | tf_op jit(solution)/shard_map/ppermute | solution.py:289

commit v3 on v2

--- a/solution.py
+++ b/solution.py
@@ -13,7 +13,7 @@
 
 LANES = 128
 ROWS = 24
-CHUNK = 16
+CHUNK = 32
 VMEM = pl.BlockSpec(memory_space=pltpu.VMEM)
 
 
@@ -209,7 +209,7 @@
         gather_totals(sums, start)
         return carry
 
-    lax.fori_loop(0, LANES // CHUNK, first_chunk, 0)
+    lax.fori_loop(0, LANES // CHUNK, first_chunk, 0, unroll=True)
     totals = jnp.transpose(total_ref[...])
     sum_s = tuple(totals[axis : axis + 1] for axis in range(3))
     by_point = tuple(
@@ -244,7 +244,7 @@
         gather_totals(sums, start)
         return carry
 
-    lax.fori_loop(0, own_seg // CHUNK, second_chunk, 0)
+    lax.fori_loop(0, own_seg // CHUNK, second_chunk, 0, unroll=True)
     totals = jnp.transpose(total_ref[...])
     sum_n = tuple(totals[axis : axis + 1] for axis in range(3))
     own_e, own_s = own_rows[0:3], own_rows[3:6]
@@ -281,7 +281,7 @@
     tiles = count // 2
     value = pl.pallas_call(
         functools.partial(pack_kernel, own_seg),
-        out_shape=jax.ShapeDtypeStruct((ROWS, LANES), jnp.float32),
+        out_shape=pltpu.VMEM((ROWS, LANES), jnp.float32),
         in_specs=[VMEM] * 6 + [pl.BlockSpec(memory_space=pltpu.SMEM)],
         out_specs=VMEM,
     )(rcv_points, rcv_normals, left_modes, vertices, connect, right_modes, mode_weights)[None]

time: 22.3 us -> 19.5 us (0.87)
  Pallas kernels: 7.84 us -> 5.36 us
  local copies, waits for them, and re-layouts: 0.76 us -> 0.02 us
  waiting for transfers between devices: 5.21 us -> 5.7 us
    pallas_call x1, Pallas kernels: 6.28 us -> 4.44 us  [on_device(): pl.pallas_call(functools.partial(pair_kernel, count, own_seg), out_shape=...]
    unnamed x6 -> x4, local copies, waits for them, and re-layouts: 0.76 us -> 0.01 us
    pallas_call x1, Pallas kernels: 1.56 us -> 0.92 us  [on_device(): pl.pallas_call(functools.partial(pack_kernel, own_seg), out_shape=pltpu.V...]
    ppermute x4, waiting for transfers between devices: 5.21 us -> 5.7 us  [on_device(): other = lax.ppermute(value, 'src', [(s, s ^ mask) for s in range(count)])]
  transfers between devices with their start and end apart: 4 -> 4, of which waited for: 4 -> 4; matrix products, arithmetic and copies ran while one was open for 3% -> 0% of each run, Pallas kernels for 0% -> 0%
where the time goes in v3:
time: 19.5 us; the launch traced here: 19.4 us
  starting transfers between devices  7.65 us (39%)
  waiting for transfers between devices  5.7 us (29%)
  Pallas kernels  5.36 us (27%)
  between operations  0.64 us (3%)
    ppermute x4, starting transfers between devices, on_device(): other = lax.ppermute(value, 'src', [(s, s ^ mask) for s in range(count)])  7.65 us
    ppermute x4, waiting for transfers between devices, on_device(): other = lax.ppermute(value, 'src', [(s, s ^ mask) for s in range(count)])  5.7 us
    pallas_call x1, Pallas kernels, on_device(): pl.pallas_call(functools.partial(pair_kernel, count, own_seg), out_shape=...  4.44 us
    pallas_call x1, Pallas kernels, on_device(): pl.pallas_call(functools.partial(pack_kernel, own_seg), out_shape=pltpu.V...  0.92 us
  transfers between devices with their start and end apart: 4, of which 4 were waited for; matrix products, arithmetic and copies ran while one was open for 0% of the time, Pallas kernels for 0%

profile of v3, /device:TPU:0, one launch (start us, length us, event | category | flops | bytes accessed | tf_op | source)
XLA Modules:
  0.0 19.4 jit_solution(2028321237527575729)
XLA Ops:
  0.6 0.9 %shard_map.86 = f32[24,128]{1,0:T(8,128)S(1)} custom-call(f32[3,128]{1,0:T(4,128)} %points_ref.1, f32[3,128]{1,0:T(4,128)} %normals_ref.1, f32[8,128]{1,0:T(8,128)} %left_ref.1, f32[3,64]{1,0:T(4,128)} %vertices_ref.1, s32[2,128]{1,0:T(2,128)} %connect_ref.1, f32[8,128]{1,0:T(8,128)} %right_ref.1, f32[8]{0:T(128)} %weights_ref.1), custom_call_target="tpu_custom_call" | custom-call | tf_op jit(solution)/shard_map/pallas_call | solution.py:282
  1.5 3.5 %collective-permute-start = (f32[1,24,128]{2,1,0:T(8,128)S(1)}, f32[1,24,128]{2,1,0:T(8,128)S(1)}, u32[]{:S(2)}, u32[]{:S(2)}) collective-permute-start(f32[1,24,128]{2,1,0:T(8,128)S(1)} %bitcast.2), channel_id=1, source_target_pairs={{0,9},{1,8},{2,11},{3,10},{4,13},{5,12},{6,15},{7,14},{8,1},{9,0},... | collective-permute-start | bytes 36872 | tf_op jit(solution)/shard_map/ppermute | solution.py:289
  5.1 1.4 %collective-permute-done = f32[1,24,128]{2,1,0:T(8,128)S(1)} collective-permute-done((f32[1,24,128]{2,1,0:T(8,128)S(1)}, f32[1,24,128]{2,1,0:T(8,128)S(1)}, u32[]{:S(2)}, u32[]{:S(2)}) %collective-permute-start) | collective-permute-done | bytes 12320 | tf_op jit(solution)/shard_map/ppermute | solution.py:289
  6.5 1.9 %collective-permute-start.1 = (f32[2,24,128]{2,1,0:T(8,128)S(1)}, f32[2,24,128]{2,1,0:T(8,128)S(1)}, u32[]{:S(2)}, u32[]{:S(2)}) collective-permute-start(f32[2,24,128]{2,1,0:T(8,128)S(1)} %pad_maximum_fusion.2), channel_id=1, source_target_pairs={{0,5},{1,4},{2,7},{3,6},{4,1},{5,0},{6,3},{7,2},{8,13},{9,12},{10,... | collective-permute-start | bytes 73736 | tf_op jit(solution)/shard_map/ppermute | solution.py:289
  8.4 1.5 %collective-permute-done.1 = f32[2,24,128]{2,1,0:T(8,128)S(1)} collective-permute-done((f32[2,24,128]{2,1,0:T(8,128)S(1)}, f32[2,24,128]{2,1,0:T(8,128)S(1)}, u32[]{:S(2)}, u32[]{:S(2)}) %collective-permute-start.1) | collective-permute-done | bytes 24608 | tf_op jit(solution)/shard_map/ppermute | solution.py:289
  9.9 1.7 %collective-permute-start.2 = (f32[4,24,128]{2,1,0:T(8,128)S(1)}, f32[4,24,128]{2,1,0:T(8,128)S(1)}, u32[]{:S(2)}, u32[]{:S(2)}) collective-permute-start(f32[4,24,128]{2,1,0:T(8,128)S(1)} %pad_maximum_fusion.1), channel_id=1, source_target_pairs={{0,3},{1,2},{2,1},{3,0},{4,7},{5,6},{6,5},{7,4},{8,11},{9,10},{10,... | collective-permute-start | bytes 147464 | tf_op jit(solution)/shard_map/ppermute | solution.py:289
  11.6 1.8 %collective-permute-done.2 = f32[4,24,128]{2,1,0:T(8,128)S(1)} collective-permute-done((f32[4,24,128]{2,1,0:T(8,128)S(1)}, f32[4,24,128]{2,1,0:T(8,128)S(1)}, u32[]{:S(2)}, u32[]{:S(2)}) %collective-permute-start.2) | collective-permute-done | bytes 49184 | tf_op jit(solution)/shard_map/ppermute | solution.py:289
  13.4 0.6 %collective-permute-start.3 = (f32[8,24,128]{2,1,0:T(8,128)S(1)}, f32[8,24,128]{2,1,0:T(8,128)S(1)}, u32[]{:S(2)}, u32[]{:S(2)}) collective-permute-start(f32[8,24,128]{2,1,0:T(8,128)S(1)} %pad_maximum_fusion), channel_id=1, source_target_pairs={{0,1},{1,0},{2,3},{3,2},{4,5},{5,4},{6,7},{7,6},{8,9},{9,8},{10,11... | collective-permute-start | bytes 294920 | tf_op jit(solution)/shard_map/ppermute | solution.py:289
  14.0 0.9 %collective-permute-done.3 = f32[8,24,128]{2,1,0:T(8,128)S(1)} collective-permute-done((f32[8,24,128]{2,1,0:T(8,128)S(1)}, f32[8,24,128]{2,1,0:T(8,128)S(1)}, u32[]{:S(2)}, u32[]{:S(2)}) %collective-permute-start.3) | collective-permute-done | bytes 98336 | tf_op jit(solution)/shard_map/ppermute | solution.py:289
  14.9 4.4 %shard_map.87 = (f32[6,128]{1,0:T(8,128)}, f32[3,64]{1,0:T(4,128)}) custom-call(f32[16,24,128]{2,1,0:T(8,128)S(1)} %constant_dynamic-update-slice_fusion.data_ref), custom_call_target="tpu_custom_call" | custom-call | tf_op jit(solution)/shard_map/pallas_call | solution.py:291
  (8 shorter events, 0.0 us)
Async XLA Ops:
  1.5 4.9 %collective-permute-start = (f32[1,24,128]{2,1,0:T(8,128)S(1)}, f32[1,24,128]{2,1,0:T(8,128)S(1)}, u32[]{:S(2)}, u32[]{:S(2)}) collective-permute-start(f32[1,24,128]{2,1,0:T(8,128)S(1)} %bitcast.2), channel_id=1, source_target_pairs={{0,9},{1,8},{2,11},{3,10},{4,13},{5,12},{6,15},{7,14},{8,1},{9,0},... | collective-permute-start | bytes 36872 | tf_op jit(solution)/shard_map/ppermute | solution.py:289
  6.5 3.4 %collective-permute-start.1 = (f32[2,24,128]{2,1,0:T(8,128)S(1)}, f32[2,24,128]{2,1,0:T(8,128)S(1)}, u32[]{:S(2)}, u32[]{:S(2)}) collective-permute-start(f32[2,24,128]{2,1,0:T(8,128)S(1)} %pad_maximum_fusion.2), channel_id=1, source_target_pairs={{0,5},{1,4},{2,7},{3,6},{4,1},{5,0},{6,3},{7,2},{8,13},{9,12},{10,... | collective-permute-start | bytes 73736 | tf_op jit(solution)/shard_map/ppermute | solution.py:289
  9.9 3.5 %collective-permute-start.2 = (f32[4,24,128]{2,1,0:T(8,128)S(1)}, f32[4,24,128]{2,1,0:T(8,128)S(1)}, u32[]{:S(2)}, u32[]{:S(2)}) collective-permute-start(f32[4,24,128]{2,1,0:T(8,128)S(1)} %pad_maximum_fusion.1), channel_id=1, source_target_pairs={{0,3},{1,2},{2,1},{3,0},{4,7},{5,6},{6,5},{7,4},{8,11},{9,10},{10,... | collective-permute-start | bytes 147464 | tf_op jit(solution)/shard_map/ppermute | solution.py:289
  13.4 1.5 %collective-permute-start.3 = (f32[8,24,128]{2,1,0:T(8,128)S(1)}, f32[8,24,128]{2,1,0:T(8,128)S(1)}, u32[]{:S(2)}, u32[]{:S(2)}) collective-permute-start(f32[8,24,128]{2,1,0:T(8,128)S(1)} %pad_maximum_fusion), channel_id=1, source_target_pairs={{0,1},{1,0},{2,3},{3,2},{4,5},{5,4},{6,7},{7,6},{8,9},{9,8},{10,11... | collective-permute-start | bytes 294920 | tf_op jit(solution)/shard_map/ppermute | solution.py:289

commit v4 on v3

v4 whole, which is shorter than its diff:
```python
import functools
import math

import jax
import jax.numpy as jnp
from jax import lax
from jax.experimental import pallas as pl
from jax.experimental.pallas import tpu as pltpu
from jax.sharding import PartitionSpec as P

core_term = 0.05
inverse_four_pi = 0.25 / math.pi

LANES = 128
ROWS = 24
CHUNK = 32
VMEM = pl.BlockSpec(memory_space=pltpu.VMEM)


def exchange_masks(count):
    masks = []
    step = count // 2
    while step > 1:
        masks.append(step + 1)
        step //= 2
    return masks + [1]


def mask_at(place, masks):
    value = 0
    for bit, mask in enumerate(masks):
        if place >> bit & 1:
            value ^= mask
    return value


def place_of(value, masks):
    place = 0
    rest = value & 1
    for bit, mask in enumerate(masks[:-1]):
        taken = lax.shift_right_logical(value, mask.bit_length() - 1) & 1
        place = place + taken * (1 << bit)
        rest = rest ^ taken
    return place + rest * (1 << (len(masks) - 1))


def high_low(value):
    high = value.astype(jnp.bfloat16).astype(jnp.float32)
    return high, value - high


def dot_nt(left, right):
    return lax.dot_general(left, right, (((1,), (1,)), ((), ())), preferred_element_type=jnp.float32)


def cross(a, b):
    return (a[1] * b[2] - a[2] * b[1], a[2] * b[0] - a[0] * b[2], a[0] * b[1] - a[1] * b[0])


def pair_terms(point, normal, moment, first, segment, turn, span, span_core, scale, want_span):
    rel = tuple(p - e for p, e in zip(point, first))
    cross_n = (moment[0] * segment[0] + moment[1] * segment[1] + moment[2] * segment[2]) - (
        normal[0] * turn[0] + normal[1] * turn[1] + normal[2] * turn[2]
    )
    dist_sq = rel[0] * rel[0] + rel[1] * rel[1] + rel[2] * rel[2]
    along = segment[0] * rel[0] + segment[1] * rel[1] + segment[2] * rel[2]
    other = along - span
    second_sq = dist_sq - along - other
    inv_first = lax.rsqrt(dist_sq)
    inv_second = lax.rsqrt(second_sq)
    inv_den = 1.0 / ((span * dist_sq + span_core) - along * along)
    part_first = along * inv_first
    part_second = other * inv_second
    line = part_first - part_second
    scaled = scale * inv_den
    by_normal = scaled * line
    by_line = scaled * cross_n
    by_den = (by_normal * cross_n) * inv_den
    by_den2 = by_den + by_den
    cube_first = part_first * (inv_first * inv_first)
    cube_second = part_second * (inv_second * inv_second)
    by_dist2 = by_line * (cube_second - cube_first) - by_den2 * span
    by_along = by_line * ((inv_first - inv_second) - cube_second) + by_den2 * along
    if not want_span:
        return rel, by_normal, by_dist2, by_along
    by_span2 = by_line * ((inv_second + inv_second) + cube_second) - by_den2 * (dist_sq + core_term)
    return rel, by_normal, by_dist2, by_along, by_span2


def segment_terms(first, second):
    segment = tuple(b - a for a, b in zip(first, second))
    span = segment[0] * segment[0] + segment[1] * segment[1] + segment[2] * segment[2]
    return segment, cross(segment, first), span, core_term * span + core_term


def pack_kernel(own_seg, points_ref, normals_ref, left_ref, vertices_ref, connect_ref, right_ref, weights_ref, out_ref):
    base = lax.axis_index("src") * own_seg
    row8 = lax.broadcasted_iota(jnp.int32, (8, LANES), 0)
    weight = jnp.zeros((8, LANES), jnp.float32)
    for mode in range(8):
        weight = jnp.where(row8 == mode, weights_ref[mode], weight)
    weighted = right_ref[...] * (weight * inverse_four_pi)
    high, rest = high_low(weighted)
    middle, low = high_low(rest)
    parts = jnp.concatenate([high, middle, low, jnp.zeros_like(low)], 0).astype(jnp.bfloat16)
    local = connect_ref[0:1, :] - base
    hit = lax.broadcasted_iota(jnp.int32, (LANES, LANES), 0) == local
    folded = dot_nt(parts, hit.astype(jnp.float32).astype(jnp.bfloat16))
    folded = folded[0:8] + (folded[8:16] + folded[16:24])
    out_ref[0:8, :] = left_ref[...]
    out_ref[8:10, :] = points_ref[0:2, :]
    out_ref[10:11, :] = 0.5 + 0.2 * points_ref[2:3, :]
    out_ref[11:14, :] = normals_ref[...]
    out_ref[14:16, :] = jnp.zeros((2, LANES), jnp.float32)
    out_ref[16:24, :] = folded
    out_ref[16:18, own_seg : 2 * own_seg] = vertices_ref[0:2, :]
    out_ref[18:19, own_seg : 2 * own_seg] = 0.2 * vertices_ref[2:3, :]


def pair_sums(data_ref, begin, end, own_seg, scratch, old1, old2):
    seg_ref, rec_ref, scale1_ref, scale2_ref, total1_ref, total2_ref = scratch
    blocks = end - begin
    tiles = blocks // 2
    lane = lax.broadcasted_iota(jnp.int32, (1, LANES), 1)
    low_half = lane < own_seg
    at_edge = (lane == own_seg - 1) | (lane == 2 * own_seg - 1)

    folded = []
    for tile in range(tiles):
        block_a, block_b = data_ref[begin + 2 * tile, 16:24, :], data_ref[begin + 2 * tile + 1, 16:24, :]
        both = jnp.where(low_half, block_a, pltpu.roll(block_b, own_seg, 1))
        folded.append(jnp.where(at_edge, 0.0, both))
        first = jnp.where(low_half, pltpu.roll(block_a, own_seg, 1), block_b)
        second = jnp.where(at_edge, first, pltpu.roll(first, LANES - 1, 1))
        for axis in range(3):
            seg_ref[axis, tile : tile + 1, :] = first[axis : axis + 1]
            seg_ref[3 + axis, tile : tile + 1, :] = second[axis : axis + 1]
    first = tuple(seg_ref[axis] for axis in range(3))
    segment, turn, span, span_core = segment_terms(first, tuple(seg_ref[3 + axis] for axis in range(3)))
    for axis in range(3):
        seg_ref[3 + axis] = segment[axis]
        seg_ref[6 + axis] = turn[axis]
    seg_ref[9] = span
    seg_ref[10] = span_core

    point = tuple(data_ref[begin:end, 8 + axis, :] for axis in range(3))
    normal = tuple(data_ref[begin:end, 11 + axis, :] for axis in range(3))
    moment = cross(point, normal)
    for axis in range(3):
        rec_ref[axis] = point[axis]
        rec_ref[3 + axis] = normal[axis]
        rec_ref[6 + axis] = moment[axis]

    def stack_hhll(rows):
        high, low = high_low(rows)
        return jnp.transpose(jnp.concatenate([high, high, low, low], 0)).astype(jnp.bfloat16)

    def stack_hlhl(rows):
        high, low = high_low(rows)
        both = jnp.concatenate([high, low], 0).astype(jnp.bfloat16)
        return jnp.concatenate([both, both], 0)

    own_block = data_ref[0, 16:24, :]
    left_own = stack_hhll(data_ref[0, 0:8, :])
    seg_own = stack_hhll(jnp.where(at_edge, 0.0, own_block))[0:own_seg]
    scale1_ref[...] = jnp.dot(
        left_own, stack_hlhl(jnp.concatenate(folded, 1)), preferred_element_type=jnp.float32)
    scale2_ref[...] = jnp.dot(
        seg_own, stack_hlhl(jnp.concatenate([data_ref[b, 0:8, :] for b in range(begin, end)], 1)),
        preferred_element_type=jnp.float32)

    def columns(rows):
        pad = jnp.zeros((16 - len(rows), LANES), jnp.float32)
        return jnp.transpose(jnp.concatenate(list(rows) + [pad], 0))

    own_p, own_n, own_m = own_receivers(data_ref)
    own_e, own_s, own_t, own_span, own_core = own_segments(own_block, own_seg)
    cols1 = columns([*own_p, *own_n, *own_m])
    cols2 = columns([*own_e, *own_s, *own_t, own_span, own_core])

    def packed(sums):
        result = jnp.zeros((CHUNK, 16), jnp.float32)
        column = lax.broadcasted_iota(jnp.int32, (CHUNK, 16), 1)
        for index, value in enumerate(sums):
            result = jnp.where(column == index, jnp.sum(value, axis=1, keepdims=True), result)
        return result

    for start in range(0, LANES, CHUNK):
        cols = cols1[start : start + CHUNK]
        col = [jnp.broadcast_to(cols[:, k : k + 1], (CHUNK, LANES)) for k in range(9)]
        sums = [jnp.zeros((CHUNK, LANES), jnp.float32) for _ in range(9)]
        for tile in range(tiles):
            row = [seg_ref[k, tile : tile + 1, :] for k in range(11)]
            scale = scale1_ref[start : start + CHUNK, tile * LANES : (tile + 1) * LANES]
            rel, by_normal, by_dist2, by_along = pair_terms(
                col[0:3], col[3:6], col[6:9], row[0:3], row[3:6], row[6:9], row[9], row[10], scale, False)
            for axis in range(3):
                sums[axis] += by_normal * row[3 + axis]
                sums[3 + axis] += by_normal * row[6 + axis]
                sums[6 + axis] += by_dist2 * rel[axis] + by_along * row[3 + axis]
        total1_ref[start : start + CHUNK, :] = packed(sums)

    for start in range(0, own_seg, CHUNK):
        cols = cols2[start : start + CHUNK]
        col = [jnp.broadcast_to(cols[:, k : k + 1], (CHUNK, LANES)) for k in range(11)]
        sums = [jnp.zeros((CHUNK, LANES), jnp.float32) for _ in range(11)]
        for block in range(blocks):
            row = [rec_ref[k, block : block + 1, :] for k in range(9)]
            scale = scale2_ref[start : start + CHUNK, block * LANES : (block + 1) * LANES]
            rel, by_normal, by_dist2, by_along, by_span2 = pair_terms(
                row[0:3], row[3:6], row[6:9], col[0:3], col[3:6], col[6:9], col[9], col[10], scale, True)
            for axis in range(3):
                sums[axis] += by_normal * row[3 + axis]
                sums[3 + axis] += by_normal * row[6 + axis] + by_along * rel[axis]
                sums[6 + axis] += by_dist2 * rel[axis]
            sums[9] += by_along
            sums[10] += by_span2
        total2_ref[start : start + CHUNK, :] = packed(sums)
    total1, total2 = total1_ref[...], total2_ref[...]
    if old1 is not None:
        total1, total2 = total1 + old1[...], total2 + old2[...]
    return total1, total2


def own_receivers(data_ref):
    point = tuple(data_ref[0, 8 + axis : 9 + axis, :] for axis in range(3))
    normal = tuple(data_ref[0, 11 + axis : 12 + axis, :] for axis in range(3))
    return point, normal, cross(point, normal)


def own_segments(own_block, own_seg):
    lane = lax.broadcasted_iota(jnp.int32, (1, LANES), 1)
    first = pltpu.roll(own_block, own_seg, 1)
    second = jnp.where(lane == own_seg - 1, first, pltpu.roll(first, LANES - 1, 1))
    own_e = tuple(first[axis : axis + 1] for axis in range(3))
    segment, turn, span, span_core = segment_terms(own_e, tuple(second[axis : axis + 1] for axis in range(3)))
    return own_e, segment, turn, span, span_core


def early_kernel(begin, end, own_seg, *refs):
    data_ref, rest = refs[0], refs[1:]
    olds = rest[0:2] if begin else (None, None)
    rest = rest[2:] if begin else rest
    rest[0][...], rest[1][...] = pair_sums(data_ref, begin, end, own_seg, rest[2:], *olds)


def last_kernel(count, own_seg, data_ref, old1_ref, old2_ref, rcv_out, vert_out, after_ref, *scratch):
    masks = exchange_masks(count)
    me = lax.axis_index("src")
    lane = lax.broadcasted_iota(jnp.int32, (1, LANES), 1)

    def place(device):
        return place_of((device & (count - 1)) ^ me, masks)

    for block in range(count):
        after_ref[block] = data_ref[place((me ^ mask_at(block, masks)) + 1), 16:24, :]
    edge_e = tuple(data_ref[:, 16 + axis, 2 * own_seg - 1 : 2 * own_seg] for axis in range(3))
    edge_e2 = tuple(after_ref[:, axis, own_seg : own_seg + 1] for axis in range(3))
    edge_s, edge_t, edge_span, edge_core = segment_terms(edge_e, edge_e2)
    own_p, own_n, own_m = own_receivers(data_ref)
    scale = jnp.zeros((count, LANES), jnp.float32)
    for mode in range(8):
        scale += data_ref[:, 16 + mode, own_seg - 1 : own_seg] * data_ref[0, mode : mode + 1, :]
    rel, by_normal, by_dist2, by_along = pair_terms(
        own_p, own_n, own_m, edge_e, edge_s, edge_t, edge_span, edge_core, scale, False)

    def down(value):
        return jnp.sum(value, axis=0, keepdims=True)

    edge_sum_s = tuple(down(by_normal * edge_s[axis]) for axis in range(3))
    edge_sum_t = tuple(down(by_normal * edge_t[axis]) for axis in range(3))
    edge_sum_p = tuple(down(by_dist2 * rel[axis] + by_along * edge_s[axis]) for axis in range(3))

    point = tuple(data_ref[:, 8 + axis, :] for axis in range(3))
    normal = tuple(data_ref[:, 11 + axis, :] for axis in range(3))
    moment = cross(point, normal)
    own_block = data_ref[0, 16:24, :]
    before = data_ref[place(me + count - 1), 16:24, :]
    mine_last = tuple(own_block[axis : axis + 1, 2 * own_seg - 1 : 2 * own_seg] for axis in range(3))
    mine_next = tuple(after_ref[0, axis : axis + 1, own_seg : own_seg + 1] for axis in range(3))
    before_last = tuple(before[axis : axis + 1, 2 * own_seg - 1 : 2 * own_seg] for axis in range(3))
    mine_first = tuple(own_block[axis : axis + 1, own_seg : own_seg + 1] for axis in range(3))

    def edge_against_all(first, second, weight):
        segment, turn, span, span_core = segment_terms(first, second)
        scale = jnp.zeros((count, LANES), jnp.float32)
        for mode in range(8):
            scale += weight[mode : mode + 1] * data_ref[:, mode, :]
        rel, by_normal, by_dist2, by_along, by_span2 = pair_terms(
            point, normal, moment, first, segment, turn, span, span_core, scale, True)
        swung, swept = cross(rel, normal), cross(normal, segment)
        by_s = [by_normal * swung[k] + by_along * rel[k] + by_span2 * segment[k] for k in range(3)]
        by_r = [by_normal * swept[k] + by_dist2 * rel[k] + by_along * segment[k] for k in range(3)]
        return by_s, by_r

    by_s, by_r = edge_against_all(mine_last, mine_next, own_block[:, own_seg - 1 : own_seg])
    leaving = [-jnp.sum(by_s[axis] + by_r[axis]) for axis in range(3)]
    by_s, _ = edge_against_all(
        before_last, mine_first, jnp.where(me == 0, 0.0, before[:, own_seg - 1 : own_seg]))
    arriving = [jnp.sum(by_s[axis]) for axis in range(3)]

    total1, total2 = pair_sums(data_ref, count // 2, count, own_seg, scratch, old1_ref, old2_ref)
    totals = jnp.transpose(total1)
    sum_s = tuple(totals[axis : axis + 1] + edge_sum_s[axis] for axis in range(3))
    by_point, by_norm = cross(own_n, sum_s), cross(sum_s, own_p)
    for axis in range(3):
        value = by_point[axis] + (totals[6 + axis : 7 + axis] + edge_sum_p[axis])
        rcv_out[axis : axis + 1, :] = 0.2 * value if axis == 2 else value
        rcv_out[3 + axis : 4 + axis, :] = by_norm[axis] - (totals[3 + axis : 4 + axis] + edge_sum_t[axis])

    totals = jnp.transpose(total2)
    sum_n = tuple(totals[axis : axis + 1] for axis in range(3))
    own_e, own_s, _, _, _ = own_segments(own_block, own_seg)
    own_e = tuple(value[:, 0:own_seg] for value in own_e)
    own_s = tuple(value[:, 0:own_seg] for value in own_s)
    turned, swept = cross(own_e, sum_n), cross(sum_n, own_s)
    lane = lane[:, 0:own_seg]
    for axis in range(3):
        by_second = totals[3 + axis : 4 + axis] - turned[axis] + own_s[axis] * totals[10:11]
        by_rel = swept[axis] + totals[6 + axis : 7 + axis] + own_s[axis] * totals[9:10]
        shifted = jnp.concatenate([by_second[:, own_seg - 1 :], by_second[:, : own_seg - 1]], 1)
        result = jnp.where(lane == 0, arriving[axis], shifted) - (by_second + by_rel)
        result = result + jnp.where(lane == own_seg - 1, leaving[axis], 0.0)
        vert_out[axis : axis + 1, :] = 0.2 * result if axis == 2 else result


def pair_scratch(blocks, own_seg):
    return [
        pltpu.VMEM((11, blocks // 2, LANES), jnp.float32),
        pltpu.VMEM((9, blocks, LANES), jnp.float32),
        pltpu.VMEM((LANES, blocks // 2 * LANES), jnp.float32),
        pltpu.VMEM((own_seg, blocks * LANES), jnp.float32),
        pltpu.VMEM((LANES, 16), jnp.float32),
        pltpu.VMEM((own_seg, 16), jnp.float32),
    ]


def pair_cost(blocks, own_seg):
    pairs = 2 * blocks * own_seg * LANES
    return pl.CostEstimate(flops=100 * pairs, bytes_accessed=blocks * ROWS * LANES * 4, transcendentals=3 * pairs)


def on_device(rcv_points, rcv_normals, left_modes, vertices, connect, right_modes, mode_weights):
    count = lax.axis_size("src")
    own_seg = vertices.shape[1]
    value = pl.pallas_call(
        functools.partial(pack_kernel, own_seg),
        out_shape=pltpu.VMEM((ROWS, LANES), jnp.float32),
        in_specs=[VMEM] * 6 + [pl.BlockSpec(memory_space=pltpu.SMEM)],
        out_specs=VMEM,
    )(rcv_points, rcv_normals, left_modes, vertices, connect, right_modes, mode_weights)[None]
    params = pltpu.CompilerParams(vmem_limit_bytes=24 << 20)
    sums = ()
    for mask in exchange_masks(count):
        held = value.shape[0]
        other = lax.ppermute(value, "src", [(s, s ^ mask) for s in range(count)])
        if held in (count // 4, count // 2):
            begin = 0 if held == count // 4 else count // 4
            sums = pl.pallas_call(
                functools.partial(early_kernel, begin, held, own_seg),
                out_shape=(pltpu.VMEM((LANES, 16), jnp.float32), pltpu.VMEM((own_seg, 16), jnp.float32)),
                in_specs=[VMEM] * (1 + len(sums)),
                out_specs=(VMEM, VMEM),
                scratch_shapes=pair_scratch(held - begin, own_seg),
                cost_estimate=pair_cost(held - begin, own_seg),
                compiler_params=params,
            )(value, *sums)
        value = jnp.concatenate([value, other], 0)
    return pl.pallas_call(
        functools.partial(last_kernel, count, own_seg),
        out_shape=(
            jax.ShapeDtypeStruct((6, LANES), jnp.float32),
            jax.ShapeDtypeStruct((3, own_seg), jnp.float32),
        ),
        in_specs=[VMEM] * 3,
        out_specs=(VMEM, VMEM),
        scratch_shapes=[pltpu.VMEM((count, 8, LANES), jnp.float32)] + pair_scratch(count // 2, own_seg),
        cost_estimate=pair_cost(count // 2, own_seg),
        compiler_params=params,
    )(value, *sums)


def solution(mesh):
    split = P(None, ("group", "src"))
    return jax.shard_map(
        on_device, mesh=mesh, in_specs=(split,) * 6 + (P("group"),), out_specs=(split, split), check_vma=False
    )
```

time: 19.5 us -> 20.1 us (1.031)
  Pallas kernels: 5.36 us -> 8.44 us
  waiting for transfers between devices: 5.7 us -> 3.21 us
    pallas_call x1 -> x3, Pallas kernels: 4.44 us -> 7.52 us  [the longest x1 4.42 us: on_device(): pl.pallas_call(functools.partial(last_kernel, count, own_seg), out_shape=...]
    ppermute x4, waiting for transfers between devices: 5.7 us -> 3.21 us  [on_device(): other = lax.ppermute(value, 'src', [(s, s ^ mask) for s in range(count)])]
  transfers between devices with their start and end apart: 4 -> 4, of which waited for: 4 -> 3; matrix products, arithmetic and copies ran while one was open for 0% -> 0% of each run, Pallas kernels for 0% -> 16%
where the time goes in v4:
time: 20.1 us; the launch traced here: 20 us
  Pallas kernels  8.44 us (42%)
  starting transfers between devices  7.65 us (38%)
  waiting for transfers between devices  3.21 us (16%)
  between operations  0.66 us (3%)
    ppermute x4, starting transfers between devices, on_device(): other = lax.ppermute(value, 'src', [(s, s ^ mask) for s in range(count)])  7.65 us
    pallas_call x1, Pallas kernels, on_device(): pl.pallas_call(functools.partial(last_kernel, count, own_seg), out_shape=...  4.42 us
    ppermute x4, waiting for transfers between devices, on_device(): other = lax.ppermute(value, 'src', [(s, s ^ mask) for s in range(count)])  3.21 us
    pallas_call x2, Pallas kernels, on_device(): pl.pallas_call(functools.partial(early_kernel, begin, held, own_seg), out...  3.1 us
    pallas_call x1, Pallas kernels, on_device(): pl.pallas_call(functools.partial(pack_kernel, own_seg), out_shape=pltpu.V...  0.92 us
  transfers between devices with their start and end apart: 4, of which 3 were waited for; matrix products, arithmetic and copies ran while one was open for 0% of the time, Pallas kernels for 16%

profile of v4, /device:TPU:0, one launch (start us, length us, event | category | flops | bytes accessed | tf_op | source)
XLA Modules:
  0.0 20.0 jit_solution(15383504669306828099)
XLA Ops:
  0.6 0.9 %shard_map.86 = f32[24,128]{1,0:T(8,128)S(1)} custom-call(f32[3,128]{1,0:T(4,128)} %points_ref.1, f32[3,128]{1,0:T(4,128)} %normals_ref.1, f32[8,128]{1,0:T(8,128)} %left_ref.1, f32[3,64]{1,0:T(4,128)} %vertices_ref.1, s32[2,128]{1,0:T(2,128)} %connect_ref.1, f32[8,128]{1,0:T(8,128)} %right_ref.1, f32[8]{0:T(128)} %weights_ref.1), custom_call_target="tpu_custom_call" | custom-call | tf_op jit(solution)/shard_map/pallas_call | solution.py:346
  1.5 3.5 %collective-permute-start = (f32[1,24,128]{2,1,0:T(8,128)S(1)}, f32[1,24,128]{2,1,0:T(8,128)S(1)}, u32[]{:S(2)}, u32[]{:S(2)}) collective-permute-start(f32[1,24,128]{2,1,0:T(8,128)S(1)} %bitcast.2), channel_id=1, source_target_pairs={{0,9},{1,8},{2,11},{3,10},{4,13},{5,12},{6,15},{7,14},{8,1},{9,0},... | collective-permute-start | bytes 36872 | tf_op jit(solution)/shard_map/ppermute | solution.py:356
  5.1 1.4 %collective-permute-done = f32[1,24,128]{2,1,0:T(8,128)S(1)} collective-permute-done((f32[1,24,128]{2,1,0:T(8,128)S(1)}, f32[1,24,128]{2,1,0:T(8,128)S(1)}, u32[]{:S(2)}, u32[]{:S(2)}) %collective-permute-start) | collective-permute-done | bytes 12320 | tf_op jit(solution)/shard_map/ppermute | solution.py:356
  6.5 1.9 %collective-permute-start.1 = (f32[2,24,128]{2,1,0:T(8,128)S(1)}, f32[2,24,128]{2,1,0:T(8,128)S(1)}, u32[]{:S(2)}, u32[]{:S(2)}) collective-permute-start(f32[2,24,128]{2,1,0:T(8,128)S(1)} %pad_maximum_fusion.2), channel_id=1, source_target_pairs={{0,5},{1,4},{2,7},{3,6},{4,1},{5,0},{6,3},{7,2},{8,13},{9,12},{10,... | collective-permute-start | bytes 73736 | tf_op jit(solution)/shard_map/ppermute | solution.py:356
  8.4 1.5 %collective-permute-done.1 = f32[2,24,128]{2,1,0:T(8,128)S(1)} collective-permute-done((f32[2,24,128]{2,1,0:T(8,128)S(1)}, f32[2,24,128]{2,1,0:T(8,128)S(1)}, u32[]{:S(2)}, u32[]{:S(2)}) %collective-permute-start.1) | collective-permute-done | bytes 24608 | tf_op jit(solution)/shard_map/ppermute | solution.py:356
  9.9 1.7 %collective-permute-start.2 = (f32[4,24,128]{2,1,0:T(8,128)S(1)}, f32[4,24,128]{2,1,0:T(8,128)S(1)}, u32[]{:S(2)}, u32[]{:S(2)}) collective-permute-start(f32[4,24,128]{2,1,0:T(8,128)S(1)} %pad_maximum_fusion.1.refs_0_), channel_id=1, source_target_pairs={{0,3},{1,2},{2,1},{3,0},{4,7},{5,6},{6,5},{7,4},{8,11},{9,10},{10,... | collective-permute-start | bytes 147464 | tf_op jit(solution)/shard_map/ppermute | solution.py:356
  11.6 1.5 %shard_map.87 = (f32[128,16]{1,0:T(8,128)S(1)}, f32[64,16]{1,0:T(8,128)S(1)}) custom-call(f32[4,24,128]{2,1,0:T(8,128)S(1)} %pad_maximum_fusion.1.refs_0_), custom_call_target="tpu_custom_call" | custom-call | flops 6553600 | bytes 49152 | tf_op jit(solution)/shard_map/pallas_call | solution.py:359
  13.1 0.3 %collective-permute-done.2 = f32[4,24,128]{2,1,0:T(8,128)S(1)} collective-permute-done((f32[4,24,128]{2,1,0:T(8,128)S(1)}, f32[4,24,128]{2,1,0:T(8,128)S(1)}, u32[]{:S(2)}, u32[]{:S(2)}) %collective-permute-start.2) | collective-permute-done | bytes 49184 | tf_op jit(solution)/shard_map/ppermute | solution.py:356
  13.4 0.6 %collective-permute-start.3 = (f32[8,24,128]{2,1,0:T(8,128)S(1)}, f32[8,24,128]{2,1,0:T(8,128)S(1)}, u32[]{:S(2)}, u32[]{:S(2)}) collective-permute-start(f32[8,24,128]{2,1,0:T(8,128)S(1)} %pad_maximum_fusion.refs_0_), channel_id=1, source_target_pairs={{0,1},{1,0},{2,3},{3,2},{4,5},{5,4},{6,7},{7,6},{8,9},{9,8},{10,11... | collective-permute-start | bytes 294920 | tf_op jit(solution)/shard_map/ppermute | solution.py:356
  14.0 1.6 %shard_map.88 = (f32[128,16]{1,0:T(8,128)S(1)}, f32[64,16]{1,0:T(8,128)S(1)}) custom-call(f32[8,24,128]{2,1,0:T(8,128)S(1)} %pad_maximum_fusion.refs_0_, f32[128,16]{1,0:T(8,128)S(1)} %get-tuple-element.6.refs_1_, f32[64,16]{1,0:T(8,128)S(1)} %get-tuple-element.7.refs_2_), custom_call_target="tpu_custom_call" | custom-call | flops 6553600 | bytes 49152 | tf_op jit(solution)/shard_map/pallas_call | solution.py:359
  15.5 0.0 collective-permute-done.3
  15.6 4.4 %shard_map.89 = (f32[6,128]{1,0:T(8,128)}, f32[3,64]{1,0:T(4,128)}) custom-call(f32[16,24,128]{2,1,0:T(8,128)S(1)} %constant_dynamic-update-slice_fusion.data_ref, f32[128,16]{1,0:T(8,128)S(1)} %get-tuple-element.8.old1_ref, f32[64,16]{1,0:T(8,128)S(1)} %get-tuple-element.9.old2_ref), custom_call_target="tpu_custom_call" | custom-call | flops 13107200 | bytes 98304 | tf_op jit(solution)/shard_map/pallas_call | solution.py:369
  (8 shorter events, 0.0 us)
Async XLA Ops:
  1.5 4.9 %collective-permute-start = (f32[1,24,128]{2,1,0:T(8,128)S(1)}, f32[1,24,128]{2,1,0:T(8,128)S(1)}, u32[]{:S(2)}, u32[]{:S(2)}) collective-permute-start(f32[1,24,128]{2,1,0:T(8,128)S(1)} %bitcast.2), channel_id=1, source_target_pairs={{0,9},{1,8},{2,11},{3,10},{4,13},{5,12},{6,15},{7,14},{8,1},{9,0},... | collective-permute-start | bytes 36872 | tf_op jit(solution)/shard_map/ppermute | solution.py:356
  6.5 3.4 %collective-permute-start.1 = (f32[2,24,128]{2,1,0:T(8,128)S(1)}, f32[2,24,128]{2,1,0:T(8,128)S(1)}, u32[]{:S(2)}, u32[]{:S(2)}) collective-permute-start(f32[2,24,128]{2,1,0:T(8,128)S(1)} %pad_maximum_fusion.2), channel_id=1, source_target_pairs={{0,5},{1,4},{2,7},{3,6},{4,1},{5,0},{6,3},{7,2},{8,13},{9,12},{10,... | collective-permute-start | bytes 73736 | tf_op jit(solution)/shard_map/ppermute | solution.py:356
  9.9 3.5 %collective-permute-start.2 = (f32[4,24,128]{2,1,0:T(8,128)S(1)}, f32[4,24,128]{2,1,0:T(8,128)S(1)}, u32[]{:S(2)}, u32[]{:S(2)}) collective-permute-start(f32[4,24,128]{2,1,0:T(8,128)S(1)} %pad_maximum_fusion.1.refs_0_), channel_id=1, source_target_pairs={{0,3},{1,2},{2,1},{3,0},{4,7},{5,6},{6,5},{7,4},{8,11},{9,10},{10,... | collective-permute-start | bytes 147464 | tf_op jit(solution)/shard_map/ppermute | solution.py:356
  13.4 2.1 %collective-permute-start.3 = (f32[8,24,128]{2,1,0:T(8,128)S(1)}, f32[8,24,128]{2,1,0:T(8,128)S(1)}, u32[]{:S(2)}, u32[]{:S(2)}) collective-permute-start(f32[8,24,128]{2,1,0:T(8,128)S(1)} %pad_maximum_fusion.refs_0_), channel_id=1, source_target_pairs={{0,1},{1,0},{2,3},{3,2},{4,5},{5,4},{6,7},{7,6},{8,9},{9,8},{10,11... | collective-permute-start | bytes 294920 | tf_op jit(solution)/shard_map/ppermute | solution.py:356

commit v5 on v4

--- a/solution.py
+++ b/solution.py
@@ -252,54 +252,71 @@
     def place(device):
         return place_of((device & (count - 1)) ^ me, masks)
 
+    total1, total2 = pair_sums(data_ref, count // 2, count, own_seg, scratch, old1_ref, old2_ref)
     for block in range(count):
         after_ref[block] = data_ref[place((me ^ mask_at(block, masks)) + 1), 16:24, :]
-    edge_e = tuple(data_ref[:, 16 + axis, 2 * own_seg - 1 : 2 * own_seg] for axis in range(3))
-    edge_e2 = tuple(after_ref[:, axis, own_seg : own_seg + 1] for axis in range(3))
-    edge_s, edge_t, edge_span, edge_core = segment_terms(edge_e, edge_e2)
+
+    def spread(column):
+        return jnp.broadcast_to(column, (column.shape[0], LANES))
+
+    own_block = data_ref[0, 16:24, :]
+    before = data_ref[place(me + count - 1), 16:24, :]
     own_p, own_n, own_m = own_receivers(data_ref)
-    scale = jnp.zeros((count, LANES), jnp.float32)
-    for mode in range(8):
-        scale += data_ref[:, 16 + mode, own_seg - 1 : own_seg] * data_ref[0, mode : mode + 1, :]
-    rel, by_normal, by_dist2, by_along = pair_terms(
-        own_p, own_n, own_m, edge_e, edge_s, edge_t, edge_span, edge_core, scale, False)
-
-    def down(value):
-        return jnp.sum(value, axis=0, keepdims=True)
-
-    edge_sum_s = tuple(down(by_normal * edge_s[axis]) for axis in range(3))
-    edge_sum_t = tuple(down(by_normal * edge_t[axis]) for axis in range(3))
-    edge_sum_p = tuple(down(by_dist2 * rel[axis] + by_along * edge_s[axis]) for axis in range(3))
-
     point = tuple(data_ref[:, 8 + axis, :] for axis in range(3))
     normal = tuple(data_ref[:, 11 + axis, :] for axis in range(3))
     moment = cross(point, normal)
-    own_block = data_ref[0, 16:24, :]
-    before = data_ref[place(me + count - 1), 16:24, :]
-    mine_last = tuple(own_block[axis : axis + 1, 2 * own_seg - 1 : 2 * own_seg] for axis in range(3))
-    mine_next = tuple(after_ref[0, axis : axis + 1, own_seg : own_seg + 1] for axis in range(3))
-    before_last = tuple(before[axis : axis + 1, 2 * own_seg - 1 : 2 * own_seg] for axis in range(3))
-    mine_first = tuple(own_block[axis : axis + 1, own_seg : own_seg + 1] for axis in range(3))
-
-    def edge_against_all(first, second, weight):
-        segment, turn, span, span_core = segment_terms(first, second)
-        scale = jnp.zeros((count, LANES), jnp.float32)
-        for mode in range(8):
-            scale += weight[mode : mode + 1] * data_ref[:, mode, :]
-        rel, by_normal, by_dist2, by_along, by_span2 = pair_terms(
-            point, normal, moment, first, segment, turn, span, span_core, scale, True)
-        swung, swept = cross(rel, normal), cross(normal, segment)
-        by_s = [by_normal * swung[k] + by_along * rel[k] + by_span2 * segment[k] for k in range(3)]
-        by_r = [by_normal * swept[k] + by_dist2 * rel[k] + by_along * segment[k] for k in range(3)]
-        return by_s, by_r
-
-    by_s, by_r = edge_against_all(mine_last, mine_next, own_block[:, own_seg - 1 : own_seg])
-    leaving = [-jnp.sum(by_s[axis] + by_r[axis]) for axis in range(3)]
-    by_s, _ = edge_against_all(
-        before_last, mine_first, jnp.where(me == 0, 0.0, before[:, own_seg - 1 : own_seg]))
-    arriving = [jnp.sum(by_s[axis]) for axis in range(3)]
-
-    total1, total2 = pair_sums(data_ref, count // 2, count, own_seg, scratch, old1_ref, old2_ref)
+    mine_last = spread(own_block[:, 2 * own_seg - 1 : 2 * own_seg])
+    mine_next = spread(after_ref[0, :, own_seg : own_seg + 1])
+    mine_weight = spread(own_block[:, own_seg - 1 : own_seg])
+    before_last = spread(before[:, 2 * own_seg - 1 : 2 * own_seg])
+    before_weight = spread(jnp.where(me == 0, 0.0, before[:, own_seg - 1 : own_seg]))
+    mine_first = spread(own_block[:, own_seg : own_seg + 1])
+
+    def rows(value, axis):
+        return jnp.broadcast_to(value[axis : axis + 1], (count, LANES))
+
+    def stacked(own, every):
+        return tuple(
+            jnp.concatenate([jnp.broadcast_to(a, (count, LANES)), b, b], 0) for a, b in zip(own, every))
+
+    first = tuple(
+        jnp.concatenate(
+            [spread(data_ref[:, 16 + axis, 2 * own_seg - 1 : 2 * own_seg]), rows(mine_last, axis), rows(before_last, axis)], 0)
+        for axis in range(3))
+    second = tuple(
+        jnp.concatenate(
+            [spread(after_ref[:, axis, own_seg : own_seg + 1]), rows(mine_next, axis), rows(mine_first, axis)], 0)
+        for axis in range(3))
+    scales = [jnp.zeros((count, LANES), jnp.float32)] * 3
+    for mode in range(8):
+        left = data_ref[:, mode, :]
+        scales[0] += spread(data_ref[:, 16 + mode, own_seg - 1 : own_seg]) * data_ref[0, mode : mode + 1, :]
+        scales[1] += mine_weight[mode : mode + 1] * left
+        scales[2] += before_weight[mode : mode + 1] * left
+    segment, turn, span, span_core = segment_terms(first, second)
+    normals = stacked(own_n, normal)
+    rel, by_normal, by_dist2, by_along, by_span2 = pair_terms(
+        stacked(own_p, point), normals, stacked(own_m, moment),
+        first, segment, turn, span, span_core, jnp.concatenate(scales, 0), True)
+
+    def down(value):
+        return jnp.sum(value, axis=0, keepdims=True)
+
+    against_own, mine, ahead = slice(0, count), slice(count, 2 * count), slice(2 * count, 3 * count)
+    swung, swept = cross(rel, normals), cross(normals, segment)
+    edge_sum_s, edge_sum_t, edge_sum_p, leaving, arriving = [], [], [], [], []
+    for axis in range(3):
+        by_s = by_normal * swung[axis] + by_along * rel[axis] + by_span2 * segment[axis]
+        by_p = by_dist2 * rel[axis] + by_along * segment[axis]
+        by_r = by_normal * swept[axis] + by_p
+        edge_sum_s.append(down((by_normal * segment[axis])[against_own]))
+        edge_sum_t.append(down((by_normal * turn[axis])[against_own]))
+        edge_sum_p.append(down(by_p[against_own]))
+        leaving.append(down((by_s + by_r)[mine]))
+        arriving.append(down(by_s[ahead]))
+    edges = jnp.concatenate(leaving + arriving + leaving[0:2], 0)
+    edges = jnp.broadcast_to(jnp.sum(edges, axis=1, keepdims=True), (8, LANES))[:, 0:own_seg]
+
     totals = jnp.transpose(total1)
     sum_s = tuple(totals[axis : axis + 1] + edge_sum_s[axis] for axis in range(3))
     by_point, by_norm = cross(own_n, sum_s), cross(sum_s, own_p)
@@ -319,8 +336,8 @@
         by_second = totals[3 + axis : 4 + axis] - turned[axis] + own_s[axis] * totals[10:11]
         by_rel = swept[axis] + totals[6 + axis : 7 + axis] + own_s[axis] * totals[9:10]
         shifted = jnp.concatenate([by_second[:, own_seg - 1 :], by_second[:, : own_seg - 1]], 1)
-        result = jnp.where(lane == 0, arriving[axis], shifted) - (by_second + by_rel)
-        result = result + jnp.where(lane == own_seg - 1, leaving[axis], 0.0)
+        result = jnp.where(lane == 0, edges[3 + axis : 4 + axis], shifted) - (by_second + by_rel)
+        result = result - jnp.where(lane == own_seg - 1, edges[axis : axis + 1], 0.0)
         vert_out[axis : axis + 1, :] = 0.2 * result if axis == 2 else result
 
 

time: 20.1 us -> 19.2 us (0.955)
  Pallas kernels: 8.44 us -> 7.46 us
    pallas_call x1, Pallas kernels: 4.42 us -> 3.44 us  [on_device(): pl.pallas_call(functools.partial(last_kernel, count, own_seg), out_shape=...]
where the time goes in v5:
time: 19.2 us; the launch traced here: 19 us
  starting transfers between devices  7.65 us (40%)
  Pallas kernels  7.46 us (39%)
  waiting for transfers between devices  3.21 us (17%)
  between operations  0.66 us (3%)
    ppermute x4, starting transfers between devices, on_device(): other = lax.ppermute(value, 'src', [(s, s ^ mask) for s in range(count)])  7.65 us
    pallas_call x1, Pallas kernels, on_device(): pl.pallas_call(functools.partial(last_kernel, count, own_seg), out_shape=...  3.44 us
    ppermute x4, waiting for transfers between devices, on_device(): other = lax.ppermute(value, 'src', [(s, s ^ mask) for s in range(count)])  3.21 us
    pallas_call x2, Pallas kernels, on_device(): pl.pallas_call(functools.partial(early_kernel, begin, held, own_seg), out...  3.1 us
    pallas_call x1, Pallas kernels, on_device(): pl.pallas_call(functools.partial(pack_kernel, own_seg), out_shape=pltpu.V...  0.92 us
  transfers between devices with their start and end apart: 4, of which 3 were waited for; matrix products, arithmetic and copies ran while one was open for 0% of the time, Pallas kernels for 16%

profile of v5, /device:TPU:0, one launch (start us, length us, event | category | flops | bytes accessed | tf_op | source)
XLA Modules:
  0.0 19.0 jit_solution(5378036510003072936)
XLA Ops:
  0.6 0.9 %shard_map.86 = f32[24,128]{1,0:T(8,128)S(1)} custom-call(f32[3,128]{1,0:T(4,128)} %points_ref.1, f32[3,128]{1,0:T(4,128)} %normals_ref.1, f32[8,128]{1,0:T(8,128)} %left_ref.1, f32[3,64]{1,0:T(4,128)} %vertices_ref.1, s32[2,128]{1,0:T(2,128)} %connect_ref.1, f32[8,128]{1,0:T(8,128)} %right_ref.1, f32[8]{0:T(128)} %weights_ref.1), custom_call_target="tpu_custom_call" | custom-call | tf_op jit(solution)/shard_map/pallas_call | solution.py:363
  1.5 3.5 %collective-permute-start = (f32[1,24,128]{2,1,0:T(8,128)S(1)}, f32[1,24,128]{2,1,0:T(8,128)S(1)}, u32[]{:S(2)}, u32[]{:S(2)}) collective-permute-start(f32[1,24,128]{2,1,0:T(8,128)S(1)} %bitcast.2), channel_id=1, source_target_pairs={{0,9},{1,8},{2,11},{3,10},{4,13},{5,12},{6,15},{7,14},{8,1},{9,0},... | collective-permute-start | bytes 36872 | tf_op jit(solution)/shard_map/ppermute | solution.py:373
  5.1 1.4 %collective-permute-done = f32[1,24,128]{2,1,0:T(8,128)S(1)} collective-permute-done((f32[1,24,128]{2,1,0:T(8,128)S(1)}, f32[1,24,128]{2,1,0:T(8,128)S(1)}, u32[]{:S(2)}, u32[]{:S(2)}) %collective-permute-start) | collective-permute-done | bytes 12320 | tf_op jit(solution)/shard_map/ppermute | solution.py:373
  6.5 1.9 %collective-permute-start.1 = (f32[2,24,128]{2,1,0:T(8,128)S(1)}, f32[2,24,128]{2,1,0:T(8,128)S(1)}, u32[]{:S(2)}, u32[]{:S(2)}) collective-permute-start(f32[2,24,128]{2,1,0:T(8,128)S(1)} %pad_maximum_fusion.2), channel_id=1, source_target_pairs={{0,5},{1,4},{2,7},{3,6},{4,1},{5,0},{6,3},{7,2},{8,13},{9,12},{10,... | collective-permute-start | bytes 73736 | tf_op jit(solution)/shard_map/ppermute | solution.py:373
  8.4 1.5 %collective-permute-done.1 = f32[2,24,128]{2,1,0:T(8,128)S(1)} collective-permute-done((f32[2,24,128]{2,1,0:T(8,128)S(1)}, f32[2,24,128]{2,1,0:T(8,128)S(1)}, u32[]{:S(2)}, u32[]{:S(2)}) %collective-permute-start.1) | collective-permute-done | bytes 24608 | tf_op jit(solution)/shard_map/ppermute | solution.py:373
  9.9 1.7 %collective-permute-start.2 = (f32[4,24,128]{2,1,0:T(8,128)S(1)}, f32[4,24,128]{2,1,0:T(8,128)S(1)}, u32[]{:S(2)}, u32[]{:S(2)}) collective-permute-start(f32[4,24,128]{2,1,0:T(8,128)S(1)} %pad_maximum_fusion.1.refs_0_), channel_id=1, source_target_pairs={{0,3},{1,2},{2,1},{3,0},{4,7},{5,6},{6,5},{7,4},{8,11},{9,10},{10,... | collective-permute-start | bytes 147464 | tf_op jit(solution)/shard_map/ppermute | solution.py:373
  11.6 1.5 %shard_map.87 = (f32[128,16]{1,0:T(8,128)S(1)}, f32[64,16]{1,0:T(8,128)S(1)}) custom-call(f32[4,24,128]{2,1,0:T(8,128)S(1)} %pad_maximum_fusion.1.refs_0_), custom_call_target="tpu_custom_call" | custom-call | flops 6553600 | bytes 49152 | tf_op jit(solution)/shard_map/pallas_call | solution.py:376
  13.1 0.3 %collective-permute-done.2 = f32[4,24,128]{2,1,0:T(8,128)S(1)} collective-permute-done((f32[4,24,128]{2,1,0:T(8,128)S(1)}, f32[4,24,128]{2,1,0:T(8,128)S(1)}, u32[]{:S(2)}, u32[]{:S(2)}) %collective-permute-start.2) | collective-permute-done | bytes 49184 | tf_op jit(solution)/shard_map/ppermute | solution.py:373
  13.4 0.6 %collective-permute-start.3 = (f32[8,24,128]{2,1,0:T(8,128)S(1)}, f32[8,24,128]{2,1,0:T(8,128)S(1)}, u32[]{:S(2)}, u32[]{:S(2)}) collective-permute-start(f32[8,24,128]{2,1,0:T(8,128)S(1)} %pad_maximum_fusion.refs_0_), channel_id=1, source_target_pairs={{0,1},{1,0},{2,3},{3,2},{4,5},{5,4},{6,7},{7,6},{8,9},{9,8},{10,11... | collective-permute-start | bytes 294920 | tf_op jit(solution)/shard_map/ppermute | solution.py:373
  14.0 1.6 %shard_map.88 = (f32[128,16]{1,0:T(8,128)S(1)}, f32[64,16]{1,0:T(8,128)S(1)}) custom-call(f32[8,24,128]{2,1,0:T(8,128)S(1)} %pad_maximum_fusion.refs_0_, f32[128,16]{1,0:T(8,128)S(1)} %get-tuple-element.6.refs_1_, f32[64,16]{1,0:T(8,128)S(1)} %get-tuple-element.7.refs_2_), custom_call_target="tpu_custom_call" | custom-call | flops 6553600 | bytes 49152 | tf_op jit(solution)/shard_map/pallas_call | solution.py:376
  15.5 0.0 collective-permute-done.3
  15.6 3.4 %shard_map.89 = (f32[6,128]{1,0:T(8,128)}, f32[3,64]{1,0:T(4,128)}) custom-call(f32[16,24,128]{2,1,0:T(8,128)S(1)} %constant_dynamic-update-slice_fusion.data_ref, f32[128,16]{1,0:T(8,128)S(1)} %get-tuple-element.8.old1_ref, f32[64,16]{1,0:T(8,128)S(1)} %get-tuple-element.9.old2_ref), custom_call_target="tpu_custom_call" | custom-call | flops 13107200 | bytes 98304 | tf_op jit(solution)/shard_map/pallas_call | solution.py:386
  (8 shorter events, 0.0 us)
Async XLA Ops:
  1.5 4.9 %collective-permute-start = (f32[1,24,128]{2,1,0:T(8,128)S(1)}, f32[1,24,128]{2,1,0:T(8,128)S(1)}, u32[]{:S(2)}, u32[]{:S(2)}) collective-permute-start(f32[1,24,128]{2,1,0:T(8,128)S(1)} %bitcast.2), channel_id=1, source_target_pairs={{0,9},{1,8},{2,11},{3,10},{4,13},{5,12},{6,15},{7,14},{8,1},{9,0},... | collective-permute-start | bytes 36872 | tf_op jit(solution)/shard_map/ppermute | solution.py:373
  6.5 3.4 %collective-permute-start.1 = (f32[2,24,128]{2,1,0:T(8,128)S(1)}, f32[2,24,128]{2,1,0:T(8,128)S(1)}, u32[]{:S(2)}, u32[]{:S(2)}) collective-permute-start(f32[2,24,128]{2,1,0:T(8,128)S(1)} %pad_maximum_fusion.2), channel_id=1, source_target_pairs={{0,5},{1,4},{2,7},{3,6},{4,1},{5,0},{6,3},{7,2},{8,13},{9,12},{10,... | collective-permute-start | bytes 73736 | tf_op jit(solution)/shard_map/ppermute | solution.py:373
  9.9 3.5 %collective-permute-start.2 = (f32[4,24,128]{2,1,0:T(8,128)S(1)}, f32[4,24,128]{2,1,0:T(8,128)S(1)}, u32[]{:S(2)}, u32[]{:S(2)}) collective-permute-start(f32[4,24,128]{2,1,0:T(8,128)S(1)} %pad_maximum_fusion.1.refs_0_), channel_id=1, source_target_pairs={{0,3},{1,2},{2,1},{3,0},{4,7},{5,6},{6,5},{7,4},{8,11},{9,10},{10,... | collective-permute-start | bytes 147464 | tf_op jit(solution)/shard_map/ppermute | solution.py:373
  13.4 2.1 %collective-permute-start.3 = (f32[8,24,128]{2,1,0:T(8,128)S(1)}, f32[8,24,128]{2,1,0:T(8,128)S(1)}, u32[]{:S(2)}, u32[]{:S(2)}) collective-permute-start(f32[8,24,128]{2,1,0:T(8,128)S(1)} %pad_maximum_fusion.refs_0_), channel_id=1, source_target_pairs={{0,1},{1,0},{2,3},{3,2},{4,5},{5,4},{6,7},{7,6},{8,9},{9,8},{10,11... | collective-permute-start | bytes 294920 | tf_op jit(solution)/shard_map/ppermute | solution.py:373

commit v6 on v5

--- a/solution.py
+++ b/solution.py
@@ -13,7 +13,7 @@
 
 LANES = 128
 ROWS = 24
-CHUNK = 32
+CHUNK = 64
 VMEM = pl.BlockSpec(memory_space=pltpu.VMEM)
 
 
@@ -117,13 +117,50 @@
     out_ref[18:19, own_seg : 2 * own_seg] = 0.2 * vertices_ref[2:3, :]
 
 
-def pair_sums(data_ref, begin, end, own_seg, scratch, old1, old2):
-    seg_ref, rec_ref, scale1_ref, scale2_ref, total1_ref, total2_ref = scratch
+def stack_hhll(rows):
+    high, low = high_low(rows)
+    return jnp.transpose(jnp.concatenate([high, high, low, low], 0)).astype(jnp.bfloat16)
+
+
+def stack_hlhl(rows):
+    high, low = high_low(rows)
+    both = jnp.concatenate([high, low], 0).astype(jnp.bfloat16)
+    return jnp.concatenate([both, both], 0)
+
+
+def lane_edges(own_seg):
+    lane = lax.broadcasted_iota(jnp.int32, (1, LANES), 1)
+    return (lane == own_seg - 1) | (lane == 2 * own_seg - 1)
+
+
+def own_kernel(own_seg, data_ref, col1_ref, col2_ref, left_ref, right_ref, pick_ref):
+    def columns(rows, out_ref):
+        pad = jnp.zeros((16 - len(rows), LANES), jnp.float32)
+        cols = jnp.transpose(jnp.concatenate(list(rows) + [pad], 0))
+        count = out_ref.shape[1]
+        for k in range(len(rows)):
+            out_ref[k] = jnp.broadcast_to(cols[0:count, k : k + 1], (count, LANES))
+
+    own_block = data_ref[0, 16:24, :]
+    point, normal, moment = own_receivers(data_ref)
+    columns([*point, *normal, *moment], col1_ref)
+    own_e, own_s, own_t, span, span_core = own_segments(own_block, own_seg)
+    columns([*own_e, *own_s, *own_t, span, span_core], col2_ref)
+    left_ref[...] = stack_hhll(data_ref[0, 0:8, :])
+    right_ref[...] = stack_hhll(jnp.where(lane_edges(own_seg), 0.0, own_block))[0:own_seg]
+    group = lax.broadcasted_iota(jnp.int32, pick_ref.shape, 0) // LANES
+    picked = group == lax.broadcasted_iota(jnp.int32, pick_ref.shape, 1)
+    pick_ref[...] = picked.astype(jnp.float32).astype(jnp.bfloat16)
+
+
+def pair_sums(data_ref, own_refs, begin, end, own_seg, scratch, old1, old2, new1, new2):
+    seg_ref, rec_ref, scale1_ref, scale2_ref = scratch
+    col1_ref, col2_ref, left_ref, right_ref = own_refs[0:4]
     blocks = end - begin
     tiles = blocks // 2
     lane = lax.broadcasted_iota(jnp.int32, (1, LANES), 1)
     low_half = lane < own_seg
-    at_edge = (lane == own_seg - 1) | (lane == 2 * own_seg - 1)
+    at_edge = lane_edges(own_seg)
 
     folded = []
     for tile in range(tiles):
@@ -151,44 +188,20 @@
         rec_ref[3 + axis] = normal[axis]
         rec_ref[6 + axis] = moment[axis]
 
-    def stack_hhll(rows):
-        high, low = high_low(rows)
-        return jnp.transpose(jnp.concatenate([high, high, low, low], 0)).astype(jnp.bfloat16)
-
-    def stack_hlhl(rows):
-        high, low = high_low(rows)
-        both = jnp.concatenate([high, low], 0).astype(jnp.bfloat16)
-        return jnp.concatenate([both, both], 0)
-
-    own_block = data_ref[0, 16:24, :]
-    left_own = stack_hhll(data_ref[0, 0:8, :])
-    seg_own = stack_hhll(jnp.where(at_edge, 0.0, own_block))[0:own_seg]
     scale1_ref[...] = jnp.dot(
-        left_own, stack_hlhl(jnp.concatenate(folded, 1)), preferred_element_type=jnp.float32)
+        left_ref[...], stack_hlhl(jnp.concatenate(folded, 1)), preferred_element_type=jnp.float32)
     scale2_ref[...] = jnp.dot(
-        seg_own, stack_hlhl(jnp.concatenate([data_ref[b, 0:8, :] for b in range(begin, end)], 1)),
+        right_ref[...], stack_hlhl(jnp.concatenate([data_ref[b, 0:8, :] for b in range(begin, end)], 1)),
         preferred_element_type=jnp.float32)
 
-    def columns(rows):
-        pad = jnp.zeros((16 - len(rows), LANES), jnp.float32)
-        return jnp.transpose(jnp.concatenate(list(rows) + [pad], 0))
-
-    own_p, own_n, own_m = own_receivers(data_ref)
-    own_e, own_s, own_t, own_span, own_core = own_segments(own_block, own_seg)
-    cols1 = columns([*own_p, *own_n, *own_m])
-    cols2 = columns([*own_e, *own_s, *own_t, own_span, own_core])
-
-    def packed(sums):
-        result = jnp.zeros((CHUNK, 16), jnp.float32)
-        column = lax.broadcasted_iota(jnp.int32, (CHUNK, 16), 1)
-        for index, value in enumerate(sums):
-            result = jnp.where(column == index, jnp.sum(value, axis=1, keepdims=True), result)
-        return result
+    def initial(old, count, start):
+        if old is None:
+            return [jnp.zeros((CHUNK, LANES), jnp.float32) for _ in range(count)]
+        return [old[k, start : start + CHUNK, :] for k in range(count)]
 
     for start in range(0, LANES, CHUNK):
-        cols = cols1[start : start + CHUNK]
-        col = [jnp.broadcast_to(cols[:, k : k + 1], (CHUNK, LANES)) for k in range(9)]
-        sums = [jnp.zeros((CHUNK, LANES), jnp.float32) for _ in range(9)]
+        col = [col1_ref[k, start : start + CHUNK, :] for k in range(9)]
+        sums = initial(old1, 9, start)
         for tile in range(tiles):
             row = [seg_ref[k, tile : tile + 1, :] for k in range(11)]
             scale = scale1_ref[start : start + CHUNK, tile * LANES : (tile + 1) * LANES]
@@ -198,12 +211,12 @@
                 sums[axis] += by_normal * row[3 + axis]
                 sums[3 + axis] += by_normal * row[6 + axis]
                 sums[6 + axis] += by_dist2 * rel[axis] + by_along * row[3 + axis]
-        total1_ref[start : start + CHUNK, :] = packed(sums)
+        for k in range(9):
+            new1[k, start : start + CHUNK, :] = sums[k]
 
     for start in range(0, own_seg, CHUNK):
-        cols = cols2[start : start + CHUNK]
-        col = [jnp.broadcast_to(cols[:, k : k + 1], (CHUNK, LANES)) for k in range(11)]
-        sums = [jnp.zeros((CHUNK, LANES), jnp.float32) for _ in range(11)]
+        col = [col2_ref[k, start : start + CHUNK, :] for k in range(11)]
+        sums = initial(old2, 11, start)
         for block in range(blocks):
             row = [rec_ref[k, block : block + 1, :] for k in range(9)]
             scale = scale2_ref[start : start + CHUNK, block * LANES : (block + 1) * LANES]
@@ -215,11 +228,18 @@
                 sums[6 + axis] += by_dist2 * rel[axis]
             sums[9] += by_along
             sums[10] += by_span2
-        total2_ref[start : start + CHUNK, :] = packed(sums)
-    total1, total2 = total1_ref[...], total2_ref[...]
-    if old1 is not None:
-        total1, total2 = total1 + old1[...], total2 + old2[...]
-    return total1, total2
+        for k in range(11):
+            new2[k, start : start + CHUNK, :] = sums[k]
+
+
+def lane_sums(sums_ref, pick_ref):
+    count = sums_ref.shape[0]
+    parts = [high_low(sums_ref[k]) for k in range(count)]
+    pick = pick_ref[0 : count * LANES, :]
+    high = jnp.concatenate([part[0] for part in parts], 1).astype(jnp.bfloat16)
+    low = jnp.concatenate([part[1] for part in parts], 1).astype(jnp.bfloat16)
+    return jnp.dot(high, pick, preferred_element_type=jnp.float32) + jnp.dot(
+        low, pick, preferred_element_type=jnp.float32)
 
 
 def own_receivers(data_ref):
@@ -238,13 +258,16 @@
 
 
 def early_kernel(begin, end, own_seg, *refs):
-    data_ref, rest = refs[0], refs[1:]
+    data_ref, own_refs, rest = refs[0], refs[1:6], refs[6:]
     olds = rest[0:2] if begin else (None, None)
     rest = rest[2:] if begin else rest
-    rest[0][...], rest[1][...] = pair_sums(data_ref, begin, end, own_seg, rest[2:], *olds)
-
-
-def last_kernel(count, own_seg, data_ref, old1_ref, old2_ref, rcv_out, vert_out, after_ref, *scratch):
+    pair_sums(data_ref, own_refs, begin, end, own_seg, rest[2:], *olds, rest[0], rest[1])
+
+
+def last_kernel(count, own_seg, *refs):
+    data_ref, own_refs, old1_ref, old2_ref, rcv_out, vert_out, after_ref, new1_ref, new2_ref = (
+        refs[0], refs[1:6], *refs[6:13])
+    scratch = refs[13:]
     masks = exchange_masks(count)
     me = lax.axis_index("src")
     lane = lax.broadcasted_iota(jnp.int32, (1, LANES), 1)
@@ -252,7 +275,10 @@
     def place(device):
         return place_of((device & (count - 1)) ^ me, masks)
 
-    total1, total2 = pair_sums(data_ref, count // 2, count, own_seg, scratch, old1_ref, old2_ref)
+    pair_sums(
+        data_ref, own_refs, count // 2, count, own_seg, scratch, old1_ref, old2_ref, new1_ref, new2_ref)
+    total1 = lane_sums(new1_ref, own_refs[4])
+    total2 = lane_sums(new2_ref, own_refs[4])
     for block in range(count):
         after_ref[block] = data_ref[place((me ^ mask_at(block, masks)) + 1), 16:24, :]
 
@@ -347,9 +373,15 @@
         pltpu.VMEM((9, blocks, LANES), jnp.float32),
         pltpu.VMEM((LANES, blocks // 2 * LANES), jnp.float32),
         pltpu.VMEM((own_seg, blocks * LANES), jnp.float32),
-        pltpu.VMEM((LANES, 16), jnp.float32),
-        pltpu.VMEM((own_seg, 16), jnp.float32),
     ]
+
+
+def sum_shapes(own_seg):
+    return [pltpu.VMEM((9, LANES, LANES), jnp.float32), pltpu.VMEM((11, own_seg, LANES), jnp.float32)]
+
+
+def last_scratch(count, own_seg):
+    return [pltpu.VMEM((count, 8, LANES), jnp.float32)] + sum_shapes(own_seg) + pair_scratch(count // 2, own_seg)
 
 
 def pair_cost(blocks, own_seg):
@@ -367,6 +399,19 @@
         out_specs=VMEM,
     )(rcv_points, rcv_normals, left_modes, vertices, connect, right_modes, mode_weights)[None]
     params = pltpu.CompilerParams(vmem_limit_bytes=24 << 20)
+    own = pl.pallas_call(
+        functools.partial(own_kernel, own_seg),
+        out_shape=(
+            *sum_shapes(own_seg),
+            pltpu.VMEM((LANES, 32), jnp.bfloat16),
+            pltpu.VMEM((own_seg, 32), jnp.bfloat16),
+            pltpu.VMEM((11 * LANES, 16), jnp.bfloat16),
+        ),
+        in_specs=[VMEM],
+        out_specs=(VMEM,) * 5,
+        cost_estimate=pair_cost(2, own_seg),
+        compiler_params=params,
+    )(value)
     sums = ()
     for mask in exchange_masks(count):
         held = value.shape[0]
@@ -375,13 +420,13 @@
             begin = 0 if held == count // 4 else count // 4
             sums = pl.pallas_call(
                 functools.partial(early_kernel, begin, held, own_seg),
-                out_shape=(pltpu.VMEM((LANES, 16), jnp.float32), pltpu.VMEM((own_seg, 16), jnp.float32)),
-                in_specs=[VMEM] * (1 + len(sums)),
+                out_shape=tuple(sum_shapes(own_seg)),
+                in_specs=[VMEM] * (6 + len(sums)),
                 out_specs=(VMEM, VMEM),
                 scratch_shapes=pair_scratch(held - begin, own_seg),
                 cost_estimate=pair_cost(held - begin, own_seg),
                 compiler_params=params,
-            )(value, *sums)
+            )(value, *own, *sums)
         value = jnp.concatenate([value, other], 0)
     return pl.pallas_call(
         functools.partial(last_kernel, count, own_seg),
@@ -389,12 +434,12 @@
             jax.ShapeDtypeStruct((6, LANES), jnp.float32),
             jax.ShapeDtypeStruct((3, own_seg), jnp.float32),
         ),
-        in_specs=[VMEM] * 3,
+        in_specs=[VMEM] * 8,
         out_specs=(VMEM, VMEM),
-        scratch_shapes=[pltpu.VMEM((count, 8, LANES), jnp.float32)] + pair_scratch(count // 2, own_seg),
+        scratch_shapes=last_scratch(count, own_seg),
         cost_estimate=pair_cost(count // 2, own_seg),
         compiler_params=params,
-    )(value, *sums)
+    )(value, *own, *sums)
 
 
 def solution(mesh):

time: 19.2 us -> 18.2 us (0.948)
  Pallas kernels: 7.46 us -> 6.54 us
    pallas_call x2, Pallas kernels: 3.1 us -> 1.7 us  [on_device(): pl.pallas_call(functools.partial(early_kernel, begin, held, own_seg), out...]
    pallas_call x0 -> x1, Pallas kernels: none -> 0.8 us  [on_device(): pl.pallas_call(functools.partial(own_kernel, own_seg), out_shape=(*sum_sh...]
    pallas_call x1, Pallas kernels: 3.44 us -> 3.13 us  [on_device(): pl.pallas_call(functools.partial(last_kernel, count, own_seg), out_shape=...]
  transfers between devices with their start and end apart: 4 -> 4, of which waited for: 3 -> 4; matrix products, arithmetic and copies ran while one was open for 0% -> 0% of each run, Pallas kernels for 16% -> 14%
where the time goes in v6:
time: 18.2 us; the launch traced here: 18.1 us
  starting transfers between devices  7.65 us (42%)
  Pallas kernels  6.54 us (36%)
  waiting for transfers between devices  3.17 us (17%)
  between operations  0.67 us (4%)
    ppermute x4, starting transfers between devices, on_device(): other = lax.ppermute(value, 'src', [(s, s ^ mask) for s in range(count)])  7.65 us
    ppermute x4, waiting for transfers between devices, on_device(): other = lax.ppermute(value, 'src', [(s, s ^ mask) for s in range(count)])  3.17 us
    pallas_call x1, Pallas kernels, on_device(): pl.pallas_call(functools.partial(last_kernel, count, own_seg), out_shape=...  3.13 us
    pallas_call x2, Pallas kernels, on_device(): pl.pallas_call(functools.partial(early_kernel, begin, held, own_seg), out...  1.7 us
    pallas_call x1, Pallas kernels, on_device(): pl.pallas_call(functools.partial(pack_kernel, own_seg), out_shape=pltpu.V...  0.92 us
    pallas_call x1, Pallas kernels, on_device(): pl.pallas_call(functools.partial(own_kernel, own_seg), out_shape=(*sum_sh...  0.8 us
  transfers between devices with their start and end apart: 4, of which 4 were waited for; matrix products, arithmetic and copies ran while one was open for 0% of the time, Pallas kernels for 14%

profile of v6, /device:TPU:0, one launch (start us, length us, event | category | flops | bytes accessed | tf_op | source)
XLA Modules:
  0.0 18.1 jit_solution(9973645659774099773)
XLA Ops:
  0.6 0.9 %shard_map.86 = f32[24,128]{1,0:T(8,128)S(1)} custom-call(f32[3,128]{1,0:T(4,128)} %points_ref.1, f32[3,128]{1,0:T(4,128)} %normals_ref.1, f32[8,128]{1,0:T(8,128)} %left_ref.1, f32[3,64]{1,0:T(4,128)} %vertices_ref.1, s32[2,128]{1,0:T(2,128)} %connect_ref.1, f32[8,128]{1,0:T(8,128)} %right_ref.1, f32[8]{0:T(128)} %weights_ref.1), custom_call_target="tpu_custom_call" | custom-call | tf_op jit(solution)/shard_map/pallas_call | solution.py:395
  1.5 3.5 %collective-permute-start = (f32[1,24,128]{2,1,0:T(8,128)S(1)}, f32[1,24,128]{2,1,0:T(8,128)S(1)}, u32[]{:S(2)}, u32[]{:S(2)}) collective-permute-start(f32[1,24,128]{2,1,0:T(8,128)S(1)} %bitcast.2), channel_id=1, source_target_pairs={{0,9},{1,8},{2,11},{3,10},{4,13},{5,12},{6,15},{7,14},{8,1},{9,0},... | collective-permute-start | bytes 36872 | tf_op jit(solution)/shard_map/ppermute | solution.py:418
  5.1 0.8 %shard_map.87 = (f32[9,128,128]{2,1,0:T(8,128)S(1)}, f32[11,64,128]{2,1,0:T(8,128)S(1)}, bf16[128,32]{1,0:T(8,128)(2,1)S(1)}, bf16[64,32]{1,0:T(8,128)(2,1)S(1)}, bf16[1408,16]{1,0:T(8,128)(2,1)S(1)}) custom-call(f32[1,24,128]{2,1,0:T(8,128)S(1)} %bitcast.3), custom_call_target="tpu_custom_call" | custom-call | flops 3276800 | bytes 24576 | tf_op jit(solution)/shard_map/pallas_call | solution.py:402
  5.9 0.6 %collective-permute-done = f32[1,24,128]{2,1,0:T(8,128)S(1)} collective-permute-done((f32[1,24,128]{2,1,0:T(8,128)S(1)}, f32[1,24,128]{2,1,0:T(8,128)S(1)}, u32[]{:S(2)}, u32[]{:S(2)}) %collective-permute-start) | collective-permute-done | bytes 12320 | tf_op jit(solution)/shard_map/ppermute | solution.py:418
  6.5 1.9 %collective-permute-start.1 = (f32[2,24,128]{2,1,0:T(8,128)S(1)}, f32[2,24,128]{2,1,0:T(8,128)S(1)}, u32[]{:S(2)}, u32[]{:S(2)}) collective-permute-start(f32[2,24,128]{2,1,0:T(8,128)S(1)} %pad_maximum_fusion.2), channel_id=1, source_target_pairs={{0,5},{1,4},{2,7},{3,6},{4,1},{5,0},{6,3},{7,2},{8,13},{9,12},{10,... | collective-permute-start | bytes 73736 | tf_op jit(solution)/shard_map/ppermute | solution.py:418
  8.4 1.5 %collective-permute-done.1 = f32[2,24,128]{2,1,0:T(8,128)S(1)} collective-permute-done((f32[2,24,128]{2,1,0:T(8,128)S(1)}, f32[2,24,128]{2,1,0:T(8,128)S(1)}, u32[]{:S(2)}, u32[]{:S(2)}) %collective-permute-start.1) | collective-permute-done | bytes 24608 | tf_op jit(solution)/shard_map/ppermute | solution.py:418
  9.9 1.7 %collective-permute-start.2 = (f32[4,24,128]{2,1,0:T(8,128)S(1)}, f32[4,24,128]{2,1,0:T(8,128)S(1)}, u32[]{:S(2)}, u32[]{:S(2)}) collective-permute-start(f32[4,24,128]{2,1,0:T(8,128)S(1)} %pad_maximum_fusion.1.refs_0_), channel_id=1, source_target_pairs={{0,3},{1,2},{2,1},{3,0},{4,7},{5,6},{6,5},{7,4},{8,11},{9,10},{10,... | collective-permute-start | bytes 147464 | tf_op jit(solution)/shard_map/ppermute | solution.py:418
  11.6 0.8 %shard_map.88 = (f32[9,128,128]{2,1,0:T(8,128)S(1)}, f32[11,64,128]{2,1,0:T(8,128)S(1)}) custom-call(f32[4,24,128]{2,1,0:T(8,128)S(1)} %pad_maximum_fusion.1.refs_0_, f32[9,128,128]{2,1,0:T(8,128)S(1)} %get-tuple-element.11.refs_1_, f32[11,64,128]{2,1,0:T(8,128)S(1)} %get-tuple-element.12.refs_2_, bf16[128,32]{1,0:T(8,128)(2,1)S(1)} %get-tuple-element.13.refs_3_, ...), custom_call_target="tpu_custom_call" | custom-call | flops 6553600 | bytes 49152 | tf_op jit(solution)/shard_map/pallas_call | solution.py:421
  12.4 1.0 %collective-permute-done.2 = f32[4,24,128]{2,1,0:T(8,128)S(1)} collective-permute-done((f32[4,24,128]{2,1,0:T(8,128)S(1)}, f32[4,24,128]{2,1,0:T(8,128)S(1)}, u32[]{:S(2)}, u32[]{:S(2)}) %collective-permute-start.2) | collective-permute-done | bytes 49184 | tf_op jit(solution)/shard_map/ppermute | solution.py:418
  13.4 0.6 %collective-permute-start.3 = (f32[8,24,128]{2,1,0:T(8,128)S(1)}, f32[8,24,128]{2,1,0:T(8,128)S(1)}, u32[]{:S(2)}, u32[]{:S(2)}) collective-permute-start(f32[8,24,128]{2,1,0:T(8,128)S(1)} %pad_maximum_fusion.refs_0_), channel_id=1, source_target_pairs={{0,1},{1,0},{2,3},{3,2},{4,5},{5,4},{6,7},{7,6},{8,9},{9,8},{10,11... | collective-permute-start | bytes 294920 | tf_op jit(solution)/shard_map/ppermute | solution.py:418
  14.0 0.9 %shard_map.89 = (f32[9,128,128]{2,1,0:T(8,128)S(1)}, f32[11,64,128]{2,1,0:T(8,128)S(1)}) custom-call(f32[8,24,128]{2,1,0:T(8,128)S(1)} %pad_maximum_fusion.refs_0_, f32[9,128,128]{2,1,0:T(8,128)S(1)} %get-tuple-element.11.refs_1_, f32[11,64,128]{2,1,0:T(8,128)S(1)} %get-tuple-element.12.refs_2_, bf16[128,32]{1,0:T(8,128)(2,1)S(1)} %get-tuple-element.13.refs_3_, ...), custom_call_target="tpu_custom_call" | custom-call | flops 6553600 | bytes 49152 | tf_op jit(solution)/shard_map/pallas_call | solution.py:421
  14.9 0.1 collective-permute-done.3
  14.9 3.1 %shard_map.90 = (f32[6,128]{1,0:T(8,128)}, f32[3,64]{1,0:T(4,128)}) custom-call(f32[16,24,128]{2,1,0:T(8,128)S(1)} %constant_dynamic-update-slice_fusion.refs_0_, f32[9,128,128]{2,1,0:T(8,128)S(1)} %get-tuple-element.11.refs_1_, f32[11,64,128]{2,1,0:T(8,128)S(1)} %get-tuple-element.12.refs_2_, bf16[128,32]{1,0:T(8,128)(2,1)S(1)} %get-tuple-element.13.refs_3_, ...), custom_call_target="tpu_custom_call" | custom-call | flops 13107200 | bytes 98304 | tf_op jit(solution)/shard_map/pallas_call | solution.py:431
  (8 shorter events, 0.0 us)
Async XLA Ops:
  1.5 4.9 %collective-permute-start = (f32[1,24,128]{2,1,0:T(8,128)S(1)}, f32[1,24,128]{2,1,0:T(8,128)S(1)}, u32[]{:S(2)}, u32[]{:S(2)}) collective-permute-start(f32[1,24,128]{2,1,0:T(8,128)S(1)} %bitcast.2), channel_id=1, source_target_pairs={{0,9},{1,8},{2,11},{3,10},{4,13},{5,12},{6,15},{7,14},{8,1},{9,0},... | collective-permute-start | bytes 36872 | tf_op jit(solution)/shard_map/ppermute | solution.py:418
  6.5 3.4 %collective-permute-start.1 = (f32[2,24,128]{2,1,0:T(8,128)S(1)}, f32[2,24,128]{2,1,0:T(8,128)S(1)}, u32[]{:S(2)}, u32[]{:S(2)}) collective-permute-start(f32[2,24,128]{2,1,0:T(8,128)S(1)} %pad_maximum_fusion.2), channel_id=1, source_target_pairs={{0,5},{1,4},{2,7},{3,6},{4,1},{5,0},{6,3},{7,2},{8,13},{9,12},{10,... | collective-permute-start | bytes 73736 | tf_op jit(solution)/shard_map/ppermute | solution.py:418
  9.9 3.5 %collective-permute-start.2 = (f32[4,24,128]{2,1,0:T(8,128)S(1)}, f32[4,24,128]{2,1,0:T(8,128)S(1)}, u32[]{:S(2)}, u32[]{:S(2)}) collective-permute-start(f32[4,24,128]{2,1,0:T(8,128)S(1)} %pad_maximum_fusion.1.refs_0_), channel_id=1, source_target_pairs={{0,3},{1,2},{2,1},{3,0},{4,7},{5,6},{6,5},{7,4},{8,11},{9,10},{10,... | collective-permute-start | bytes 147464 | tf_op jit(solution)/shard_map/ppermute | solution.py:418
  13.4 1.5 %collective-permute-start.3 = (f32[8,24,128]{2,1,0:T(8,128)S(1)}, f32[8,24,128]{2,1,0:T(8,128)S(1)}, u32[]{:S(2)}, u32[]{:S(2)}) collective-permute-start(f32[8,24,128]{2,1,0:T(8,128)S(1)} %pad_maximum_fusion.refs_0_), channel_id=1, source_target_pairs={{0,1},{1,0},{2,3},{3,2},{4,5},{5,4},{6,7},{7,6},{8,9},{9,8},{10,11... | collective-permute-start | bytes 294920 | tf_op jit(solution)/shard_map/ppermute | solution.py:418

commit v7 on v6

--- a/solution.py
+++ b/solution.py
@@ -14,6 +14,7 @@
 LANES = 128
 ROWS = 24
 CHUNK = 64
+FINISH = 32
 VMEM = pl.BlockSpec(memory_space=pltpu.VMEM)
 
 
@@ -133,7 +134,7 @@
     return (lane == own_seg - 1) | (lane == 2 * own_seg - 1)
 
 
-def own_kernel(own_seg, data_ref, col1_ref, col2_ref, left_ref, right_ref, pick_ref):
+def own_kernel(own_seg, data_ref, col1_ref, col2_ref, left_ref, right_ref):
     def columns(rows, out_ref):
         pad = jnp.zeros((16 - len(rows), LANES), jnp.float32)
         cols = jnp.transpose(jnp.concatenate(list(rows) + [pad], 0))
@@ -148,14 +149,11 @@
     columns([*own_e, *own_s, *own_t, span, span_core], col2_ref)
     left_ref[...] = stack_hhll(data_ref[0, 0:8, :])
     right_ref[...] = stack_hhll(jnp.where(lane_edges(own_seg), 0.0, own_block))[0:own_seg]
-    group = lax.broadcasted_iota(jnp.int32, pick_ref.shape, 0) // LANES
-    picked = group == lax.broadcasted_iota(jnp.int32, pick_ref.shape, 1)
-    pick_ref[...] = picked.astype(jnp.float32).astype(jnp.bfloat16)
 
 
 def pair_sums(data_ref, own_refs, begin, end, own_seg, scratch, old1, old2, new1, new2):
     seg_ref, rec_ref, scale1_ref, scale2_ref = scratch
-    col1_ref, col2_ref, left_ref, right_ref = own_refs[0:4]
+    col1_ref, col2_ref, left_ref, right_ref = own_refs
     blocks = end - begin
     tiles = blocks // 2
     lane = lax.broadcasted_iota(jnp.int32, (1, LANES), 1)
@@ -232,14 +230,36 @@
             new2[k, start : start + CHUNK, :] = sums[k]
 
 
-def lane_sums(sums_ref, pick_ref):
-    count = sums_ref.shape[0]
-    parts = [high_low(sums_ref[k]) for k in range(count)]
-    pick = pick_ref[0 : count * LANES, :]
-    high = jnp.concatenate([part[0] for part in parts], 1).astype(jnp.bfloat16)
-    low = jnp.concatenate([part[1] for part in parts], 1).astype(jnp.bfloat16)
-    return jnp.dot(high, pick, preferred_element_type=jnp.float32) + jnp.dot(
-        low, pick, preferred_element_type=jnp.float32)
+def lane_sums(values):
+    rows = values[0].shape[0]
+    column = lax.broadcasted_iota(jnp.int32, (rows, 16), 1)
+    result = jnp.zeros((rows, 16), jnp.float32)
+    for index, value in enumerate(values):
+        result = jnp.where(column == index, jnp.sum(value, axis=1, keepdims=True), result)
+    return result
+
+
+def receiver_totals(sums_ref, col_ref):
+    parts = []
+    for start in range(0, LANES, FINISH):
+        sums = [sums_ref[k, start : start + FINISH, :] for k in range(9)]
+        col = [col_ref[k, start : start + FINISH, :] for k in range(6)]
+        by_point = [a + b for a, b in zip(cross(col[3:6], sums[0:3]), sums[6:9])]
+        by_normal = [a - b for a, b in zip(cross(sums[0:3], col[0:3]), sums[3:6])]
+        parts.append(lane_sums(by_point + by_normal))
+    return jnp.transpose(jnp.concatenate(parts, 0))
+
+
+def segment_totals(sums_ref, col_ref, own_seg):
+    parts = []
+    for start in range(0, own_seg, FINISH):
+        sums = [sums_ref[k, start : start + FINISH, :] for k in range(11)]
+        col = [col_ref[k, start : start + FINISH, :] for k in range(6)]
+        turned, swept = cross(col[0:3], sums[0:3]), cross(sums[0:3], col[3:6])
+        by_s = [sums[3 + k] - turned[k] + col[3 + k] * sums[10] for k in range(3)]
+        by_both = [by_s[k] + (swept[k] + sums[6 + k] + col[3 + k] * sums[9]) for k in range(3)]
+        parts.append(lane_sums(by_s + by_both))
+    return jnp.transpose(jnp.concatenate(parts, 0))
 
 
 def own_receivers(data_ref):
@@ -257,17 +277,17 @@
     return own_e, segment, turn, span, span_core
 
 
-def early_kernel(begin, end, own_seg, *refs):
-    data_ref, own_refs, rest = refs[0], refs[1:6], refs[6:]
-    olds = rest[0:2] if begin else (None, None)
-    rest = rest[2:] if begin else rest
-    pair_sums(data_ref, own_refs, begin, end, own_seg, rest[2:], *olds, rest[0], rest[1])
+def early_kernel(chained, own_seg, *refs):
+    data_ref, own_refs, rest = refs[0], refs[1:5], refs[5:]
+    olds = rest[0:2] if chained else (None, None)
+    rest = rest[2:] if chained else rest
+    pair_sums(data_ref, own_refs, 0, data_ref.shape[0], own_seg, rest[2:], *olds, rest[0], rest[1])
 
 
 def last_kernel(count, own_seg, *refs):
     data_ref, own_refs, old1_ref, old2_ref, rcv_out, vert_out, after_ref, new1_ref, new2_ref = (
-        refs[0], refs[1:6], *refs[6:13])
-    scratch = refs[13:]
+        refs[0], refs[1:5], *refs[5:12])
+    scratch = refs[12:]
     masks = exchange_masks(count)
     me = lax.axis_index("src")
     lane = lax.broadcasted_iota(jnp.int32, (1, LANES), 1)
@@ -276,9 +296,7 @@
         return place_of((device & (count - 1)) ^ me, masks)
 
     pair_sums(
-        data_ref, own_refs, count // 2, count, own_seg, scratch, old1_ref, old2_ref, new1_ref, new2_ref)
-    total1 = lane_sums(new1_ref, own_refs[4])
-    total2 = lane_sums(new2_ref, own_refs[4])
+        data_ref, own_refs, count - count // 4, count, own_seg, scratch, old1_ref, old2_ref, new1_ref, new2_ref)
     for block in range(count):
         after_ref[block] = data_ref[place((me ^ mask_at(block, masks)) + 1), 16:24, :]
 
@@ -343,26 +361,19 @@
     edges = jnp.concatenate(leaving + arriving + leaving[0:2], 0)
     edges = jnp.broadcast_to(jnp.sum(edges, axis=1, keepdims=True), (8, LANES))[:, 0:own_seg]
 
-    totals = jnp.transpose(total1)
-    sum_s = tuple(totals[axis : axis + 1] + edge_sum_s[axis] for axis in range(3))
-    by_point, by_norm = cross(own_n, sum_s), cross(sum_s, own_p)
+    totals = receiver_totals(new1_ref, own_refs[0])
+    by_point, by_norm = cross(own_n, edge_sum_s), cross(edge_sum_s, own_p)
     for axis in range(3):
-        value = by_point[axis] + (totals[6 + axis : 7 + axis] + edge_sum_p[axis])
+        value = totals[axis : axis + 1] + (by_point[axis] + edge_sum_p[axis])
         rcv_out[axis : axis + 1, :] = 0.2 * value if axis == 2 else value
-        rcv_out[3 + axis : 4 + axis, :] = by_norm[axis] - (totals[3 + axis : 4 + axis] + edge_sum_t[axis])
-
-    totals = jnp.transpose(total2)
-    sum_n = tuple(totals[axis : axis + 1] for axis in range(3))
-    own_e, own_s, _, _, _ = own_segments(own_block, own_seg)
-    own_e = tuple(value[:, 0:own_seg] for value in own_e)
-    own_s = tuple(value[:, 0:own_seg] for value in own_s)
-    turned, swept = cross(own_e, sum_n), cross(sum_n, own_s)
+        rcv_out[3 + axis : 4 + axis, :] = totals[3 + axis : 4 + axis] + (by_norm[axis] - edge_sum_t[axis])
+
+    totals = segment_totals(new2_ref, own_refs[1], own_seg)
     lane = lane[:, 0:own_seg]
     for axis in range(3):
-        by_second = totals[3 + axis : 4 + axis] - turned[axis] + own_s[axis] * totals[10:11]
-        by_rel = swept[axis] + totals[6 + axis : 7 + axis] + own_s[axis] * totals[9:10]
+        by_second = totals[axis : axis + 1]
         shifted = jnp.concatenate([by_second[:, own_seg - 1 :], by_second[:, : own_seg - 1]], 1)
-        result = jnp.where(lane == 0, edges[3 + axis : 4 + axis], shifted) - (by_second + by_rel)
+        result = jnp.where(lane == 0, edges[3 + axis : 4 + axis], shifted) - totals[3 + axis : 4 + axis]
         result = result - jnp.where(lane == own_seg - 1, edges[axis : axis + 1], 0.0)
         vert_out[axis : axis + 1, :] = 0.2 * result if axis == 2 else result
 
@@ -381,7 +392,7 @@
 
 
 def last_scratch(count, own_seg):
-    return [pltpu.VMEM((count, 8, LANES), jnp.float32)] + sum_shapes(own_seg) + pair_scratch(count // 2, own_seg)
+    return [pltpu.VMEM((count, 8, LANES), jnp.float32)] + sum_shapes(own_seg) + pair_scratch(count // 4, own_seg)
 
 
 def pair_cost(blocks, own_seg):
@@ -405,39 +416,47 @@
             *sum_shapes(own_seg),
             pltpu.VMEM((LANES, 32), jnp.bfloat16),
             pltpu.VMEM((own_seg, 32), jnp.bfloat16),
-            pltpu.VMEM((11 * LANES, 16), jnp.bfloat16),
         ),
         in_specs=[VMEM],
-        out_specs=(VMEM,) * 5,
+        out_specs=(VMEM,) * 4,
         cost_estimate=pair_cost(2, own_seg),
         compiler_params=params,
     )(value)
-    sums = ()
-    for mask in exchange_masks(count):
-        held = value.shape[0]
-        other = lax.ppermute(value, "src", [(s, s ^ mask) for s in range(count)])
-        if held in (count // 4, count // 2):
-            begin = 0 if held == count // 4 else count // 4
-            sums = pl.pallas_call(
-                functools.partial(early_kernel, begin, held, own_seg),
-                out_shape=tuple(sum_shapes(own_seg)),
-                in_specs=[VMEM] * (6 + len(sums)),
-                out_specs=(VMEM, VMEM),
-                scratch_shapes=pair_scratch(held - begin, own_seg),
-                cost_estimate=pair_cost(held - begin, own_seg),
-                compiler_params=params,
-            )(value, *own, *sums)
-        value = jnp.concatenate([value, other], 0)
+
+    def exchange(block, mask):
+        return lax.ppermute(block, "src", [(s, s ^ mask) for s in range(count)])
+
+    def add_pairs(block, *sums):
+        return pl.pallas_call(
+            functools.partial(early_kernel, len(sums) > 0, own_seg),
+            out_shape=tuple(sum_shapes(own_seg)),
+            in_specs=[VMEM] * (5 + len(sums)),
+            out_specs=(VMEM, VMEM),
+            scratch_shapes=pair_scratch(block.shape[0], own_seg),
+            cost_estimate=pair_cost(block.shape[0], own_seg),
+            compiler_params=params,
+        )(block, *own, *sums)
+
+    masks = exchange_masks(count)
+    for mask in masks[:-2]:
+        value = jnp.concatenate([value, exchange(value, mask)], 0)
+    across, beside = exchange(value, masks[-2]), exchange(value, masks[-1])
+    sums = add_pairs(value)
+    sums = add_pairs(beside, *sums)
+    across, sums = lax.optimization_barrier((across, sums))
+    opposite = exchange(across, masks[-1])
+    sums = add_pairs(across, *sums)
+    value = jnp.concatenate([value, across, beside, opposite], 0)
     return pl.pallas_call(
         functools.partial(last_kernel, count, own_seg),
         out_shape=(
             jax.ShapeDtypeStruct((6, LANES), jnp.float32),
             jax.ShapeDtypeStruct((3, own_seg), jnp.float32),
         ),
-        in_specs=[VMEM] * 8,
+        in_specs=[VMEM] * 7,
         out_specs=(VMEM, VMEM),
         scratch_shapes=last_scratch(count, own_seg),
-        cost_estimate=pair_cost(count // 2, own_seg),
+        cost_estimate=pair_cost(count // 4, own_seg),
         compiler_params=params,
     )(value, *own, *sums)
 

time: 18.2 us -> 17.8 us (0.978)
  waiting for transfers between devices: 3.17 us -> 2.95 us
    pallas_call x1, Pallas kernels: 3.13 us -> 2.23 us  [on_device(): pl.pallas_call(functools.partial(last_kernel, count, own_seg), out_shape=...]
    pallas_call x2 -> x3, Pallas kernels: 1.7 us -> 2.57 us  [add_pairs(): pl.pallas_call(functools.partial(early_kernel, len(sums) > 0, own_seg), o...]
    ppermute x4 -> x5, waiting for transfers between devices: 3.17 us -> 2.95 us  [exchange(): return lax.ppermute(block, 'src', [(s, s ^ mask) for s in range(count)])]
    ppermute x4 -> x5, starting transfers between devices: 7.65 us -> 7.59 us  [exchange(): return lax.ppermute(block, 'src', [(s, s ^ mask) for s in range(count)])]
  transfers between devices with their start and end apart: 4 -> 5, of which waited for: 4 -> 4; matrix products, arithmetic and copies ran while one was open for 0% -> 0% of each run, Pallas kernels for 14% -> 18%
where the time goes in v7:
time: 17.8 us; the launch traced here: 17.6 us
  starting transfers between devices  7.59 us (43%)
  Pallas kernels  6.4 us (36%)
  waiting for transfers between devices  2.95 us (17%)
  between operations  0.68 us (4%)
    ppermute x5, starting transfers between devices, exchange(): return lax.ppermute(block, 'src', [(s, s ^ mask) for s in range(count)])  7.59 us
    ppermute x5, waiting for transfers between devices, exchange(): return lax.ppermute(block, 'src', [(s, s ^ mask) for s in range(count)])  2.95 us
    pallas_call x3, Pallas kernels, add_pairs(): pl.pallas_call(functools.partial(early_kernel, len(sums) > 0, own_seg), o...  2.57 us
    pallas_call x1, Pallas kernels, on_device(): pl.pallas_call(functools.partial(last_kernel, count, own_seg), out_shape=...  2.23 us
    pallas_call x1, Pallas kernels, on_device(): pl.pallas_call(functools.partial(pack_kernel, own_seg), out_shape=pltpu.V...  0.92 us
    pallas_call x1, Pallas kernels, on_device(): pl.pallas_call(functools.partial(own_kernel, own_seg), out_shape=(*sum_sh...  0.68 us
  transfers between devices with their start and end apart: 5, of which 4 were waited for; matrix products, arithmetic and copies ran while one was open for 0% of the time, Pallas kernels for 18%

profile of v7, /device:TPU:0, one launch (start us, length us, event | category | flops | bytes accessed | tf_op | source)
XLA Modules:
  0.0 17.6 jit_solution(830329343504663275)
XLA Ops:
  0.6 0.9 %shard_map.86 = f32[24,128]{1,0:T(8,128)S(1)} custom-call(f32[3,128]{1,0:T(4,128)} %points_ref.1, f32[3,128]{1,0:T(4,128)} %normals_ref.1, f32[8,128]{1,0:T(8,128)} %left_ref.1, f32[3,64]{1,0:T(4,128)} %vertices_ref.1, s32[2,128]{1,0:T(2,128)} %connect_ref.1, f32[8,128]{1,0:T(8,128)} %right_ref.1, f32[8]{0:T(128)} %weights_ref.1), custom_call_target="tpu_custom_call" | custom-call | tf_op jit(solution)/shard_map/pallas_call | solution.py:406
  1.5 3.5 %collective-permute-start = (f32[1,24,128]{2,1,0:T(8,128)S(1)}, f32[1,24,128]{2,1,0:T(8,128)S(1)}, u32[]{:S(2)}, u32[]{:S(2)}) collective-permute-start(f32[1,24,128]{2,1,0:T(8,128)S(1)} %bitcast.2), channel_id=1, source_target_pairs={{0,9},{1,8},{2,11},{3,10},{4,13},{5,12},{6,15},{7,14},{8,1},{9,0},... | collective-permute-start | bytes 36872 | tf_op jit(solution)/shard_map/ppermute | solution.py:427
  5.1 0.7 %shard_map.87 = (f32[9,128,128]{2,1,0:T(8,128)S(1)}, f32[11,64,128]{2,1,0:T(8,128)S(1)}, bf16[128,32]{1,0:T(8,128)(2,1)S(1)}, bf16[64,32]{1,0:T(8,128)(2,1)S(1)}) custom-call(f32[1,24,128]{2,1,0:T(8,128)S(1)} %bitcast.3), custom_call_target="tpu_custom_call" | custom-call | flops 3276800 | bytes 24576 | tf_op jit(solution)/shard_map/pallas_call | solution.py:413
  5.8 0.7 %collective-permute-done = f32[1,24,128]{2,1,0:T(8,128)S(1)} collective-permute-done((f32[1,24,128]{2,1,0:T(8,128)S(1)}, f32[1,24,128]{2,1,0:T(8,128)S(1)}, u32[]{:S(2)}, u32[]{:S(2)}) %collective-permute-start) | collective-permute-done | bytes 12320 | tf_op jit(solution)/shard_map/ppermute | solution.py:427
  6.5 1.9 %collective-permute-start.1 = (f32[2,24,128]{2,1,0:T(8,128)S(1)}, f32[2,24,128]{2,1,0:T(8,128)S(1)}, u32[]{:S(2)}, u32[]{:S(2)}) collective-permute-start(f32[2,24,128]{2,1,0:T(8,128)S(1)} %pad_maximum_fusion.1), channel_id=1, source_target_pairs={{0,5},{1,4},{2,7},{3,6},{4,1},{5,0},{6,3},{7,2},{8,13},{9,12},{10,... | collective-permute-start | bytes 73736 | tf_op jit(solution)/shard_map/ppermute | solution.py:427
  8.4 1.5 %collective-permute-done.1 = f32[2,24,128]{2,1,0:T(8,128)S(1)} collective-permute-done((f32[2,24,128]{2,1,0:T(8,128)S(1)}, f32[2,24,128]{2,1,0:T(8,128)S(1)}, u32[]{:S(2)}, u32[]{:S(2)}) %collective-permute-start.1) | collective-permute-done | bytes 24608 | tf_op jit(solution)/shard_map/ppermute | solution.py:427
  9.9 0.5 %collective-permute-start.3 = (f32[4,24,128]{2,1,0:T(8,128)S(1)}, f32[4,24,128]{2,1,0:T(8,128)S(1)}, u32[]{:S(2)}, u32[]{:S(2)}) collective-permute-start(f32[4,24,128]{2,1,0:T(8,128)S(1)} %pad_maximum_fusion.refs_0_), channel_id=1, source_target_pairs={{0,1},{1,0},{2,3},{3,2},{4,5},{5,4},{6,7},{7,6},{8,9},{9,8},{10,11... | collective-permute-start | bytes 147464 | tf_op jit(solution)/shard_map/ppermute | solution.py:427
  10.4 1.6 %collective-permute-start.2 = (f32[4,24,128]{2,1,0:T(8,128)S(1)}, f32[4,24,128]{2,1,0:T(8,128)S(1)}, u32[]{:S(2)}, u32[]{:S(2)}) collective-permute-start(f32[4,24,128]{2,1,0:T(8,128)S(1)} %pad_maximum_fusion.refs_0_), channel_id=1, source_target_pairs={{0,3},{1,2},{2,1},{3,0},{4,7},{5,6},{6,5},{7,4},{8,11},{9,10},{10,... | collective-permute-start | bytes 147464 | tf_op jit(solution)/shard_map/ppermute | solution.py:427
  12.0 0.8 %shard_map.88 = (f32[9,128,128]{2,1,0:T(8,128)S(1)}, f32[11,64,128]{2,1,0:T(8,128)S(1)}) custom-call(f32[4,24,128]{2,1,0:T(8,128)S(1)} %pad_maximum_fusion.refs_0_, f32[9,128,128]{2,1,0:T(8,128)S(1)} %get-tuple-element.15.refs_1_, f32[11,64,128]{2,1,0:T(8,128)S(1)} %get-tuple-element.16.refs_2_, bf16[128,32]{1,0:T(8,128)(2,1)S(1)} %get-tuple-element.17.refs_3_, ...), custom_call_target="tpu_custom_call" | custom-call | flops 6553600 | bytes 49152 | tf_op jit(solution)/shard_map/pallas_call | solution.py:430
  12.8 0.0 collective-permute-done.3.refs_0_
  12.8 0.9 %shard_map.89 = (f32[9,128,128]{2,1,0:T(8,128)S(1)}, f32[11,64,128]{2,1,0:T(8,128)S(1)}) custom-call(f32[4,24,128]{2,1,0:T(8,128)S(1)} %collective-permute-done.3.refs_0_, f32[9,128,128]{2,1,0:T(8,128)S(1)} %get-tuple-element.15.refs_1_, f32[11,64,128]{2,1,0:T(8,128)S(1)} %get-tuple-element.16.refs_2_, bf16[128,32]{1,0:T(8,128)(2,1)S(1)} %get-tuple-element.17.refs_3_, ...), custom_call_target="tpu_custom_call" | custom-call | flops 6553600 | bytes 49152 | tf_op jit(solution)/shard_map/pallas_call | solution.py:430
  13.7 0.5 %collective-permute-done.2.refs_0_ = f32[4,24,128]{2,1,0:T(8,128)S(1)} collective-permute-done((f32[4,24,128]{2,1,0:T(8,128)S(1)}, f32[4,24,128]{2,1,0:T(8,128)S(1)}, u32[]{:S(2)}, u32[]{:S(2)}) %collective-permute-start.2) | collective-permute-done | bytes 49184 | tf_op jit(solution)/shard_map/ppermute | solution.py:427
  14.2 0.1 collective-permute-start.4
  14.3 0.9 %shard_map.90 = (f32[9,128,128]{2,1,0:T(8,128)S(1)}, f32[11,64,128]{2,1,0:T(8,128)S(1)}) custom-call(f32[4,24,128]{2,1,0:T(8,128)S(1)} %collective-permute-done.2.refs_0_, f32[9,128,128]{2,1,0:T(8,128)S(1)} %get-tuple-element.15.refs_1_, f32[11,64,128]{2,1,0:T(8,128)S(1)} %get-tuple-element.16.refs_2_, bf16[128,32]{1,0:T(8,128)(2,1)S(1)} %get-tuple-element.17.refs_3_, ...), custom_call_target="tpu_custom_call" | custom-call | flops 6553600 | bytes 49152 | tf_op jit(solution)/shard_map/pallas_call | solution.py:430
  15.2 0.2 %collective-permute-done.4 = f32[4,24,128]{2,1,0:T(8,128)S(1)} collective-permute-done((f32[4,24,128]{2,1,0:T(8,128)S(1)}, f32[4,24,128]{2,1,0:T(8,128)S(1)}, u32[]{:S(2)}, u32[]{:S(2)}) %collective-permute-start.4) | collective-permute-done | bytes 49184 | tf_op jit(solution)/shard_map/ppermute | solution.py:427
  15.4 2.2 %shard_map.91 = (f32[6,128]{1,0:T(8,128)}, f32[3,64]{1,0:T(4,128)}) custom-call(f32[16,24,128]{2,1,0:T(8,128)S(1)} %constant_dynamic-update-slice_fusion.refs_0_, f32[9,128,128]{2,1,0:T(8,128)S(1)} %get-tuple-element.15.refs_1_, f32[11,64,128]{2,1,0:T(8,128)S(1)} %get-tuple-element.16.refs_2_, bf16[128,32]{1,0:T(8,128)(2,1)S(1)} %get-tuple-element.17.refs_3_, ...), custom_call_target="tpu_custom_call" | custom-call | flops 6553600 | bytes 49152 | tf_op jit(solution)/shard_map/pallas_call | solution.py:450
  (8 shorter events, 0.0 us)
Async XLA Ops:
  1.5 4.9 %collective-permute-start = (f32[1,24,128]{2,1,0:T(8,128)S(1)}, f32[1,24,128]{2,1,0:T(8,128)S(1)}, u32[]{:S(2)}, u32[]{:S(2)}) collective-permute-start(f32[1,24,128]{2,1,0:T(8,128)S(1)} %bitcast.2), channel_id=1, source_target_pairs={{0,9},{1,8},{2,11},{3,10},{4,13},{5,12},{6,15},{7,14},{8,1},{9,0},... | collective-permute-start | bytes 36872 | tf_op jit(solution)/shard_map/ppermute | solution.py:427
  6.5 3.4 %collective-permute-start.1 = (f32[2,24,128]{2,1,0:T(8,128)S(1)}, f32[2,24,128]{2,1,0:T(8,128)S(1)}, u32[]{:S(2)}, u32[]{:S(2)}) collective-permute-start(f32[2,24,128]{2,1,0:T(8,128)S(1)} %pad_maximum_fusion.1), channel_id=1, source_target_pairs={{0,5},{1,4},{2,7},{3,6},{4,1},{5,0},{6,3},{7,2},{8,13},{9,12},{10,... | collective-permute-start | bytes 73736 | tf_op jit(solution)/shard_map/ppermute | solution.py:427
  9.9 2.9 %collective-permute-start.3 = (f32[4,24,128]{2,1,0:T(8,128)S(1)}, f32[4,24,128]{2,1,0:T(8,128)S(1)}, u32[]{:S(2)}, u32[]{:S(2)}) collective-permute-start(f32[4,24,128]{2,1,0:T(8,128)S(1)} %pad_maximum_fusion.refs_0_), channel_id=1, source_target_pairs={{0,1},{1,0},{2,3},{3,2},{4,5},{5,4},{6,7},{7,6},{8,9},{9,8},{10,11... | collective-permute-start | bytes 147464 | tf_op jit(solution)/shard_map/ppermute | solution.py:427
  10.4 3.8 %collective-permute-start.2 = (f32[4,24,128]{2,1,0:T(8,128)S(1)}, f32[4,24,128]{2,1,0:T(8,128)S(1)}, u32[]{:S(2)}, u32[]{:S(2)}) collective-permute-start(f32[4,24,128]{2,1,0:T(8,128)S(1)} %pad_maximum_fusion.refs_0_), channel_id=1, source_target_pairs={{0,3},{1,2},{2,1},{3,0},{4,7},{5,6},{6,5},{7,4},{8,11},{9,10},{10,... | collective-permute-start | bytes 147464 | tf_op jit(solution)/shard_map/ppermute | solution.py:427
  14.2 1.2 %collective-permute-start.4 = (f32[4,24,128]{2,1,0:T(8,128)S(1)}, f32[4,24,128]{2,1,0:T(8,128)S(1)}, u32[]{:S(2)}, u32[]{:S(2)}) collective-permute-start(f32[4,24,128]{2,1,0:T(8,128)S(1)} %collective-permute-done.2.refs_0_), channel_id=1, source_target_pairs={{0,1},{1,0},{2,3},{3,2},{4,5},{5,4},{6,7},{7,6},{8,9},{9,8},{10,11... | collective-permute-start | bytes 147464 | tf_op jit(solution)/shard_map/ppermute | solution.py:427

commit v8 on v7

--- a/solution.py
+++ b/solution.py
@@ -151,7 +151,7 @@
     right_ref[...] = stack_hhll(jnp.where(lane_edges(own_seg), 0.0, own_block))[0:own_seg]
 
 
-def pair_sums(data_ref, own_refs, begin, end, own_seg, scratch, old1, old2, new1, new2):
+def pair_sums(data_ref, own_refs, begin, end, own_seg, scratch, old1, old2, new1, new2, between=None):
     seg_ref, rec_ref, scale1_ref, scale2_ref = scratch
     col1_ref, col2_ref, left_ref, right_ref = own_refs
     blocks = end - begin
@@ -212,6 +212,9 @@
         for k in range(9):
             new1[k, start : start + CHUNK, :] = sums[k]
 
+    if between is not None:
+        between()
+
     for start in range(0, own_seg, CHUNK):
         col = [col2_ref[k, start : start + CHUNK, :] for k in range(11)]
         sums = initial(old2, 11, start)
@@ -250,7 +253,7 @@
     return jnp.transpose(jnp.concatenate(parts, 0))
 
 
-def segment_totals(sums_ref, col_ref, own_seg):
+def segment_totals(sums_ref, col_ref, own_seg, arriving, leaving):
     parts = []
     for start in range(0, own_seg, FINISH):
         sums = [sums_ref[k, start : start + FINISH, :] for k in range(11)]
@@ -258,6 +261,10 @@
         turned, swept = cross(col[0:3], sums[0:3]), cross(sums[0:3], col[3:6])
         by_s = [sums[3 + k] - turned[k] + col[3 + k] * sums[10] for k in range(3)]
         by_both = [by_s[k] + (swept[k] + sums[6 + k] + col[3 + k] * sums[9]) for k in range(3)]
+        if start + FINISH == own_seg:
+            last = lax.broadcasted_iota(jnp.int32, (FINISH, LANES), 0) == FINISH - 1
+            by_s = [jnp.where(last, a, b) for a, b in zip(arriving, by_s)]
+            by_both = [jnp.where(last, a, b) for a, b in zip(leaving, by_both)]
         parts.append(lane_sums(by_s + by_both))
     return jnp.transpose(jnp.concatenate(parts, 0))
 
@@ -295,86 +302,87 @@
     def place(device):
         return place_of((device & (count - 1)) ^ me, masks)
 
+    def edge_sums():
+        for block in range(count):
+            after_ref[block] = data_ref[place((me ^ mask_at(block, masks)) + 1), 16:24, :]
+
+        def spread(column):
+            return jnp.broadcast_to(column, (column.shape[0], LANES))
+
+        own_block = data_ref[0, 16:24, :]
+        before = data_ref[place(me + count - 1), 16:24, :]
+        own_p, own_n, own_m = own_receivers(data_ref)
+        point = tuple(data_ref[:, 8 + axis, :] for axis in range(3))
+        normal = tuple(data_ref[:, 11 + axis, :] for axis in range(3))
+        moment = cross(point, normal)
+        mine_last = spread(own_block[:, 2 * own_seg - 1 : 2 * own_seg])
+        mine_next = spread(after_ref[0, :, own_seg : own_seg + 1])
+        mine_weight = spread(own_block[:, own_seg - 1 : own_seg])
+        before_last = spread(before[:, 2 * own_seg - 1 : 2 * own_seg])
+        before_weight = spread(jnp.where(me == 0, 0.0, before[:, own_seg - 1 : own_seg]))
+        mine_first = spread(own_block[:, own_seg : own_seg + 1])
+
+        def rows(value, axis):
+            return jnp.broadcast_to(value[axis : axis + 1], (count, LANES))
+
+        def stacked(own, every):
+            return tuple(
+                jnp.concatenate([jnp.broadcast_to(a, (count, LANES)), b, b], 0) for a, b in zip(own, every))
+
+        first = tuple(
+            jnp.concatenate(
+                [spread(data_ref[:, 16 + axis, 2 * own_seg - 1 : 2 * own_seg]), rows(mine_last, axis), rows(before_last, axis)], 0)
+            for axis in range(3))
+        second = tuple(
+            jnp.concatenate(
+                [spread(after_ref[:, axis, own_seg : own_seg + 1]), rows(mine_next, axis), rows(mine_first, axis)], 0)
+            for axis in range(3))
+        scales = [jnp.zeros((count, LANES), jnp.float32)] * 3
+        for mode in range(8):
+            left = data_ref[:, mode, :]
+            scales[0] += spread(data_ref[:, 16 + mode, own_seg - 1 : own_seg]) * data_ref[0, mode : mode + 1, :]
+            scales[1] += mine_weight[mode : mode + 1] * left
+            scales[2] += before_weight[mode : mode + 1] * left
+        segment, turn, span, span_core = segment_terms(first, second)
+        normals = stacked(own_n, normal)
+        rel, by_normal, by_dist2, by_along, by_span2 = pair_terms(
+            stacked(own_p, point), normals, stacked(own_m, moment),
+            first, segment, turn, span, span_core, jnp.concatenate(scales, 0), True)
+
+        def down(value):
+            return jnp.sum(value, axis=0, keepdims=True)
+
+        against_own, mine, ahead = slice(0, count), slice(count, 2 * count), slice(2 * count, 3 * count)
+        swung, swept = cross(rel, normals), cross(normals, segment)
+        edge_s = [(by_normal * segment[axis])[against_own] for axis in range(3)]
+        edge_t = [(by_normal * turn[axis])[against_own] for axis in range(3)]
+        edge_point = [a for a in cross(own_n, edge_s)]
+        edge_normal = [down(a - b) for a, b in zip(cross(edge_s, own_p), edge_t)]
+        leaving, arriving = [], []
+        for axis in range(3):
+            by_s = by_normal * swung[axis] + by_along * rel[axis] + by_span2 * segment[axis]
+            by_p = by_dist2 * rel[axis] + by_along * segment[axis]
+            by_r = by_normal * swept[axis] + by_p
+            edge_point[axis] = down(edge_point[axis] + by_p[against_own])
+            leaving.append(down((by_s + by_r)[mine]))
+            arriving.append(down(by_s[ahead]))
+        return edge_point, edge_normal, arriving, leaving
+
+    found = []
     pair_sums(
-        data_ref, own_refs, count - count // 4, count, own_seg, scratch, old1_ref, old2_ref, new1_ref, new2_ref)
-    for block in range(count):
-        after_ref[block] = data_ref[place((me ^ mask_at(block, masks)) + 1), 16:24, :]
-
-    def spread(column):
-        return jnp.broadcast_to(column, (column.shape[0], LANES))
-
-    own_block = data_ref[0, 16:24, :]
-    before = data_ref[place(me + count - 1), 16:24, :]
-    own_p, own_n, own_m = own_receivers(data_ref)
-    point = tuple(data_ref[:, 8 + axis, :] for axis in range(3))
-    normal = tuple(data_ref[:, 11 + axis, :] for axis in range(3))
-    moment = cross(point, normal)
-    mine_last = spread(own_block[:, 2 * own_seg - 1 : 2 * own_seg])
-    mine_next = spread(after_ref[0, :, own_seg : own_seg + 1])
-    mine_weight = spread(own_block[:, own_seg - 1 : own_seg])
-    before_last = spread(before[:, 2 * own_seg - 1 : 2 * own_seg])
-    before_weight = spread(jnp.where(me == 0, 0.0, before[:, own_seg - 1 : own_seg]))
-    mine_first = spread(own_block[:, own_seg : own_seg + 1])
-
-    def rows(value, axis):
-        return jnp.broadcast_to(value[axis : axis + 1], (count, LANES))
-
-    def stacked(own, every):
-        return tuple(
-            jnp.concatenate([jnp.broadcast_to(a, (count, LANES)), b, b], 0) for a, b in zip(own, every))
-
-    first = tuple(
-        jnp.concatenate(
-            [spread(data_ref[:, 16 + axis, 2 * own_seg - 1 : 2 * own_seg]), rows(mine_last, axis), rows(before_last, axis)], 0)
-        for axis in range(3))
-    second = tuple(
-        jnp.concatenate(
-            [spread(after_ref[:, axis, own_seg : own_seg + 1]), rows(mine_next, axis), rows(mine_first, axis)], 0)
-        for axis in range(3))
-    scales = [jnp.zeros((count, LANES), jnp.float32)] * 3
-    for mode in range(8):
-        left = data_ref[:, mode, :]
-        scales[0] += spread(data_ref[:, 16 + mode, own_seg - 1 : own_seg]) * data_ref[0, mode : mode + 1, :]
-        scales[1] += mine_weight[mode : mode + 1] * left
-        scales[2] += before_weight[mode : mode + 1] * left
-    segment, turn, span, span_core = segment_terms(first, second)
-    normals = stacked(own_n, normal)
-    rel, by_normal, by_dist2, by_along, by_span2 = pair_terms(
-        stacked(own_p, point), normals, stacked(own_m, moment),
-        first, segment, turn, span, span_core, jnp.concatenate(scales, 0), True)
-
-    def down(value):
-        return jnp.sum(value, axis=0, keepdims=True)
-
-    against_own, mine, ahead = slice(0, count), slice(count, 2 * count), slice(2 * count, 3 * count)
-    swung, swept = cross(rel, normals), cross(normals, segment)
-    edge_sum_s, edge_sum_t, edge_sum_p, leaving, arriving = [], [], [], [], []
+        data_ref, own_refs, count - count // 4, count, own_seg, scratch, old1_ref, old2_ref, new1_ref, new2_ref,
+        lambda: found.extend((*edge_sums(), receiver_totals(new1_ref, own_refs[0]))))
+    edge_point, edge_normal, arriving, leaving, totals = found
     for axis in range(3):
-        by_s = by_normal * swung[axis] + by_along * rel[axis] + by_span2 * segment[axis]
-        by_p = by_dist2 * rel[axis] + by_along * segment[axis]
-        by_r = by_normal * swept[axis] + by_p
-        edge_sum_s.append(down((by_normal * segment[axis])[against_own]))
-        edge_sum_t.append(down((by_normal * turn[axis])[against_own]))
-        edge_sum_p.append(down(by_p[against_own]))
-        leaving.append(down((by_s + by_r)[mine]))
-        arriving.append(down(by_s[ahead]))
-    edges = jnp.concatenate(leaving + arriving + leaving[0:2], 0)
-    edges = jnp.broadcast_to(jnp.sum(edges, axis=1, keepdims=True), (8, LANES))[:, 0:own_seg]
-
-    totals = receiver_totals(new1_ref, own_refs[0])
-    by_point, by_norm = cross(own_n, edge_sum_s), cross(edge_sum_s, own_p)
-    for axis in range(3):
-        value = totals[axis : axis + 1] + (by_point[axis] + edge_sum_p[axis])
+        value = totals[axis : axis + 1] + edge_point[axis]
         rcv_out[axis : axis + 1, :] = 0.2 * value if axis == 2 else value
-        rcv_out[3 + axis : 4 + axis, :] = totals[3 + axis : 4 + axis] + (by_norm[axis] - edge_sum_t[axis])
-
-    totals = segment_totals(new2_ref, own_refs[1], own_seg)
-    lane = lane[:, 0:own_seg]
+        rcv_out[3 + axis : 4 + axis, :] = totals[3 + axis : 4 + axis] + edge_normal[axis]
+
+    totals = segment_totals(new2_ref, own_refs[1], own_seg, arriving, leaving)
     for axis in range(3):
         by_second = totals[axis : axis + 1]
         shifted = jnp.concatenate([by_second[:, own_seg - 1 :], by_second[:, : own_seg - 1]], 1)
-        result = jnp.where(lane == 0, edges[3 + axis : 4 + axis], shifted) - totals[3 + axis : 4 + axis]
-        result = result - jnp.where(lane == own_seg - 1, edges[axis : axis + 1], 0.0)
+        result = shifted - totals[3 + axis : 4 + axis]
         vert_out[axis : axis + 1, :] = 0.2 * result if axis == 2 else result
 
 
@@ -438,12 +446,16 @@
         )(block, *own, *sums)
 
     masks = exchange_masks(count)
-    for mask in masks[:-2]:
+    for mask in masks[:-3]:
         value = jnp.concatenate([value, exchange(value, mask)], 0)
-    across, beside = exchange(value, masks[-2]), exchange(value, masks[-1])
+    arrived, early = exchange(value, masks[-3]), exchange(value, masks[-2])
+    late = exchange(arrived, masks[-2])
+    value = jnp.concatenate([value, arrived], 0)
+    beside = exchange(value, masks[-1])
     sums = add_pairs(value)
     sums = add_pairs(beside, *sums)
-    across, sums = lax.optimization_barrier((across, sums))
+    late, sums = lax.optimization_barrier((late, sums))
+    across = jnp.concatenate([early, late], 0)
     opposite = exchange(across, masks[-1])
     sums = add_pairs(across, *sums)
     value = jnp.concatenate([value, across, beside, opposite], 0)

time: 17.8 us -> 17.4 us (0.978)
  waiting for transfers between devices: 2.95 us -> 0.93 us
  starting transfers between devices: 7.59 us -> 9.2 us
    ppermute x5 -> x6, waiting for transfers between devices: 2.95 us -> 0.93 us  [exchange(): return lax.ppermute(block, 'src', [(s, s ^ mask) for s in range(count)])]
    ppermute x5 -> x6, starting transfers between devices: 7.59 us -> 9.2 us  [exchange(): return lax.ppermute(block, 'src', [(s, s ^ mask) for s in range(count)])]
  transfers between devices with their start and end apart: 5 -> 6, of which waited for: 4 -> 2; matrix products, arithmetic and copies ran while one was open for 0% -> 0% of each run, Pallas kernels for 18% -> 19%
where the time goes in v8:
time: 17.4 us; the launch traced here: 17.2 us
  starting transfers between devices  9.2 us (53%)
  Pallas kernels  6.36 us (37%)
  waiting for transfers between devices  0.93 us (5%)
  between operations  0.7 us (4%)
    ppermute x6, starting transfers between devices, exchange(): return lax.ppermute(block, 'src', [(s, s ^ mask) for s in range(count)])  9.2 us
    pallas_call x3, Pallas kernels, add_pairs(): pl.pallas_call(functools.partial(early_kernel, len(sums) > 0, own_seg), o...  2.57 us
    pallas_call x1, Pallas kernels, on_device(): pl.pallas_call(functools.partial(last_kernel, count, own_seg), out_shape=...  2.19 us
    ppermute x6, waiting for transfers between devices, exchange(): return lax.ppermute(block, 'src', [(s, s ^ mask) for s in range(count)])  0.93 us
    pallas_call x1, Pallas kernels, on_device(): pl.pallas_call(functools.partial(pack_kernel, own_seg), out_shape=pltpu.V...  0.92 us
    pallas_call x1, Pallas kernels, on_device(): pl.pallas_call(functools.partial(own_kernel, own_seg), out_shape=(*sum_sh...  0.68 us
  transfers between devices with their start and end apart: 6, of which 2 were waited for; matrix products, arithmetic and copies ran while one was open for 0% of the time, Pallas kernels for 19%

profile of v8, /device:TPU:0, one launch (start us, length us, event | category | flops | bytes accessed | tf_op | source)
XLA Modules:
  0.0 17.2 jit_solution(14059630330455806900)
XLA Ops:
  0.6 0.9 %shard_map.86 = f32[24,128]{1,0:T(8,128)S(1)} custom-call(f32[3,128]{1,0:T(4,128)} %points_ref.1, f32[3,128]{1,0:T(4,128)} %normals_ref.1, f32[8,128]{1,0:T(8,128)} %left_ref.1, f32[3,64]{1,0:T(4,128)} %vertices_ref.1, s32[2,128]{1,0:T(2,128)} %connect_ref.1, f32[8,128]{1,0:T(8,128)} %right_ref.1, f32[8]{0:T(128)} %weights_ref.1), custom_call_target="tpu_custom_call" | custom-call | tf_op jit(solution)/shard_map/pallas_call | solution.py:414
  1.5 3.5 %collective-permute-start = (f32[1,24,128]{2,1,0:T(8,128)S(1)}, f32[1,24,128]{2,1,0:T(8,128)S(1)}, u32[]{:S(2)}, u32[]{:S(2)}) collective-permute-start(f32[1,24,128]{2,1,0:T(8,128)S(1)} %bitcast.2), channel_id=1, source_target_pairs={{0,9},{1,8},{2,11},{3,10},{4,13},{5,12},{6,15},{7,14},{8,1},{9,0},... | collective-permute-start | bytes 36872 | tf_op jit(solution)/shard_map/ppermute | solution.py:435
  5.1 0.7 %shard_map.87 = (f32[9,128,128]{2,1,0:T(8,128)S(1)}, f32[11,64,128]{2,1,0:T(8,128)S(1)}, bf16[128,32]{1,0:T(8,128)(2,1)S(1)}, bf16[64,32]{1,0:T(8,128)(2,1)S(1)}) custom-call(f32[1,24,128]{2,1,0:T(8,128)S(1)} %bitcast.3), custom_call_target="tpu_custom_call" | custom-call | flops 3276800 | bytes 24576 | tf_op jit(solution)/shard_map/pallas_call | solution.py:421
  5.8 0.7 %collective-permute-done = f32[1,24,128]{2,1,0:T(8,128)S(1)} collective-permute-done((f32[1,24,128]{2,1,0:T(8,128)S(1)}, f32[1,24,128]{2,1,0:T(8,128)S(1)}, u32[]{:S(2)}, u32[]{:S(2)}) %collective-permute-start) | collective-permute-done | bytes 12320 | tf_op jit(solution)/shard_map/ppermute | solution.py:435
  6.5 1.9 %collective-permute-start.1 = (f32[2,24,128]{2,1,0:T(8,128)S(1)}, f32[2,24,128]{2,1,0:T(8,128)S(1)}, u32[]{:S(2)}, u32[]{:S(2)}) collective-permute-start(f32[2,24,128]{2,1,0:T(8,128)S(1)} %pad_maximum_fusion.1), channel_id=1, source_target_pairs={{0,5},{1,4},{2,7},{3,6},{4,1},{5,0},{6,3},{7,2},{8,13},{9,12},{10,... | collective-permute-start | bytes 73736 | tf_op jit(solution)/shard_map/ppermute | solution.py:435
  8.4 1.6 %collective-permute-start.2 = (f32[2,24,128]{2,1,0:T(8,128)S(1)}, f32[2,24,128]{2,1,0:T(8,128)S(1)}, u32[]{:S(2)}, u32[]{:S(2)}) collective-permute-start(f32[2,24,128]{2,1,0:T(8,128)S(1)} %pad_maximum_fusion.1), channel_id=1, source_target_pairs={{0,3},{1,2},{2,1},{3,0},{4,7},{5,6},{6,5},{7,4},{8,11},{9,10},{10,... | collective-permute-start | bytes 73736 | tf_op jit(solution)/shard_map/ppermute | solution.py:435
  9.9 0.0 collective-permute-done.1
  9.9 0.5 %collective-permute-start.4 = (f32[4,24,128]{2,1,0:T(8,128)S(1)}, f32[4,24,128]{2,1,0:T(8,128)S(1)}, u32[]{:S(2)}, u32[]{:S(2)}) collective-permute-start(f32[4,24,128]{2,1,0:T(8,128)S(1)} %pad_maximum_fusion.refs_0_), channel_id=1, source_target_pairs={{0,1},{1,0},{2,3},{3,2},{4,5},{5,4},{6,7},{7,6},{8,9},{9,8},{10,11... | collective-permute-start | bytes 147464 | tf_op jit(solution)/shard_map/ppermute | solution.py:435
  10.4 1.6 %collective-permute-start.3 = (f32[2,24,128]{2,1,0:T(8,128)S(1)}, f32[2,24,128]{2,1,0:T(8,128)S(1)}, u32[]{:S(2)}, u32[]{:S(2)}) collective-permute-start(f32[2,24,128]{2,1,0:T(8,128)S(1)} %collective-permute-done.1), channel_id=1, source_target_pairs={{0,3},{1,2},{2,1},{3,0},{4,7},{5,6},{6,5},{7,4},{8,11},{9,10},{10,... | collective-permute-start | bytes 73736 | tf_op jit(solution)/shard_map/ppermute | solution.py:435
  12.0 0.0 collective-permute-done.2
  12.0 0.8 %shard_map.88 = (f32[9,128,128]{2,1,0:T(8,128)S(1)}, f32[11,64,128]{2,1,0:T(8,128)S(1)}) custom-call(f32[4,24,128]{2,1,0:T(8,128)S(1)} %pad_maximum_fusion.refs_0_, f32[9,128,128]{2,1,0:T(8,128)S(1)} %get-tuple-element.15.refs_1_, f32[11,64,128]{2,1,0:T(8,128)S(1)} %get-tuple-element.16.refs_2_, bf16[128,32]{1,0:T(8,128)(2,1)S(1)} %get-tuple-element.17.refs_3_, ...), custom_call_target="tpu_custom_call" | custom-call | flops 6553600 | bytes 49152 | tf_op jit(solution)/shard_map/pallas_call | solution.py:438
  12.8 0.0 collective-permute-done.4.refs_0_
  12.8 0.9 %shard_map.89 = (f32[9,128,128]{2,1,0:T(8,128)S(1)}, f32[11,64,128]{2,1,0:T(8,128)S(1)}) custom-call(f32[4,24,128]{2,1,0:T(8,128)S(1)} %collective-permute-done.4.refs_0_, f32[9,128,128]{2,1,0:T(8,128)S(1)} %get-tuple-element.15.refs_1_, f32[11,64,128]{2,1,0:T(8,128)S(1)} %get-tuple-element.16.refs_2_, bf16[128,32]{1,0:T(8,128)(2,1)S(1)} %get-tuple-element.17.refs_3_, ...), custom_call_target="tpu_custom_call" | custom-call | flops 6553600 | bytes 49152 | tf_op jit(solution)/shard_map/pallas_call | solution.py:438
  13.7 0.0 collective-permute-done.3
  13.7 0.2 %collective-permute-start.5 = (f32[4,24,128]{2,1,0:T(8,128)S(1)}, f32[4,24,128]{2,1,0:T(8,128)S(1)}, u32[]{:S(2)}, u32[]{:S(2)}) collective-permute-start(f32[4,24,128]{2,1,0:T(8,128)S(1)} %get-tuple-element.28.refs_0_), channel_id=1, source_target_pairs={{0,1},{1,0},{2,3},{3,2},{4,5},{5,4},{6,7},{7,6},{8,9},{9,8},{10,11... | collective-permute-start | bytes 147464 | tf_op jit(solution)/shard_map/ppermute | solution.py:435
  13.9 0.9 %shard_map.90 = (f32[9,128,128]{2,1,0:T(8,128)S(1)}, f32[11,64,128]{2,1,0:T(8,128)S(1)}) custom-call(f32[4,24,128]{2,1,0:T(8,128)S(1)} %get-tuple-element.28.refs_0_, f32[9,128,128]{2,1,0:T(8,128)S(1)} %get-tuple-element.15.refs_1_, f32[11,64,128]{2,1,0:T(8,128)S(1)} %get-tuple-element.16.refs_2_, bf16[128,32]{1,0:T(8,128)(2,1)S(1)} %get-tuple-element.17.refs_3_, ...), custom_call_target="tpu_custom_call" | custom-call | flops 6553600 | bytes 49152 | tf_op jit(solution)/shard_map/pallas_call | solution.py:438
  14.8 0.2 %collective-permute-done.5 = f32[4,24,128]{2,1,0:T(8,128)S(1)} collective-permute-done((f32[4,24,128]{2,1,0:T(8,128)S(1)}, f32[4,24,128]{2,1,0:T(8,128)S(1)}, u32[]{:S(2)}, u32[]{:S(2)}) %collective-permute-start.5) | collective-permute-done | bytes 49184 | tf_op jit(solution)/shard_map/ppermute | solution.py:435
  15.0 2.2 %shard_map.91 = (f32[6,128]{1,0:T(8,128)}, f32[3,64]{1,0:T(4,128)}) custom-call(f32[16,24,128]{2,1,0:T(8,128)S(1)} %constant_dynamic-update-slice_fusion.2.refs_0_, f32[9,128,128]{2,1,0:T(8,128)S(1)} %get-tuple-element.15.refs_1_, f32[11,64,128]{2,1,0:T(8,128)S(1)} %get-tuple-element.16.refs_2_, bf16[128,32]{1,0:T(8,128)(2,1)S(1)} %get-tuple-element.17.refs_3_, ...), custom_call_target="tpu_custom_call" | custom-call | flops 6553600 | bytes 49152 | tf_op jit(solution)/shard_map/pallas_call | solution.py:462
  (9 shorter events, 0.0 us)
Async XLA Ops:
  1.5 4.9 %collective-permute-start = (f32[1,24,128]{2,1,0:T(8,128)S(1)}, f32[1,24,128]{2,1,0:T(8,128)S(1)}, u32[]{:S(2)}, u32[]{:S(2)}) collective-permute-start(f32[1,24,128]{2,1,0:T(8,128)S(1)} %bitcast.2), channel_id=1, source_target_pairs={{0,9},{1,8},{2,11},{3,10},{4,13},{5,12},{6,15},{7,14},{8,1},{9,0},... | collective-permute-start | bytes 36872 | tf_op jit(solution)/shard_map/ppermute | solution.py:435
  6.5 3.4 %collective-permute-start.1 = (f32[2,24,128]{2,1,0:T(8,128)S(1)}, f32[2,24,128]{2,1,0:T(8,128)S(1)}, u32[]{:S(2)}, u32[]{:S(2)}) collective-permute-start(f32[2,24,128]{2,1,0:T(8,128)S(1)} %pad_maximum_fusion.1), channel_id=1, source_target_pairs={{0,5},{1,4},{2,7},{3,6},{4,1},{5,0},{6,3},{7,2},{8,13},{9,12},{10,... | collective-permute-start | bytes 73736 | tf_op jit(solution)/shard_map/ppermute | solution.py:435
  8.4 3.6 %collective-permute-start.2 = (f32[2,24,128]{2,1,0:T(8,128)S(1)}, f32[2,24,128]{2,1,0:T(8,128)S(1)}, u32[]{:S(2)}, u32[]{:S(2)}) collective-permute-start(f32[2,24,128]{2,1,0:T(8,128)S(1)} %pad_maximum_fusion.1), channel_id=1, source_target_pairs={{0,3},{1,2},{2,1},{3,0},{4,7},{5,6},{6,5},{7,4},{8,11},{9,10},{10,... | collective-permute-start | bytes 73736 | tf_op jit(solution)/shard_map/ppermute | solution.py:435
  9.9 2.9 %collective-permute-start.4 = (f32[4,24,128]{2,1,0:T(8,128)S(1)}, f32[4,24,128]{2,1,0:T(8,128)S(1)}, u32[]{:S(2)}, u32[]{:S(2)}) collective-permute-start(f32[4,24,128]{2,1,0:T(8,128)S(1)} %pad_maximum_fusion.refs_0_), channel_id=1, source_target_pairs={{0,1},{1,0},{2,3},{3,2},{4,5},{5,4},{6,7},{7,6},{8,9},{9,8},{10,11... | collective-permute-start | bytes 147464 | tf_op jit(solution)/shard_map/ppermute | solution.py:435
  10.4 3.3 %collective-permute-start.3 = (f32[2,24,128]{2,1,0:T(8,128)S(1)}, f32[2,24,128]{2,1,0:T(8,128)S(1)}, u32[]{:S(2)}, u32[]{:S(2)}) collective-permute-start(f32[2,24,128]{2,1,0:T(8,128)S(1)} %collective-permute-done.1), channel_id=1, source_target_pairs={{0,3},{1,2},{2,1},{3,0},{4,7},{5,6},{6,5},{7,4},{8,11},{9,10},{10,... | collective-permute-start | bytes 73736 | tf_op jit(solution)/shard_map/ppermute | solution.py:435
  13.7 1.3 %collective-permute-start.5 = (f32[4,24,128]{2,1,0:T(8,128)S(1)}, f32[4,24,128]{2,1,0:T(8,128)S(1)}, u32[]{:S(2)}, u32[]{:S(2)}) collective-permute-start(f32[4,24,128]{2,1,0:T(8,128)S(1)} %get-tuple-element.28.refs_0_), channel_id=1, source_target_pairs={{0,1},{1,0},{2,3},{3,2},{4,5},{5,4},{6,7},{7,6},{8,9},{9,8},{10,11... | collective-permute-start | bytes 147464 | tf_op jit(solution)/shard_map/ppermute | solution.py:435

commit v9 on v8

--- a/solution.py
+++ b/solution.py
@@ -452,13 +452,14 @@
     late = exchange(arrived, masks[-2])
     value = jnp.concatenate([value, arrived], 0)
     beside = exchange(value, masks[-1])
+    value = jnp.concatenate([value, beside], 0)
     sums = add_pairs(value)
-    sums = add_pairs(beside, *sums)
     late, sums = lax.optimization_barrier((late, sums))
     across = jnp.concatenate([early, late], 0)
     opposite = exchange(across, masks[-1])
     sums = add_pairs(across, *sums)
-    value = jnp.concatenate([value, across, beside, opposite], 0)
+    held = count // 4
+    value = jnp.concatenate([value[:held], across, value[held:], opposite], 0)
     return pl.pallas_call(
         functools.partial(last_kernel, count, own_seg),
         out_shape=(

time: 17.4 us -> 18.8 us (1.080)
  waiting for transfers between devices: 0.93 us -> 3.94 us
  starting transfers between devices: 9.2 us -> 7.73 us
    ppermute x6, waiting for transfers between devices: 0.93 us -> 3.94 us  [exchange(): return lax.ppermute(block, 'src', [(s, s ^ mask) for s in range(count)])]
    ppermute x6, starting transfers between devices: 9.2 us -> 7.73 us  [exchange(): return lax.ppermute(block, 'src', [(s, s ^ mask) for s in range(count)])]
    pallas_call x3 -> x2, Pallas kernels: 2.57 us -> 2.52 us  [add_pairs(): pl.pallas_call(functools.partial(early_kernel, len(sums) > 0, own_seg), o...]
  transfers between devices with their start and end apart: 6 -> 6, of which waited for: 2 -> 5; matrix products, arithmetic and copies ran while one was open for 0% -> 0% of each run, Pallas kernels for 19% -> 17%
where the time goes in v9:
time: 18.8 us; the launch traced here: 18.7 us
  starting transfers between devices  7.73 us (41%)
  Pallas kernels  6.31 us (34%)
  waiting for transfers between devices  3.94 us (21%)
  between operations  0.67 us (4%)
    ppermute x6, starting transfers between devices, exchange(): return lax.ppermute(block, 'src', [(s, s ^ mask) for s in range(count)])  7.73 us
    ppermute x6, waiting for transfers between devices, exchange(): return lax.ppermute(block, 'src', [(s, s ^ mask) for s in range(count)])  3.94 us
    pallas_call x2, Pallas kernels, add_pairs(): pl.pallas_call(functools.partial(early_kernel, len(sums) > 0, own_seg), o...  2.52 us
    pallas_call x1, Pallas kernels, on_device(): pl.pallas_call(functools.partial(last_kernel, count, own_seg), out_shape=...  2.19 us
    pallas_call x1, Pallas kernels, on_device(): pl.pallas_call(functools.partial(pack_kernel, own_seg), out_shape=pltpu.V...  0.92 us
    pallas_call x1, Pallas kernels, on_device(): pl.pallas_call(functools.partial(own_kernel, own_seg), out_shape=(*sum_sh...  0.68 us
  transfers between devices with their start and end apart: 6, of which 5 were waited for; matrix products, arithmetic and copies ran while one was open for 0% of the time, Pallas kernels for 17%

profile of v9, /device:TPU:0, one launch (start us, length us, event | category | flops | bytes accessed | tf_op | source)
XLA Modules:
  0.0 18.7 jit_solution(5193502006249352383)
XLA Ops:
  0.6 0.9 %shard_map.86 = f32[24,128]{1,0:T(8,128)S(1)} custom-call(f32[3,128]{1,0:T(4,128)} %points_ref.1, f32[3,128]{1,0:T(4,128)} %normals_ref.1, f32[8,128]{1,0:T(8,128)} %left_ref.1, f32[3,64]{1,0:T(4,128)} %vertices_ref.1, s32[2,128]{1,0:T(2,128)} %connect_ref.1, f32[8,128]{1,0:T(8,128)} %right_ref.1, f32[8]{0:T(128)} %weights_ref.1), custom_call_target="tpu_custom_call" | custom-call | tf_op jit(solution)/shard_map/pallas_call | solution.py:414
  1.5 3.5 %collective-permute-start = (f32[1,24,128]{2,1,0:T(8,128)S(1)}, f32[1,24,128]{2,1,0:T(8,128)S(1)}, u32[]{:S(2)}, u32[]{:S(2)}) collective-permute-start(f32[1,24,128]{2,1,0:T(8,128)S(1)} %bitcast.2), channel_id=1, source_target_pairs={{0,9},{1,8},{2,11},{3,10},{4,13},{5,12},{6,15},{7,14},{8,1},{9,0},... | collective-permute-start | bytes 36872 | tf_op jit(solution)/shard_map/ppermute | solution.py:435
  5.1 0.7 %shard_map.87 = (f32[9,128,128]{2,1,0:T(8,128)S(1)}, f32[11,64,128]{2,1,0:T(8,128)S(1)}, bf16[128,32]{1,0:T(8,128)(2,1)S(1)}, bf16[64,32]{1,0:T(8,128)(2,1)S(1)}) custom-call(f32[1,24,128]{2,1,0:T(8,128)S(1)} %bitcast.3), custom_call_target="tpu_custom_call" | custom-call | flops 3276800 | bytes 24576 | tf_op jit(solution)/shard_map/pallas_call | solution.py:421
  5.8 0.7 %collective-permute-done = f32[1,24,128]{2,1,0:T(8,128)S(1)} collective-permute-done((f32[1,24,128]{2,1,0:T(8,128)S(1)}, f32[1,24,128]{2,1,0:T(8,128)S(1)}, u32[]{:S(2)}, u32[]{:S(2)}) %collective-permute-start) | collective-permute-done | bytes 12320 | tf_op jit(solution)/shard_map/ppermute | solution.py:435
  6.5 1.8 %collective-permute-start.2 = (f32[2,24,128]{2,1,0:T(8,128)S(1)}, f32[2,24,128]{2,1,0:T(8,128)S(1)}, u32[]{:S(2)}, u32[]{:S(2)}) collective-permute-start(f32[2,24,128]{2,1,0:T(8,128)S(1)} %pad_maximum_fusion.2), channel_id=1, source_target_pairs={{0,3},{1,2},{2,1},{3,0},{4,7},{5,6},{6,5},{7,4},{8,11},{9,10},{10,... | collective-permute-start | bytes 73736 | tf_op jit(solution)/shard_map/ppermute | solution.py:435
  8.3 1.6 %collective-permute-start.1 = (f32[2,24,128]{2,1,0:T(8,128)S(1)}, f32[2,24,128]{2,1,0:T(8,128)S(1)}, u32[]{:S(2)}, u32[]{:S(2)}) collective-permute-start(f32[2,24,128]{2,1,0:T(8,128)S(1)} %pad_maximum_fusion.2), channel_id=1, source_target_pairs={{0,5},{1,4},{2,7},{3,6},{4,1},{5,0},{6,3},{7,2},{8,13},{9,12},{10,... | collective-permute-start | bytes 73736 | tf_op jit(solution)/shard_map/ppermute | solution.py:435
  9.9 1.6 %collective-permute-done.1 = f32[2,24,128]{2,1,0:T(8,128)S(1)} collective-permute-done((f32[2,24,128]{2,1,0:T(8,128)S(1)}, f32[2,24,128]{2,1,0:T(8,128)S(1)}, u32[]{:S(2)}, u32[]{:S(2)}) %collective-permute-start.1) | collective-permute-done | bytes 24608 | tf_op jit(solution)/shard_map/ppermute | solution.py:435
  11.6 0.4 %collective-permute-start.4 = (f32[4,24,128]{2,1,0:T(8,128)S(1)}, f32[4,24,128]{2,1,0:T(8,128)S(1)}, u32[]{:S(2)}, u32[]{:S(2)}) collective-permute-start(f32[4,24,128]{2,1,0:T(8,128)S(1)} %pad_maximum_fusion.1), channel_id=1, source_target_pairs={{0,1},{1,0},{2,3},{3,2},{4,5},{5,4},{6,7},{7,6},{8,9},{9,8},{10,11... | collective-permute-start | bytes 147464 | tf_op jit(solution)/shard_map/ppermute | solution.py:435
  12.0 0.2 %collective-permute-start.3 = (f32[2,24,128]{2,1,0:T(8,128)S(1)}, f32[2,24,128]{2,1,0:T(8,128)S(1)}, u32[]{:S(2)}, u32[]{:S(2)}) collective-permute-start(f32[2,24,128]{2,1,0:T(8,128)S(1)} %collective-permute-done.1), channel_id=1, source_target_pairs={{0,3},{1,2},{2,1},{3,0},{4,7},{5,6},{6,5},{7,4},{8,11},{9,10},{10,... | collective-permute-start | bytes 73736 | tf_op jit(solution)/shard_map/ppermute | solution.py:435
  12.2 0.0 collective-permute-done.2
  12.2 0.6 %collective-permute-done.4 = f32[4,24,128]{2,1,0:T(8,128)S(1)} collective-permute-done((f32[4,24,128]{2,1,0:T(8,128)S(1)}, f32[4,24,128]{2,1,0:T(8,128)S(1)}, u32[]{:S(2)}, u32[]{:S(2)}) %collective-permute-start.4) | collective-permute-done | bytes 49184 | tf_op jit(solution)/shard_map/ppermute | solution.py:435
  12.9 1.6 %shard_map.88 = (f32[9,128,128]{2,1,0:T(8,128)S(1)}, f32[11,64,128]{2,1,0:T(8,128)S(1)}) custom-call(f32[8,24,128]{2,1,0:T(8,128)S(1)} %pad_maximum_fusion.refs_0_, f32[9,128,128]{2,1,0:T(8,128)S(1)} %get-tuple-element.13.refs_1_, f32[11,64,128]{2,1,0:T(8,128)S(1)} %get-tuple-element.14.refs_2_, bf16[128,32]{1,0:T(8,128)(2,1)S(1)} %get-tuple-element.15.refs_3_, ...), custom_call_target="tpu_custom_call" | custom-call | flops 13107200 | bytes 98304 | tf_op jit(solution)/shard_map/pallas_call | solution.py:438
  14.5 0.7 %collective-permute-done.3 = f32[2,24,128]{2,1,0:T(8,128)S(1)} collective-permute-done((f32[2,24,128]{2,1,0:T(8,128)S(1)}, f32[2,24,128]{2,1,0:T(8,128)S(1)}, u32[]{:S(2)}, u32[]{:S(2)}) %collective-permute-start.3) | collective-permute-done | bytes 24608 | tf_op jit(solution)/shard_map/ppermute | solution.py:435
  15.3 0.1 collective-permute-start.5
  15.4 0.9 %shard_map.89 = (f32[9,128,128]{2,1,0:T(8,128)S(1)}, f32[11,64,128]{2,1,0:T(8,128)S(1)}) custom-call(f32[4,24,128]{2,1,0:T(8,128)S(1)} %get-tuple-element.24.refs_0_, f32[9,128,128]{2,1,0:T(8,128)S(1)} %get-tuple-element.13.refs_1_, f32[11,64,128]{2,1,0:T(8,128)S(1)} %get-tuple-element.14.refs_2_, bf16[128,32]{1,0:T(8,128)(2,1)S(1)} %get-tuple-element.15.refs_3_, ...), custom_call_target="tpu_custom_call" | custom-call | flops 6553600 | bytes 49152 | tf_op jit(solution)/shard_map/pallas_call | solution.py:438
  16.3 0.2 %collective-permute-done.5 = f32[4,24,128]{2,1,0:T(8,128)S(1)} collective-permute-done((f32[4,24,128]{2,1,0:T(8,128)S(1)}, f32[4,24,128]{2,1,0:T(8,128)S(1)}, u32[]{:S(2)}, u32[]{:S(2)}) %collective-permute-start.5) | collective-permute-done | bytes 49184 | tf_op jit(solution)/shard_map/ppermute | solution.py:435
  16.5 2.2 %shard_map.90 = (f32[6,128]{1,0:T(8,128)}, f32[3,64]{1,0:T(4,128)}) custom-call(f32[16,24,128]{2,1,0:T(8,128)S(1)} %constant_dynamic-update-slice_fusion.2.refs_0_, f32[9,128,128]{2,1,0:T(8,128)S(1)} %get-tuple-element.13.refs_1_, f32[11,64,128]{2,1,0:T(8,128)S(1)} %get-tuple-element.14.refs_2_, bf16[128,32]{1,0:T(8,128)(2,1)S(1)} %get-tuple-element.15.refs_3_, ...), custom_call_target="tpu_custom_call" | custom-call | flops 6553600 | bytes 49152 | tf_op jit(solution)/shard_map/pallas_call | solution.py:463
  (10 shorter events, 0.0 us)
Async XLA Ops:
  1.5 4.9 %collective-permute-start = (f32[1,24,128]{2,1,0:T(8,128)S(1)}, f32[1,24,128]{2,1,0:T(8,128)S(1)}, u32[]{:S(2)}, u32[]{:S(2)}) collective-permute-start(f32[1,24,128]{2,1,0:T(8,128)S(1)} %bitcast.2), channel_id=1, source_target_pairs={{0,9},{1,8},{2,11},{3,10},{4,13},{5,12},{6,15},{7,14},{8,1},{9,0},... | collective-permute-start | bytes 36872 | tf_op jit(solution)/shard_map/ppermute | solution.py:435
  6.5 5.7 %collective-permute-start.2 = (f32[2,24,128]{2,1,0:T(8,128)S(1)}, f32[2,24,128]{2,1,0:T(8,128)S(1)}, u32[]{:S(2)}, u32[]{:S(2)}) collective-permute-start(f32[2,24,128]{2,1,0:T(8,128)S(1)} %pad_maximum_fusion.2), channel_id=1, source_target_pairs={{0,3},{1,2},{2,1},{3,0},{4,7},{5,6},{6,5},{7,4},{8,11},{9,10},{10,... | collective-permute-start | bytes 73736 | tf_op jit(solution)/shard_map/ppermute | solution.py:435
  8.3 3.3 %collective-permute-start.1 = (f32[2,24,128]{2,1,0:T(8,128)S(1)}, f32[2,24,128]{2,1,0:T(8,128)S(1)}, u32[]{:S(2)}, u32[]{:S(2)}) collective-permute-start(f32[2,24,128]{2,1,0:T(8,128)S(1)} %pad_maximum_fusion.2), channel_id=1, source_target_pairs={{0,5},{1,4},{2,7},{3,6},{4,1},{5,0},{6,3},{7,2},{8,13},{9,12},{10,... | collective-permute-start | bytes 73736 | tf_op jit(solution)/shard_map/ppermute | solution.py:435
  11.6 1.3 %collective-permute-start.4 = (f32[4,24,128]{2,1,0:T(8,128)S(1)}, f32[4,24,128]{2,1,0:T(8,128)S(1)}, u32[]{:S(2)}, u32[]{:S(2)}) collective-permute-start(f32[4,24,128]{2,1,0:T(8,128)S(1)} %pad_maximum_fusion.1), channel_id=1, source_target_pairs={{0,1},{1,0},{2,3},{3,2},{4,5},{5,4},{6,7},{7,6},{8,9},{9,8},{10,11... | collective-permute-start | bytes 147464 | tf_op jit(solution)/shard_map/ppermute | solution.py:435
  12.0 3.3 %collective-permute-start.3 = (f32[2,24,128]{2,1,0:T(8,128)S(1)}, f32[2,24,128]{2,1,0:T(8,128)S(1)}, u32[]{:S(2)}, u32[]{:S(2)}) collective-permute-start(f32[2,24,128]{2,1,0:T(8,128)S(1)} %collective-permute-done.1), channel_id=1, source_target_pairs={{0,3},{1,2},{2,1},{3,0},{4,7},{5,6},{6,5},{7,4},{8,11},{9,10},{10,... | collective-permute-start | bytes 73736 | tf_op jit(solution)/shard_map/ppermute | solution.py:435
  15.3 1.2 %collective-permute-start.5 = (f32[4,24,128]{2,1,0:T(8,128)S(1)}, f32[4,24,128]{2,1,0:T(8,128)S(1)}, u32[]{:S(2)}, u32[]{:S(2)}) collective-permute-start(f32[4,24,128]{2,1,0:T(8,128)S(1)} %get-tuple-element.24.refs_0_), channel_id=1, source_target_pairs={{0,1},{1,0},{2,3},{3,2},{4,5},{5,4},{6,7},{7,6},{8,9},{9,8},{10,11... | collective-permute-start | bytes 147464 | tf_op jit(solution)/shard_map/ppermute | solution.py:435

commit v10 on v8

--- a/solution.py
+++ b/solution.py
@@ -58,11 +58,14 @@
     return (a[1] * b[2] - a[2] * b[1], a[2] * b[0] - a[0] * b[2], a[0] * b[1] - a[1] * b[0])
 
 
-def pair_terms(point, normal, moment, first, segment, turn, span, span_core, scale, want_span):
-    rel = tuple(p - e for p, e in zip(point, first))
-    cross_n = (moment[0] * segment[0] + moment[1] * segment[1] + moment[2] * segment[2]) - (
+def normal_cross(normal, moment, segment, turn):
+    return (moment[0] * segment[0] + moment[1] * segment[1] + moment[2] * segment[2]) - (
         normal[0] * turn[0] + normal[1] * turn[1] + normal[2] * turn[2]
     )
+
+
+def pair_terms(point, cross_n, first, segment, span, span_core, scale, want_span):
+    rel = tuple(p - e for p, e in zip(point, first))
     dist_sq = rel[0] * rel[0] + rel[1] * rel[1] + rel[2] * rel[2]
     along = segment[0] * rel[0] + segment[1] * rel[1] + segment[2] * rel[2]
     other = along - span
@@ -134,7 +137,7 @@
     return (lane == own_seg - 1) | (lane == 2 * own_seg - 1)
 
 
-def own_kernel(own_seg, data_ref, col1_ref, col2_ref, left_ref, right_ref):
+def own_kernel(own_seg, data_ref, col1_ref, col2_ref, left_ref, right_ref, moment_ref, turn_ref):
     def columns(rows, out_ref):
         pad = jnp.zeros((16 - len(rows), LANES), jnp.float32)
         cols = jnp.transpose(jnp.concatenate(list(rows) + [pad], 0))
@@ -144,16 +147,19 @@
 
     own_block = data_ref[0, 16:24, :]
     point, normal, moment = own_receivers(data_ref)
-    columns([*point, *normal, *moment], col1_ref)
+    columns([*point, *normal], col1_ref)
     own_e, own_s, own_t, span, span_core = own_segments(own_block, own_seg)
-    columns([*own_e, *own_s, *own_t, span, span_core], col2_ref)
+    columns([*own_e, *own_s, span, span_core], col2_ref)
     left_ref[...] = stack_hhll(data_ref[0, 0:8, :])
     right_ref[...] = stack_hhll(jnp.where(lane_edges(own_seg), 0.0, own_block))[0:own_seg]
+    pad = jnp.zeros((2, LANES), jnp.float32)
+    moment_ref[...] = stack_hhll(jnp.concatenate([*moment, *normal, pad], 0))
+    turn_ref[...] = stack_hhll(jnp.concatenate([*own_s, *(-value for value in own_t), pad], 0))[0:own_seg]
 
 
 def pair_sums(data_ref, own_refs, begin, end, own_seg, scratch, old1, old2, new1, new2, between=None):
-    seg_ref, rec_ref, scale1_ref, scale2_ref = scratch
-    col1_ref, col2_ref, left_ref, right_ref = own_refs
+    seg_ref, rec_ref, scale1_ref, scale2_ref, row1_ref, row2_ref, cross1_ref, cross2_ref = scratch
+    col1_ref, col2_ref, left_ref, right_ref, moment_ref, turn_ref = own_refs
     blocks = end - begin
     tiles = blocks // 2
     lane = lax.broadcasted_iota(jnp.int32, (1, LANES), 1)
@@ -186,6 +192,20 @@
         rec_ref[3 + axis] = normal[axis]
         rec_ref[6 + axis] = moment[axis]
 
+    for ref in (row1_ref, row2_ref):
+        ref[6:8, :] = jnp.zeros((2, ref.shape[1]), jnp.float32)
+    for axis in range(3):
+        for tile in range(tiles):
+            at = slice(tile * LANES, (tile + 1) * LANES)
+            row1_ref[axis : axis + 1, at] = segment[axis][tile : tile + 1]
+            row1_ref[3 + axis : 4 + axis, at] = -turn[axis][tile : tile + 1]
+        for block in range(blocks):
+            at = slice(block * LANES, (block + 1) * LANES)
+            row2_ref[axis : axis + 1, at] = moment[axis][block : block + 1]
+            row2_ref[3 + axis : 4 + axis, at] = normal[axis][block : block + 1]
+    cross1_ref[...] = jnp.dot(moment_ref[...], stack_hlhl(row1_ref[...]), preferred_element_type=jnp.float32)
+    cross2_ref[...] = jnp.dot(turn_ref[...], stack_hlhl(row2_ref[...]), preferred_element_type=jnp.float32)
+
     scale1_ref[...] = jnp.dot(
         left_ref[...], stack_hlhl(jnp.concatenate(folded, 1)), preferred_element_type=jnp.float32)
     scale2_ref[...] = jnp.dot(
@@ -198,13 +218,14 @@
         return [old[k, start : start + CHUNK, :] for k in range(count)]
 
     for start in range(0, LANES, CHUNK):
-        col = [col1_ref[k, start : start + CHUNK, :] for k in range(9)]
+        col = [col1_ref[k, start : start + CHUNK, :] for k in range(3)]
         sums = initial(old1, 9, start)
         for tile in range(tiles):
             row = [seg_ref[k, tile : tile + 1, :] for k in range(11)]
             scale = scale1_ref[start : start + CHUNK, tile * LANES : (tile + 1) * LANES]
             rel, by_normal, by_dist2, by_along = pair_terms(
-                col[0:3], col[3:6], col[6:9], row[0:3], row[3:6], row[6:9], row[9], row[10], scale, False)
+                col, cross1_ref[start : start + CHUNK, tile * LANES : (tile + 1) * LANES],
+                row[0:3], row[3:6], row[9], row[10], scale, False)
             for axis in range(3):
                 sums[axis] += by_normal * row[3 + axis]
                 sums[3 + axis] += by_normal * row[6 + axis]
@@ -216,13 +237,14 @@
         between()
 
     for start in range(0, own_seg, CHUNK):
-        col = [col2_ref[k, start : start + CHUNK, :] for k in range(11)]
+        col = [col2_ref[k, start : start + CHUNK, :] for k in range(8)]
         sums = initial(old2, 11, start)
         for block in range(blocks):
             row = [rec_ref[k, block : block + 1, :] for k in range(9)]
             scale = scale2_ref[start : start + CHUNK, block * LANES : (block + 1) * LANES]
             rel, by_normal, by_dist2, by_along, by_span2 = pair_terms(
-                row[0:3], row[3:6], row[6:9], col[0:3], col[3:6], col[6:9], col[9], col[10], scale, True)
+                row[0:3], cross2_ref[start : start + CHUNK, block * LANES : (block + 1) * LANES],
+                col[0:3], col[3:6], col[6], col[7], scale, True)
             for axis in range(3):
                 sums[axis] += by_normal * row[3 + axis]
                 sums[3 + axis] += by_normal * row[6 + axis] + by_along * rel[axis]
@@ -285,7 +307,7 @@
 
 
 def early_kernel(chained, own_seg, *refs):
-    data_ref, own_refs, rest = refs[0], refs[1:5], refs[5:]
+    data_ref, own_refs, rest = refs[0], refs[1:7], refs[7:]
     olds = rest[0:2] if chained else (None, None)
     rest = rest[2:] if chained else rest
     pair_sums(data_ref, own_refs, 0, data_ref.shape[0], own_seg, rest[2:], *olds, rest[0], rest[1])
@@ -293,8 +315,8 @@
 
 def last_kernel(count, own_seg, *refs):
     data_ref, own_refs, old1_ref, old2_ref, rcv_out, vert_out, after_ref, new1_ref, new2_ref = (
-        refs[0], refs[1:5], *refs[5:12])
-    scratch = refs[12:]
+        refs[0], refs[1:7], *refs[7:14])
+    scratch = refs[14:]
     masks = exchange_masks(count)
     me = lax.axis_index("src")
     lane = lax.broadcasted_iota(jnp.int32, (1, LANES), 1)
@@ -346,8 +368,8 @@
         segment, turn, span, span_core = segment_terms(first, second)
         normals = stacked(own_n, normal)
         rel, by_normal, by_dist2, by_along, by_span2 = pair_terms(
-            stacked(own_p, point), normals, stacked(own_m, moment),
-            first, segment, turn, span, span_core, jnp.concatenate(scales, 0), True)
+            stacked(own_p, point), normal_cross(normals, stacked(own_m, moment), segment, turn),
+            first, segment, span, span_core, jnp.concatenate(scales, 0), True)
 
         def down(value):
             return jnp.sum(value, axis=0, keepdims=True)
@@ -392,6 +414,10 @@
         pltpu.VMEM((9, blocks, LANES), jnp.float32),
         pltpu.VMEM((LANES, blocks // 2 * LANES), jnp.float32),
         pltpu.VMEM((own_seg, blocks * LANES), jnp.float32),
+        pltpu.VMEM((8, blocks // 2 * LANES), jnp.float32),
+        pltpu.VMEM((8, blocks * LANES), jnp.float32),
+        pltpu.VMEM((LANES, blocks // 2 * LANES), jnp.float32),
+        pltpu.VMEM((own_seg, blocks * LANES), jnp.float32),
     ]
 
 
@@ -421,12 +447,15 @@
     own = pl.pallas_call(
         functools.partial(own_kernel, own_seg),
         out_shape=(
-            *sum_shapes(own_seg),
+            pltpu.VMEM((6, LANES, LANES), jnp.float32),
+            pltpu.VMEM((8, own_seg, LANES), jnp.float32),
+            pltpu.VMEM((LANES, 32), jnp.bfloat16),
+            pltpu.VMEM((own_seg, 32), jnp.bfloat16),
             pltpu.VMEM((LANES, 32), jnp.bfloat16),
             pltpu.VMEM((own_seg, 32), jnp.bfloat16),
         ),
         in_specs=[VMEM],
-        out_specs=(VMEM,) * 4,
+        out_specs=(VMEM,) * 6,
         cost_estimate=pair_cost(2, own_seg),
         compiler_params=params,
     )(value)
@@ -438,7 +467,7 @@
         return pl.pallas_call(
             functools.partial(early_kernel, len(sums) > 0, own_seg),
             out_shape=tuple(sum_shapes(own_seg)),
-            in_specs=[VMEM] * (5 + len(sums)),
+            in_specs=[VMEM] * (7 + len(sums)),
             out_specs=(VMEM, VMEM),
             scratch_shapes=pair_scratch(block.shape[0], own_seg),
             cost_estimate=pair_cost(block.shape[0], own_seg),
@@ -465,7 +494,7 @@
             jax.ShapeDtypeStruct((6, LANES), jnp.float32),
             jax.ShapeDtypeStruct((3, own_seg), jnp.float32),
         ),
-        in_specs=[VMEM] * 7,
+        in_specs=[VMEM] * 9,
         out_specs=(VMEM, VMEM),
         scratch_shapes=last_scratch(count, own_seg),
         cost_estimate=pair_cost(count // 4, own_seg),

time: 17.4 us -> 17.2 us (0.989)
  Pallas kernels: 6.36 us -> 6.1 us
  transfers between devices with their start and end apart: 6 -> 6, of which waited for: 2 -> 2; matrix products, arithmetic and copies ran while one was open for 0% -> 0% of each run, Pallas kernels for 19% -> 18%
where the time goes in v10:
time: 17.2 us; the launch traced here: 17 us
  starting transfers between devices  9.2 us (53%)
  Pallas kernels  6.1 us (35%)
  waiting for transfers between devices  1.03 us (6%)
  between operations  0.68 us (4%)
    ppermute x6, starting transfers between devices, exchange(): return lax.ppermute(block, 'src', [(s, s ^ mask) for s in range(count)])  9.2 us
    pallas_call x3, Pallas kernels, add_pairs(): pl.pallas_call(functools.partial(early_kernel, len(sums) > 0, own_seg), o...  2.44 us
    pallas_call x1, Pallas kernels, on_device(): pl.pallas_call(functools.partial(last_kernel, count, own_seg), out_shape=...  2.1 us
    ppermute x6, waiting for transfers between devices, exchange(): return lax.ppermute(block, 'src', [(s, s ^ mask) for s in range(count)])  1.03 us
    pallas_call x1, Pallas kernels, on_device(): pl.pallas_call(functools.partial(pack_kernel, own_seg), out_shape=pltpu.V...  0.92 us
    pallas_call x1, Pallas kernels, on_device(): pl.pallas_call(functools.partial(own_kernel, own_seg), out_shape=(pltpu.V...  0.64 us
  transfers between devices with their start and end apart: 6, of which 2 were waited for; matrix products, arithmetic and copies ran while one was open for 0% of the time, Pallas kernels for 18%

profile of v10, /device:TPU:0, one launch (start us, length us, event | category | flops | bytes accessed | tf_op | source)
XLA Modules:
  0.0 17.0 jit_solution(16273221234186209726)
XLA Ops:
  0.6 0.9 %shard_map.86 = f32[24,128]{1,0:T(8,128)S(1)} custom-call(f32[3,128]{1,0:T(4,128)} %points_ref.1, f32[3,128]{1,0:T(4,128)} %normals_ref.1, f32[8,128]{1,0:T(8,128)} %left_ref.1, f32[3,64]{1,0:T(4,128)} %vertices_ref.1, s32[2,128]{1,0:T(2,128)} %connect_ref.1, f32[8,128]{1,0:T(8,128)} %right_ref.1, f32[8]{0:T(128)} %weights_ref.1), custom_call_target="tpu_custom_call" | custom-call | tf_op jit(solution)/shard_map/pallas_call | solution.py:440
  1.5 3.5 %collective-permute-start = (f32[1,24,128]{2,1,0:T(8,128)S(1)}, f32[1,24,128]{2,1,0:T(8,128)S(1)}, u32[]{:S(2)}, u32[]{:S(2)}) collective-permute-start(f32[1,24,128]{2,1,0:T(8,128)S(1)} %bitcast.2), channel_id=1, source_target_pairs={{0,9},{1,8},{2,11},{3,10},{4,13},{5,12},{6,15},{7,14},{8,1},{9,0},... | collective-permute-start | bytes 36872 | tf_op jit(solution)/shard_map/ppermute | solution.py:464
  5.1 0.6 %shard_map.87 = (f32[6,128,128]{2,1,0:T(8,128)S(1)}, f32[8,64,128]{2,1,0:T(8,128)S(1)}, bf16[128,32]{1,0:T(8,128)(2,1)S(1)}, bf16[64,32]{1,0:T(8,128)(2,1)S(1)},...) custom-call(f32[1,24,128]{2,1,0:T(8,128)S(1)} %bitcast.3), custom_call_target="tpu_custom_call" | custom-call | flops 3276800 | bytes 24576 | tf_op jit(solution)/shard_map/pallas_call | solution.py:447
  5.7 0.8 %collective-permute-done = f32[1,24,128]{2,1,0:T(8,128)S(1)} collective-permute-done((f32[1,24,128]{2,1,0:T(8,128)S(1)}, f32[1,24,128]{2,1,0:T(8,128)S(1)}, u32[]{:S(2)}, u32[]{:S(2)}) %collective-permute-start) | collective-permute-done | bytes 12320 | tf_op jit(solution)/shard_map/ppermute | solution.py:464
  6.5 1.9 %collective-permute-start.1 = (f32[2,24,128]{2,1,0:T(8,128)S(1)}, f32[2,24,128]{2,1,0:T(8,128)S(1)}, u32[]{:S(2)}, u32[]{:S(2)}) collective-permute-start(f32[2,24,128]{2,1,0:T(8,128)S(1)} %pad_maximum_fusion.1), channel_id=1, source_target_pairs={{0,5},{1,4},{2,7},{3,6},{4,1},{5,0},{6,3},{7,2},{8,13},{9,12},{10,... | collective-permute-start | bytes 73736 | tf_op jit(solution)/shard_map/ppermute | solution.py:464
  8.4 1.6 %collective-permute-start.2 = (f32[2,24,128]{2,1,0:T(8,128)S(1)}, f32[2,24,128]{2,1,0:T(8,128)S(1)}, u32[]{:S(2)}, u32[]{:S(2)}) collective-permute-start(f32[2,24,128]{2,1,0:T(8,128)S(1)} %pad_maximum_fusion.1), channel_id=1, source_target_pairs={{0,3},{1,2},{2,1},{3,0},{4,7},{5,6},{6,5},{7,4},{8,11},{9,10},{10,... | collective-permute-start | bytes 73736 | tf_op jit(solution)/shard_map/ppermute | solution.py:464
  9.9 0.0 collective-permute-done.1
  9.9 0.5 %collective-permute-start.4 = (f32[4,24,128]{2,1,0:T(8,128)S(1)}, f32[4,24,128]{2,1,0:T(8,128)S(1)}, u32[]{:S(2)}, u32[]{:S(2)}) collective-permute-start(f32[4,24,128]{2,1,0:T(8,128)S(1)} %pad_maximum_fusion.refs_0_), channel_id=1, source_target_pairs={{0,1},{1,0},{2,3},{3,2},{4,5},{5,4},{6,7},{7,6},{8,9},{9,8},{10,11... | collective-permute-start | bytes 147464 | tf_op jit(solution)/shard_map/ppermute | solution.py:464
  10.4 1.6 %collective-permute-start.3 = (f32[2,24,128]{2,1,0:T(8,128)S(1)}, f32[2,24,128]{2,1,0:T(8,128)S(1)}, u32[]{:S(2)}, u32[]{:S(2)}) collective-permute-start(f32[2,24,128]{2,1,0:T(8,128)S(1)} %collective-permute-done.1), channel_id=1, source_target_pairs={{0,3},{1,2},{2,1},{3,0},{4,7},{5,6},{6,5},{7,4},{8,11},{9,10},{10,... | collective-permute-start | bytes 73736 | tf_op jit(solution)/shard_map/ppermute | solution.py:464
  12.0 0.0 collective-permute-done.2
  12.0 0.8 %shard_map.88 = (f32[9,128,128]{2,1,0:T(8,128)S(1)}, f32[11,64,128]{2,1,0:T(8,128)S(1)}) custom-call(f32[4,24,128]{2,1,0:T(8,128)S(1)} %pad_maximum_fusion.refs_0_, f32[6,128,128]{2,1,0:T(8,128)S(1)} %get-tuple-element.17.refs_1_, f32[8,64,128]{2,1,0:T(8,128)S(1)} %get-tuple-element.18.refs_2_, bf16[128,32]{1,0:T(8,128)(2,1)S(1)} %get-tuple-element.19.refs_3_, ...), custom_call_target="tpu_custom_call" | custom-call | flops 6553600 | bytes 49152 | tf_op jit(solution)/shard_map/pallas_call | solution.py:467
  12.8 0.0 collective-permute-done.4.refs_0_
  12.8 0.8 %shard_map.89 = (f32[9,128,128]{2,1,0:T(8,128)S(1)}, f32[11,64,128]{2,1,0:T(8,128)S(1)}) custom-call(f32[4,24,128]{2,1,0:T(8,128)S(1)} %collective-permute-done.4.refs_0_, f32[6,128,128]{2,1,0:T(8,128)S(1)} %get-tuple-element.17.refs_1_, f32[8,64,128]{2,1,0:T(8,128)S(1)} %get-tuple-element.18.refs_2_, bf16[128,32]{1,0:T(8,128)(2,1)S(1)} %get-tuple-element.19.refs_3_, ...), custom_call_target="tpu_custom_call" | custom-call | flops 6553600 | bytes 49152 | tf_op jit(solution)/shard_map/pallas_call | solution.py:467
  13.6 0.0 collective-permute-done.3
  13.6 0.2 %collective-permute-start.5 = (f32[4,24,128]{2,1,0:T(8,128)S(1)}, f32[4,24,128]{2,1,0:T(8,128)S(1)}, u32[]{:S(2)}, u32[]{:S(2)}) collective-permute-start(f32[4,24,128]{2,1,0:T(8,128)S(1)} %get-tuple-element.32.refs_0_), channel_id=1, source_target_pairs={{0,1},{1,0},{2,3},{3,2},{4,5},{5,4},{6,7},{7,6},{8,9},{9,8},{10,11... | collective-permute-start | bytes 147464 | tf_op jit(solution)/shard_map/ppermute | solution.py:464
  13.9 0.8 %shard_map.90 = (f32[9,128,128]{2,1,0:T(8,128)S(1)}, f32[11,64,128]{2,1,0:T(8,128)S(1)}) custom-call(f32[4,24,128]{2,1,0:T(8,128)S(1)} %get-tuple-element.32.refs_0_, f32[6,128,128]{2,1,0:T(8,128)S(1)} %get-tuple-element.17.refs_1_, f32[8,64,128]{2,1,0:T(8,128)S(1)} %get-tuple-element.18.refs_2_, bf16[128,32]{1,0:T(8,128)(2,1)S(1)} %get-tuple-element.19.refs_3_, ...), custom_call_target="tpu_custom_call" | custom-call | flops 6553600 | bytes 49152 | tf_op jit(solution)/shard_map/pallas_call | solution.py:467
  14.7 0.2 %collective-permute-done.5 = f32[4,24,128]{2,1,0:T(8,128)S(1)} collective-permute-done((f32[4,24,128]{2,1,0:T(8,128)S(1)}, f32[4,24,128]{2,1,0:T(8,128)S(1)}, u32[]{:S(2)}, u32[]{:S(2)}) %collective-permute-start.5) | collective-permute-done | bytes 49184 | tf_op jit(solution)/shard_map/ppermute | solution.py:464
  14.9 2.1 %shard_map.91 = (f32[6,128]{1,0:T(8,128)}, f32[3,64]{1,0:T(4,128)}) custom-call(f32[16,24,128]{2,1,0:T(8,128)S(1)} %constant_dynamic-update-slice_fusion.2.refs_0_, f32[6,128,128]{2,1,0:T(8,128)S(1)} %get-tuple-element.17.refs_1_, f32[8,64,128]{2,1,0:T(8,128)S(1)} %get-tuple-element.18.refs_2_, bf16[128,32]{1,0:T(8,128)(2,1)S(1)} %get-tuple-element.19.refs_3_, ...), custom_call_target="tpu_custom_call" | custom-call | flops 6553600 | bytes 49152 | tf_op jit(solution)/shard_map/pallas_call | solution.py:491
  (9 shorter events, 0.0 us)
Async XLA Ops:
  1.5 4.9 %collective-permute-start = (f32[1,24,128]{2,1,0:T(8,128)S(1)}, f32[1,24,128]{2,1,0:T(8,128)S(1)}, u32[]{:S(2)}, u32[]{:S(2)}) collective-permute-start(f32[1,24,128]{2,1,0:T(8,128)S(1)} %bitcast.2), channel_id=1, source_target_pairs={{0,9},{1,8},{2,11},{3,10},{4,13},{5,12},{6,15},{7,14},{8,1},{9,0},... | collective-permute-start | bytes 36872 | tf_op jit(solution)/shard_map/ppermute | solution.py:464
  6.5 3.4 %collective-permute-start.1 = (f32[2,24,128]{2,1,0:T(8,128)S(1)}, f32[2,24,128]{2,1,0:T(8,128)S(1)}, u32[]{:S(2)}, u32[]{:S(2)}) collective-permute-start(f32[2,24,128]{2,1,0:T(8,128)S(1)} %pad_maximum_fusion.1), channel_id=1, source_target_pairs={{0,5},{1,4},{2,7},{3,6},{4,1},{5,0},{6,3},{7,2},{8,13},{9,12},{10,... | collective-permute-start | bytes 73736 | tf_op jit(solution)/shard_map/ppermute | solution.py:464
  8.4 3.6 %collective-permute-start.2 = (f32[2,24,128]{2,1,0:T(8,128)S(1)}, f32[2,24,128]{2,1,0:T(8,128)S(1)}, u32[]{:S(2)}, u32[]{:S(2)}) collective-permute-start(f32[2,24,128]{2,1,0:T(8,128)S(1)} %pad_maximum_fusion.1), channel_id=1, source_target_pairs={{0,3},{1,2},{2,1},{3,0},{4,7},{5,6},{6,5},{7,4},{8,11},{9,10},{10,... | collective-permute-start | bytes 73736 | tf_op jit(solution)/shard_map/ppermute | solution.py:464
  9.9 2.8 %collective-permute-start.4 = (f32[4,24,128]{2,1,0:T(8,128)S(1)}, f32[4,24,128]{2,1,0:T(8,128)S(1)}, u32[]{:S(2)}, u32[]{:S(2)}) collective-permute-start(f32[4,24,128]{2,1,0:T(8,128)S(1)} %pad_maximum_fusion.refs_0_), channel_id=1, source_target_pairs={{0,1},{1,0},{2,3},{3,2},{4,5},{5,4},{6,7},{7,6},{8,9},{9,8},{10,11... | collective-permute-start | bytes 147464 | tf_op jit(solution)/shard_map/ppermute | solution.py:464
  10.4 3.3 %collective-permute-start.3 = (f32[2,24,128]{2,1,0:T(8,128)S(1)}, f32[2,24,128]{2,1,0:T(8,128)S(1)}, u32[]{:S(2)}, u32[]{:S(2)}) collective-permute-start(f32[2,24,128]{2,1,0:T(8,128)S(1)} %collective-permute-done.1), channel_id=1, source_target_pairs={{0,3},{1,2},{2,1},{3,0},{4,7},{5,6},{6,5},{7,4},{8,11},{9,10},{10,... | collective-permute-start | bytes 73736 | tf_op jit(solution)/shard_map/ppermute | solution.py:464
  13.6 1.3 %collective-permute-start.5 = (f32[4,24,128]{2,1,0:T(8,128)S(1)}, f32[4,24,128]{2,1,0:T(8,128)S(1)}, u32[]{:S(2)}, u32[]{:S(2)}) collective-permute-start(f32[4,24,128]{2,1,0:T(8,128)S(1)} %get-tuple-element.32.refs_0_), channel_id=1, source_target_pairs={{0,1},{1,0},{2,3},{3,2},{4,5},{5,4},{6,7},{7,6},{8,9},{9,8},{10,11... | collective-permute-start | bytes 147464 | tf_op jit(solution)/shard_map/ppermute | solution.py:464

commit v11 on v10

--- a/solution.py
+++ b/solution.py
@@ -392,7 +392,7 @@
 
     found = []
     pair_sums(
-        data_ref, own_refs, count - count // 4, count, own_seg, scratch, old1_ref, old2_ref, new1_ref, new2_ref,
+        data_ref, own_refs, count - count // 8, count, own_seg, scratch, old1_ref, old2_ref, new1_ref, new2_ref,
         lambda: found.extend((*edge_sums(), receiver_totals(new1_ref, own_refs[0]))))
     edge_point, edge_normal, arriving, leaving, totals = found
     for axis in range(3):
@@ -426,7 +426,7 @@
 
 
 def last_scratch(count, own_seg):
-    return [pltpu.VMEM((count, 8, LANES), jnp.float32)] + sum_shapes(own_seg) + pair_scratch(count // 4, own_seg)
+    return [pltpu.VMEM((count, 8, LANES), jnp.float32)] + sum_shapes(own_seg) + pair_scratch(count // 8, own_seg)
 
 
 def pair_cost(blocks, own_seg):
@@ -480,14 +480,13 @@
     arrived, early = exchange(value, masks[-3]), exchange(value, masks[-2])
     late = exchange(arrived, masks[-2])
     value = jnp.concatenate([value, arrived], 0)
-    beside = exchange(value, masks[-1])
+    beside, beside_early = exchange(value, masks[-1]), exchange(early, masks[-1])
     sums = add_pairs(value)
     sums = add_pairs(beside, *sums)
     late, sums = lax.optimization_barrier((late, sums))
-    across = jnp.concatenate([early, late], 0)
-    opposite = exchange(across, masks[-1])
-    sums = add_pairs(across, *sums)
-    value = jnp.concatenate([value, across, beside, opposite], 0)
+    beside_late = exchange(late, masks[-1])
+    sums = add_pairs(jnp.concatenate([early, late, beside_early], 0), *sums)
+    value = jnp.concatenate([value, early, late, beside, beside_early, beside_late], 0)
     return pl.pallas_call(
         functools.partial(last_kernel, count, own_seg),
         out_shape=(
@@ -497,7 +496,7 @@
         in_specs=[VMEM] * 9,
         out_specs=(VMEM, VMEM),
         scratch_shapes=last_scratch(count, own_seg),
-        cost_estimate=pair_cost(count // 4, own_seg),
+        cost_estimate=pair_cost(count // 8, own_seg),
         compiler_params=params,
     )(value, *own, *sums)
 

time: 17.2 us -> 17.5 us (1.017)
  starting transfers between devices: 9.2 us -> 9.57 us
  waiting for transfers between devices: 1.03 us -> 0.77 us
    pallas_call x3, Pallas kernels: 2.44 us -> 2.87 us  [add_pairs(): pl.pallas_call(functools.partial(early_kernel, len(sums) > 0, own_seg), o...]
    ppermute x6 -> x7, starting transfers between devices: 9.2 us -> 9.57 us  [exchange(): return lax.ppermute(block, 'src', [(s, s ^ mask) for s in range(count)])]
    pallas_call x1, Pallas kernels: 2.1 us -> 1.77 us  [on_device(): pl.pallas_call(functools.partial(last_kernel, count, own_seg), out_shape=...]
    ppermute x6 -> x7, waiting for transfers between devices: 1.03 us -> 0.77 us  [exchange(): return lax.ppermute(block, 'src', [(s, s ^ mask) for s in range(count)])]
  transfers between devices with their start and end apart: 6 -> 7, of which waited for: 2 -> 1; matrix products, arithmetic and copies ran while one was open for 0% -> 0% of each run, Pallas kernels for 18% -> 20%
where the time goes in v11:
time: 17.5 us; the launch traced here: 17.3 us
  starting transfers between devices  9.57 us (55%)
  Pallas kernels  6.2 us (35%)
  waiting for transfers between devices  0.77 us (4%)
  between operations  0.72 us (4%)
    ppermute x7, starting transfers between devices, exchange(): return lax.ppermute(block, 'src', [(s, s ^ mask) for s in range(count)])  9.57 us
    pallas_call x3, Pallas kernels, add_pairs(): pl.pallas_call(functools.partial(early_kernel, len(sums) > 0, own_seg), o...  2.87 us
    pallas_call x1, Pallas kernels, on_device(): pl.pallas_call(functools.partial(last_kernel, count, own_seg), out_shape=...  1.77 us
    pallas_call x1, Pallas kernels, on_device(): pl.pallas_call(functools.partial(pack_kernel, own_seg), out_shape=pltpu.V...  0.92 us
    ppermute x7, waiting for transfers between devices, exchange(): return lax.ppermute(block, 'src', [(s, s ^ mask) for s in range(count)])  0.77 us
    pallas_call x1, Pallas kernels, on_device(): pl.pallas_call(functools.partial(own_kernel, own_seg), out_shape=(pltpu.V...  0.64 us
  transfers between devices with their start and end apart: 7, of which 1 were waited for; matrix products, arithmetic and copies ran while one was open for 0% of the time, Pallas kernels for 20%

profile of v11, /device:TPU:0, one launch (start us, length us, event | category | flops | bytes accessed | tf_op | source)
XLA Modules:
  0.0 17.3 jit_solution(2769440139400730649)
XLA Ops:
  0.6 0.9 %shard_map.86 = f32[24,128]{1,0:T(8,128)S(1)} custom-call(f32[3,128]{1,0:T(4,128)} %points_ref.1, f32[3,128]{1,0:T(4,128)} %normals_ref.1, f32[8,128]{1,0:T(8,128)} %left_ref.1, f32[3,64]{1,0:T(4,128)} %vertices_ref.1, s32[2,128]{1,0:T(2,128)} %connect_ref.1, f32[8,128]{1,0:T(8,128)} %right_ref.1, f32[8]{0:T(128)} %weights_ref.1), custom_call_target="tpu_custom_call" | custom-call | tf_op jit(solution)/shard_map/pallas_call | solution.py:440
  1.5 3.5 %collective-permute-start = (f32[1,24,128]{2,1,0:T(8,128)S(1)}, f32[1,24,128]{2,1,0:T(8,128)S(1)}, u32[]{:S(2)}, u32[]{:S(2)}) collective-permute-start(f32[1,24,128]{2,1,0:T(8,128)S(1)} %bitcast.2), channel_id=1, source_target_pairs={{0,9},{1,8},{2,11},{3,10},{4,13},{5,12},{6,15},{7,14},{8,1},{9,0},... | collective-permute-start | bytes 36872 | tf_op jit(solution)/shard_map/ppermute | solution.py:464
  5.1 0.6 %shard_map.87 = (f32[6,128,128]{2,1,0:T(8,128)S(1)}, f32[8,64,128]{2,1,0:T(8,128)S(1)}, bf16[128,32]{1,0:T(8,128)(2,1)S(1)}, bf16[64,32]{1,0:T(8,128)(2,1)S(1)},...) custom-call(f32[1,24,128]{2,1,0:T(8,128)S(1)} %bitcast.3), custom_call_target="tpu_custom_call" | custom-call | flops 3276800 | bytes 24576 | tf_op jit(solution)/shard_map/pallas_call | solution.py:447
  5.7 0.8 %collective-permute-done = f32[1,24,128]{2,1,0:T(8,128)S(1)} collective-permute-done((f32[1,24,128]{2,1,0:T(8,128)S(1)}, f32[1,24,128]{2,1,0:T(8,128)S(1)}, u32[]{:S(2)}, u32[]{:S(2)}) %collective-permute-start) | collective-permute-done | bytes 12320 | tf_op jit(solution)/shard_map/ppermute | solution.py:464
  6.5 1.9 %collective-permute-start.1 = (f32[2,24,128]{2,1,0:T(8,128)S(1)}, f32[2,24,128]{2,1,0:T(8,128)S(1)}, u32[]{:S(2)}, u32[]{:S(2)}) collective-permute-start(f32[2,24,128]{2,1,0:T(8,128)S(1)} %pad_maximum_fusion.2), channel_id=1, source_target_pairs={{0,5},{1,4},{2,7},{3,6},{4,1},{5,0},{6,3},{7,2},{8,13},{9,12},{10,... | collective-permute-start | bytes 73736 | tf_op jit(solution)/shard_map/ppermute | solution.py:464
  8.4 1.6 %collective-permute-start.2 = (f32[2,24,128]{2,1,0:T(8,128)S(1)}, f32[2,24,128]{2,1,0:T(8,128)S(1)}, u32[]{:S(2)}, u32[]{:S(2)}) collective-permute-start(f32[2,24,128]{2,1,0:T(8,128)S(1)} %pad_maximum_fusion.2), channel_id=1, source_target_pairs={{0,3},{1,2},{2,1},{3,0},{4,7},{5,6},{6,5},{7,4},{8,11},{9,10},{10,... | collective-permute-start | bytes 73736 | tf_op jit(solution)/shard_map/ppermute | solution.py:464
  9.9 0.0 collective-permute-done.1
  9.9 0.5 %collective-permute-start.4 = (f32[4,24,128]{2,1,0:T(8,128)S(1)}, f32[4,24,128]{2,1,0:T(8,128)S(1)}, u32[]{:S(2)}, u32[]{:S(2)}) collective-permute-start(f32[4,24,128]{2,1,0:T(8,128)S(1)} %pad_maximum_fusion.1.refs_0_), channel_id=1, source_target_pairs={{0,1},{1,0},{2,3},{3,2},{4,5},{5,4},{6,7},{7,6},{8,9},{9,8},{10,11... | collective-permute-start | bytes 147464 | tf_op jit(solution)/shard_map/ppermute | solution.py:464
  10.4 1.6 %collective-permute-start.3 = (f32[2,24,128]{2,1,0:T(8,128)S(1)}, f32[2,24,128]{2,1,0:T(8,128)S(1)}, u32[]{:S(2)}, u32[]{:S(2)}) collective-permute-start(f32[2,24,128]{2,1,0:T(8,128)S(1)} %collective-permute-done.1), channel_id=1, source_target_pairs={{0,3},{1,2},{2,1},{3,0},{4,7},{5,6},{6,5},{7,4},{8,11},{9,10},{10,... | collective-permute-start | bytes 73736 | tf_op jit(solution)/shard_map/ppermute | solution.py:464
  12.0 0.0 collective-permute-done.2
  12.0 0.1 collective-permute-start.5
  12.1 0.8 %shard_map.88 = (f32[9,128,128]{2,1,0:T(8,128)S(1)}, f32[11,64,128]{2,1,0:T(8,128)S(1)}) custom-call(f32[4,24,128]{2,1,0:T(8,128)S(1)} %pad_maximum_fusion.1.refs_0_, f32[6,128,128]{2,1,0:T(8,128)S(1)} %get-tuple-element.17.refs_1_, f32[8,64,128]{2,1,0:T(8,128)S(1)} %get-tuple-element.18.refs_2_, bf16[128,32]{1,0:T(8,128)(2,1)S(1)} %get-tuple-element.19.refs_3_, ...), custom_call_target="tpu_custom_call" | custom-call | flops 6553600 | bytes 49152 | tf_op jit(solution)/shard_map/pallas_call | solution.py:467
  12.9 0.0 collective-permute-done.4.refs_0_
  12.9 0.8 %shard_map.89 = (f32[9,128,128]{2,1,0:T(8,128)S(1)}, f32[11,64,128]{2,1,0:T(8,128)S(1)}) custom-call(f32[4,24,128]{2,1,0:T(8,128)S(1)} %collective-permute-done.4.refs_0_, f32[6,128,128]{2,1,0:T(8,128)S(1)} %get-tuple-element.17.refs_1_, f32[8,64,128]{2,1,0:T(8,128)S(1)} %get-tuple-element.18.refs_2_, bf16[128,32]{1,0:T(8,128)(2,1)S(1)} %get-tuple-element.19.refs_3_, ...), custom_call_target="tpu_custom_call" | custom-call | flops 6553600 | bytes 49152 | tf_op jit(solution)/shard_map/pallas_call | solution.py:467
  13.8 0.0 collective-permute-done.3
  13.8 0.4 %collective-permute-start.6 = (f32[2,24,128]{2,1,0:T(8,128)S(1)}, f32[2,24,128]{2,1,0:T(8,128)S(1)}, u32[]{:S(2)}, u32[]{:S(2)}) collective-permute-start(f32[2,24,128]{2,1,0:T(8,128)S(1)} %collective-permute-done.3), channel_id=1, source_target_pairs={{0,1},{1,0},{2,3},{3,2},{4,5},{5,4},{6,7},{7,6},{8,9},{9,8},{10,11... | collective-permute-start | bytes 73736 | tf_op jit(solution)/shard_map/ppermute | solution.py:464
  14.2 0.0 collective-permute-done.5
  14.3 1.2 %shard_map.90 = (f32[9,128,128]{2,1,0:T(8,128)S(1)}, f32[11,64,128]{2,1,0:T(8,128)S(1)}) custom-call(f32[6,24,128]{2,1,0:T(8,128)S(1)} %pad_maximum_fusion.refs_0_, f32[6,128,128]{2,1,0:T(8,128)S(1)} %get-tuple-element.17.refs_1_, f32[8,64,128]{2,1,0:T(8,128)S(1)} %get-tuple-element.18.refs_2_, bf16[128,32]{1,0:T(8,128)(2,1)S(1)} %get-tuple-element.19.refs_3_, ...), custom_call_target="tpu_custom_call" | custom-call | flops 9830400 | bytes 73728 | tf_op jit(solution)/shard_map/pallas_call | solution.py:467
  15.5 0.0 collective-permute-done.6
  15.5 1.8 %shard_map.91 = (f32[6,128]{1,0:T(8,128)}, f32[3,64]{1,0:T(4,128)}) custom-call(f32[16,24,128]{2,1,0:T(8,128)S(1)} %constant_dynamic-update-slice_fusion.refs_0_, f32[6,128,128]{2,1,0:T(8,128)S(1)} %get-tuple-element.17.refs_1_, f32[8,64,128]{2,1,0:T(8,128)S(1)} %get-tuple-element.18.refs_2_, bf16[128,32]{1,0:T(8,128)(2,1)S(1)} %get-tuple-element.19.refs_3_, ...), custom_call_target="tpu_custom_call" | custom-call | flops 3276800 | bytes 24576 | tf_op jit(solution)/shard_map/pallas_call | solution.py:490
  (11 shorter events, 0.0 us)
Async XLA Ops:
  1.5 4.9 %collective-permute-start = (f32[1,24,128]{2,1,0:T(8,128)S(1)}, f32[1,24,128]{2,1,0:T(8,128)S(1)}, u32[]{:S(2)}, u32[]{:S(2)}) collective-permute-start(f32[1,24,128]{2,1,0:T(8,128)S(1)} %bitcast.2), channel_id=1, source_target_pairs={{0,9},{1,8},{2,11},{3,10},{4,13},{5,12},{6,15},{7,14},{8,1},{9,0},... | collective-permute-start | bytes 36872 | tf_op jit(solution)/shard_map/ppermute | solution.py:464
  6.5 3.4 %collective-permute-start.1 = (f32[2,24,128]{2,1,0:T(8,128)S(1)}, f32[2,24,128]{2,1,0:T(8,128)S(1)}, u32[]{:S(2)}, u32[]{:S(2)}) collective-permute-start(f32[2,24,128]{2,1,0:T(8,128)S(1)} %pad_maximum_fusion.2), channel_id=1, source_target_pairs={{0,5},{1,4},{2,7},{3,6},{4,1},{5,0},{6,3},{7,2},{8,13},{9,12},{10,... | collective-permute-start | bytes 73736 | tf_op jit(solution)/shard_map/ppermute | solution.py:464
  8.4 3.6 %collective-permute-start.2 = (f32[2,24,128]{2,1,0:T(8,128)S(1)}, f32[2,24,128]{2,1,0:T(8,128)S(1)}, u32[]{:S(2)}, u32[]{:S(2)}) collective-permute-start(f32[2,24,128]{2,1,0:T(8,128)S(1)} %pad_maximum_fusion.2), channel_id=1, source_target_pairs={{0,3},{1,2},{2,1},{3,0},{4,7},{5,6},{6,5},{7,4},{8,11},{9,10},{10,... | collective-permute-start | bytes 73736 | tf_op jit(solution)/shard_map/ppermute | solution.py:464
  9.9 3.0 %collective-permute-start.4 = (f32[4,24,128]{2,1,0:T(8,128)S(1)}, f32[4,24,128]{2,1,0:T(8,128)S(1)}, u32[]{:S(2)}, u32[]{:S(2)}) collective-permute-start(f32[4,24,128]{2,1,0:T(8,128)S(1)} %pad_maximum_fusion.1.refs_0_), channel_id=1, source_target_pairs={{0,1},{1,0},{2,3},{3,2},{4,5},{5,4},{6,7},{7,6},{8,9},{9,8},{10,11... | collective-permute-start | bytes 147464 | tf_op jit(solution)/shard_map/ppermute | solution.py:464
  10.4 3.4 %collective-permute-start.3 = (f32[2,24,128]{2,1,0:T(8,128)S(1)}, f32[2,24,128]{2,1,0:T(8,128)S(1)}, u32[]{:S(2)}, u32[]{:S(2)}) collective-permute-start(f32[2,24,128]{2,1,0:T(8,128)S(1)} %collective-permute-done.1), channel_id=1, source_target_pairs={{0,3},{1,2},{2,1},{3,0},{4,7},{5,6},{6,5},{7,4},{8,11},{9,10},{10,... | collective-permute-start | bytes 73736 | tf_op jit(solution)/shard_map/ppermute | solution.py:464
  12.0 2.3 %collective-permute-start.5 = (f32[2,24,128]{2,1,0:T(8,128)S(1)}, f32[2,24,128]{2,1,0:T(8,128)S(1)}, u32[]{:S(2)}, u32[]{:S(2)}) collective-permute-start(f32[2,24,128]{2,1,0:T(8,128)S(1)} %collective-permute-done.2), channel_id=1, source_target_pairs={{0,1},{1,0},{2,3},{3,2},{4,5},{5,4},{6,7},{7,6},{8,9},{9,8},{10,11... | collective-permute-start | bytes 73736 | tf_op jit(solution)/shard_map/ppermute | solution.py:464
  13.8 1.7 %collective-permute-start.6 = (f32[2,24,128]{2,1,0:T(8,128)S(1)}, f32[2,24,128]{2,1,0:T(8,128)S(1)}, u32[]{:S(2)}, u32[]{:S(2)}) collective-permute-start(f32[2,24,128]{2,1,0:T(8,128)S(1)} %collective-permute-done.3), channel_id=1, source_target_pairs={{0,1},{1,0},{2,3},{3,2},{4,5},{5,4},{6,7},{7,6},{8,9},{9,8},{10,11... | collective-permute-start | bytes 73736 | tf_op jit(solution)/shard_map/ppermute | solution.py:464

commit v12 on v11

--- a/solution.py
+++ b/solution.py
@@ -54,6 +54,25 @@
     return lax.dot_general(left, right, (((1,), (1,)), ((), ())), preferred_element_type=jnp.float32)
 
 
+def dot3(a, b):
+    return a[0] * b[0] + a[1] * b[1] + a[2] * b[2]
+
+
+def three_parts(value):
+    high, rest = high_low(value)
+    return high, *high_low(rest)
+
+
+def stack_left(rows):
+    high, middle, low = three_parts(rows)
+    return jnp.transpose(jnp.concatenate([high, high, middle, high, low, middle], 0)).astype(jnp.bfloat16)
+
+
+def stack_right(rows):
+    high, middle, low = three_parts(rows)
+    return jnp.concatenate([high, middle, high, low, high, middle], 0).astype(jnp.bfloat16)
+
+
 def cross(a, b):
     return (a[1] * b[2] - a[2] * b[1], a[2] * b[0] - a[0] * b[2], a[0] * b[1] - a[1] * b[0])
 
@@ -64,10 +83,7 @@
     )
 
 
-def pair_terms(point, cross_n, first, segment, span, span_core, scale, want_span):
-    rel = tuple(p - e for p, e in zip(point, first))
-    dist_sq = rel[0] * rel[0] + rel[1] * rel[1] + rel[2] * rel[2]
-    along = segment[0] * rel[0] + segment[1] * rel[1] + segment[2] * rel[2]
+def pair_terms(dist_sq, along, cross_n, span, span_core, scale, want_span):
     other = along - span
     second_sq = dist_sq - along - other
     inv_first = lax.rsqrt(dist_sq)
@@ -86,9 +102,9 @@
     by_dist2 = by_line * (cube_second - cube_first) - by_den2 * span
     by_along = by_line * ((inv_first - inv_second) - cube_second) + by_den2 * along
     if not want_span:
-        return rel, by_normal, by_dist2, by_along
+        return by_normal, by_dist2, by_along
     by_span2 = by_line * ((inv_second + inv_second) + cube_second) - by_den2 * (dist_sq + core_term)
-    return rel, by_normal, by_dist2, by_along, by_span2
+    return by_normal, by_dist2, by_along, by_span2
 
 
 def segment_terms(first, second):
@@ -137,7 +153,7 @@
     return (lane == own_seg - 1) | (lane == 2 * own_seg - 1)
 
 
-def own_kernel(own_seg, data_ref, col1_ref, col2_ref, left_ref, right_ref, moment_ref, turn_ref):
+def own_kernel(own_seg, data_ref, col1_ref, col2_ref, left_ref, right_ref, moment_ref, turn_ref, point_ref, reach_ref):
     def columns(rows, out_ref):
         pad = jnp.zeros((16 - len(rows), LANES), jnp.float32)
         cols = jnp.transpose(jnp.concatenate(list(rows) + [pad], 0))
@@ -155,11 +171,18 @@
     pad = jnp.zeros((2, LANES), jnp.float32)
     moment_ref[...] = stack_hhll(jnp.concatenate([*moment, *normal, pad], 0))
     turn_ref[...] = stack_hhll(jnp.concatenate([*own_s, *(-value for value in own_t), pad], 0))[0:own_seg]
+    one, pad = jnp.ones((1, LANES), jnp.float32), jnp.zeros((3, LANES), jnp.float32)
+    point_ref[...] = stack_left(jnp.concatenate([*point, one, dot3(point, point), pad], 0))
+    along = jnp.concatenate([*own_s, -dot3(own_s, own_e), 0.0 * one, pad], 0)
+    dist_sq = jnp.concatenate([*(-2.0 * value for value in own_e), dot3(own_e, own_e), one, pad], 0)
+    reach_ref[0:own_seg, :] = stack_left(along)[0:own_seg]
+    reach_ref[own_seg : 2 * own_seg, :] = stack_left(dist_sq)[0:own_seg]
 
 
 def pair_sums(data_ref, own_refs, begin, end, own_seg, scratch, old1, old2, new1, new2, between=None):
-    seg_ref, rec_ref, scale1_ref, scale2_ref, row1_ref, row2_ref, cross1_ref, cross2_ref = scratch
-    col1_ref, col2_ref, left_ref, right_ref, moment_ref, turn_ref = own_refs
+    seg_ref, rec_ref, scale1_ref, scale2_ref, row1_ref, row2_ref, cross1_ref, cross2_ref = scratch[0:8]
+    near1_ref, near2_ref, reach1_ref, reach2_ref = scratch[8:]
+    col1_ref, col2_ref, left_ref, right_ref, moment_ref, turn_ref, point_ref, reach_ref = own_refs
     blocks = end - begin
     tiles = blocks // 2
     lane = lax.broadcasted_iota(jnp.int32, (1, LANES), 1)
@@ -206,6 +229,25 @@
     cross1_ref[...] = jnp.dot(moment_ref[...], stack_hlhl(row1_ref[...]), preferred_element_type=jnp.float32)
     cross2_ref[...] = jnp.dot(turn_ref[...], stack_hlhl(row2_ref[...]), preferred_element_type=jnp.float32)
 
+    near1_ref[3:8, :] = jnp.zeros((5, near1_ref.shape[1]), jnp.float32)
+    near1_ref[4:5, tiles * LANES :] = jnp.ones((1, tiles * LANES), jnp.float32)
+    near2_ref[3:4, :] = jnp.ones((1, near2_ref.shape[1]), jnp.float32)
+    near2_ref[4:8, :] = jnp.zeros((4, near2_ref.shape[1]), jnp.float32)
+    offset, length, reach = -dot3(segment, first), dot3(first, first), dot3(point, point)
+    for tile in range(tiles):
+        at, after = slice(tile * LANES, (tile + 1) * LANES), slice((tiles + tile) * LANES, (tiles + tile + 1) * LANES)
+        for axis in range(3):
+            near1_ref[axis : axis + 1, at] = segment[axis][tile : tile + 1]
+            near1_ref[axis : axis + 1, after] = -2.0 * first[axis][tile : tile + 1]
+        near1_ref[3:4, at] = offset[tile : tile + 1]
+        near1_ref[3:4, after] = length[tile : tile + 1]
+    for block in range(blocks):
+        at = slice(block * LANES, (block + 1) * LANES)
+        near2_ref[0:3, at] = data_ref[begin + block, 8:11, :]
+        near2_ref[4:5, at] = reach[block : block + 1]
+    reach1_ref[...] = jnp.dot(point_ref[...], stack_right(near1_ref[...]), preferred_element_type=jnp.float32)
+    reach2_ref[...] = jnp.dot(reach_ref[...], stack_right(near2_ref[...]), preferred_element_type=jnp.float32)
+
     scale1_ref[...] = jnp.dot(
         left_ref[...], stack_hlhl(jnp.concatenate(folded, 1)), preferred_element_type=jnp.float32)
     scale2_ref[...] = jnp.dot(
@@ -218,41 +260,44 @@
         return [old[k, start : start + CHUNK, :] for k in range(count)]
 
     for start in range(0, LANES, CHUNK):
-        col = [col1_ref[k, start : start + CHUNK, :] for k in range(3)]
-        sums = initial(old1, 9, start)
+        rows = slice(start, start + CHUNK)
+        sums = initial(old1, 10, start)
         for tile in range(tiles):
+            at, after = slice(tile * LANES, (tile + 1) * LANES), slice((tiles + tile) * LANES, (tiles + tile + 1) * LANES)
             row = [seg_ref[k, tile : tile + 1, :] for k in range(11)]
-            scale = scale1_ref[start : start + CHUNK, tile * LANES : (tile + 1) * LANES]
-            rel, by_normal, by_dist2, by_along = pair_terms(
-                col, cross1_ref[start : start + CHUNK, tile * LANES : (tile + 1) * LANES],
-                row[0:3], row[3:6], row[9], row[10], scale, False)
+            by_normal, by_dist2, by_along = pair_terms(
+                reach1_ref[rows, after], reach1_ref[rows, at], cross1_ref[rows, at], row[9], row[10],
+                scale1_ref[rows, at], False)
             for axis in range(3):
                 sums[axis] += by_normal * row[3 + axis]
                 sums[3 + axis] += by_normal * row[6 + axis]
-                sums[6 + axis] += by_dist2 * rel[axis] + by_along * row[3 + axis]
-        for k in range(9):
-            new1[k, start : start + CHUNK, :] = sums[k]
+                sums[6 + axis] += by_along * row[3 + axis] - by_dist2 * row[axis]
+            sums[9] += by_dist2
+        for k in range(10):
+            new1[k, rows, :] = sums[k]
 
     if between is not None:
         between()
 
     for start in range(0, own_seg, CHUNK):
-        col = [col2_ref[k, start : start + CHUNK, :] for k in range(8)]
-        sums = initial(old2, 11, start)
+        rows, under = slice(start, start + CHUNK), slice(own_seg + start, own_seg + start + CHUNK)
+        span, span_core = col2_ref[6, rows, :], col2_ref[7, rows, :]
+        sums = initial(old2, 12, start)
         for block in range(blocks):
+            at = slice(block * LANES, (block + 1) * LANES)
             row = [rec_ref[k, block : block + 1, :] for k in range(9)]
-            scale = scale2_ref[start : start + CHUNK, block * LANES : (block + 1) * LANES]
-            rel, by_normal, by_dist2, by_along, by_span2 = pair_terms(
-                row[0:3], cross2_ref[start : start + CHUNK, block * LANES : (block + 1) * LANES],
-                col[0:3], col[3:6], col[6], col[7], scale, True)
+            by_normal, by_dist2, by_along, by_span2 = pair_terms(
+                reach2_ref[under, at], reach2_ref[rows, at], cross2_ref[rows, at], span, span_core,
+                scale2_ref[rows, at], True)
             for axis in range(3):
                 sums[axis] += by_normal * row[3 + axis]
-                sums[3 + axis] += by_normal * row[6 + axis] + by_along * rel[axis]
-                sums[6 + axis] += by_dist2 * rel[axis]
+                sums[3 + axis] += by_normal * row[6 + axis] + by_along * row[axis]
+                sums[6 + axis] += by_dist2 * row[axis]
             sums[9] += by_along
             sums[10] += by_span2
-        for k in range(11):
-            new2[k, start : start + CHUNK, :] = sums[k]
+            sums[11] += by_dist2
+        for k in range(12):
+            new2[k, rows, :] = sums[k]
 
 
 def lane_sums(values):
@@ -267,9 +312,9 @@
 def receiver_totals(sums_ref, col_ref):
     parts = []
     for start in range(0, LANES, FINISH):
-        sums = [sums_ref[k, start : start + FINISH, :] for k in range(9)]
+        sums = [sums_ref[k, start : start + FINISH, :] for k in range(10)]
         col = [col_ref[k, start : start + FINISH, :] for k in range(6)]
-        by_point = [a + b for a, b in zip(cross(col[3:6], sums[0:3]), sums[6:9])]
+        by_point = [a + b + p * sums[9] for a, b, p in zip(cross(col[3:6], sums[0:3]), sums[6:9], col[0:3])]
         by_normal = [a - b for a, b in zip(cross(sums[0:3], col[0:3]), sums[3:6])]
         parts.append(lane_sums(by_point + by_normal))
     return jnp.transpose(jnp.concatenate(parts, 0))
@@ -278,11 +323,12 @@
 def segment_totals(sums_ref, col_ref, own_seg, arriving, leaving):
     parts = []
     for start in range(0, own_seg, FINISH):
-        sums = [sums_ref[k, start : start + FINISH, :] for k in range(11)]
+        sums = [sums_ref[k, start : start + FINISH, :] for k in range(12)]
         col = [col_ref[k, start : start + FINISH, :] for k in range(6)]
         turned, swept = cross(col[0:3], sums[0:3]), cross(sums[0:3], col[3:6])
-        by_s = [sums[3 + k] - turned[k] + col[3 + k] * sums[10] for k in range(3)]
-        by_both = [by_s[k] + (swept[k] + sums[6 + k] + col[3 + k] * sums[9]) for k in range(3)]
+        by_s = [sums[3 + k] - turned[k] - col[k] * sums[9] + col[3 + k] * sums[10] for k in range(3)]
+        by_both = [
+            by_s[k] + (swept[k] + sums[6 + k] - col[k] * sums[11] + col[3 + k] * sums[9]) for k in range(3)]
         if start + FINISH == own_seg:
             last = lax.broadcasted_iota(jnp.int32, (FINISH, LANES), 0) == FINISH - 1
             by_s = [jnp.where(last, a, b) for a, b in zip(arriving, by_s)]
@@ -307,7 +353,7 @@
 
 
 def early_kernel(chained, own_seg, *refs):
-    data_ref, own_refs, rest = refs[0], refs[1:7], refs[7:]
+    data_ref, own_refs, rest = refs[0], refs[1:9], refs[9:]
     olds = rest[0:2] if chained else (None, None)
     rest = rest[2:] if chained else rest
     pair_sums(data_ref, own_refs, 0, data_ref.shape[0], own_seg, rest[2:], *olds, rest[0], rest[1])
@@ -315,8 +361,8 @@
 
 def last_kernel(count, own_seg, *refs):
     data_ref, own_refs, old1_ref, old2_ref, rcv_out, vert_out, after_ref, new1_ref, new2_ref = (
-        refs[0], refs[1:7], *refs[7:14])
-    scratch = refs[14:]
+        refs[0], refs[1:9], *refs[9:16])
+    scratch = refs[16:]
     masks = exchange_masks(count)
     me = lax.axis_index("src")
     lane = lax.broadcasted_iota(jnp.int32, (1, LANES), 1)
@@ -367,9 +413,10 @@
             scales[2] += before_weight[mode : mode + 1] * left
         segment, turn, span, span_core = segment_terms(first, second)
         normals = stacked(own_n, normal)
-        rel, by_normal, by_dist2, by_along, by_span2 = pair_terms(
-            stacked(own_p, point), normal_cross(normals, stacked(own_m, moment), segment, turn),
-            first, segment, span, span_core, jnp.concatenate(scales, 0), True)
+        rel = tuple(p - e for p, e in zip(stacked(own_p, point), first))
+        by_normal, by_dist2, by_along, by_span2 = pair_terms(
+            dot3(rel, rel), dot3(segment, rel), normal_cross(normals, stacked(own_m, moment), segment, turn),
+            span, span_core, jnp.concatenate(scales, 0), True)
 
         def down(value):
             return jnp.sum(value, axis=0, keepdims=True)
@@ -418,11 +465,15 @@
         pltpu.VMEM((8, blocks * LANES), jnp.float32),
         pltpu.VMEM((LANES, blocks // 2 * LANES), jnp.float32),
         pltpu.VMEM((own_seg, blocks * LANES), jnp.float32),
+        pltpu.VMEM((8, blocks * LANES), jnp.float32),
+        pltpu.VMEM((8, blocks * LANES), jnp.float32),
+        pltpu.VMEM((LANES, blocks * LANES), jnp.float32),
+        pltpu.VMEM((2 * own_seg, blocks * LANES), jnp.float32),
     ]
 
 
 def sum_shapes(own_seg):
-    return [pltpu.VMEM((9, LANES, LANES), jnp.float32), pltpu.VMEM((11, own_seg, LANES), jnp.float32)]
+    return [pltpu.VMEM((10, LANES, LANES), jnp.float32), pltpu.VMEM((12, own_seg, LANES), jnp.float32)]
 
 
 def last_scratch(count, own_seg):
@@ -453,9 +504,11 @@
             pltpu.VMEM((own_seg, 32), jnp.bfloat16),
             pltpu.VMEM((LANES, 32), jnp.bfloat16),
             pltpu.VMEM((own_seg, 32), jnp.bfloat16),
+            pltpu.VMEM((LANES, 48), jnp.bfloat16),
+            pltpu.VMEM((2 * own_seg, 48), jnp.bfloat16),
         ),
         in_specs=[VMEM],
-        out_specs=(VMEM,) * 6,
+        out_specs=(VMEM,) * 8,
         cost_estimate=pair_cost(2, own_seg),
         compiler_params=params,
     )(value)
@@ -467,7 +520,7 @@
         return pl.pallas_call(
             functools.partial(early_kernel, len(sums) > 0, own_seg),
             out_shape=tuple(sum_shapes(own_seg)),
-            in_specs=[VMEM] * (7 + len(sums)),
+            in_specs=[VMEM] * (9 + len(sums)),
             out_specs=(VMEM, VMEM),
             scratch_shapes=pair_scratch(block.shape[0], own_seg),
             cost_estimate=pair_cost(block.shape[0], own_seg),
@@ -493,7 +546,7 @@
             jax.ShapeDtypeStruct((6, LANES), jnp.float32),
             jax.ShapeDtypeStruct((3, own_seg), jnp.float32),
         ),
-        in_specs=[VMEM] * 9,
+        in_specs=[VMEM] * 11,
         out_specs=(VMEM, VMEM),
         scratch_shapes=last_scratch(count, own_seg),
         cost_estimate=pair_cost(count // 8, own_seg),

time: 17.5 us -> 17.6 us (level)
  transfers between devices with their start and end apart: 7 -> 7, of which waited for: 1 -> 1; matrix products, arithmetic and copies ran while one was open for 0% -> 0% of each run, Pallas kernels for 20% -> 21%
where the time goes in v12:
time: 17.6 us; the launch traced here: 17.4 us
  starting transfers between devices  9.57 us (54%)
  Pallas kernels  6.36 us (36%)
  waiting for transfers between devices  0.74 us (4%)
  between operations  0.72 us (4%)
    ppermute x7, starting transfers between devices, exchange(): return lax.ppermute(block, 'src', [(s, s ^ mask) for s in range(count)])  9.57 us
    pallas_call x3, Pallas kernels, add_pairs(): pl.pallas_call(functools.partial(early_kernel, len(sums) > 0, own_seg), o...  2.93 us
    pallas_call x1, Pallas kernels, on_device(): pl.pallas_call(functools.partial(last_kernel, count, own_seg), out_shape=...  1.84 us
    pallas_call x1, Pallas kernels, on_device(): pl.pallas_call(functools.partial(pack_kernel, own_seg), out_shape=pltpu.V...  0.92 us
    ppermute x7, waiting for transfers between devices, exchange(): return lax.ppermute(block, 'src', [(s, s ^ mask) for s in range(count)])  0.74 us
    pallas_call x1, Pallas kernels, on_device(): pl.pallas_call(functools.partial(own_kernel, own_seg), out_shape=(pltpu.V...  0.68 us
  transfers between devices with their start and end apart: 7, of which 1 were waited for; matrix products, arithmetic and copies ran while one was open for 0% of the time, Pallas kernels for 21%

profile of v12, /device:TPU:0, one launch (start us, length us, event | category | flops | bytes accessed | tf_op | source)
XLA Modules:
  0.0 17.4 jit_solution(3694293558925101959)
XLA Ops:
  0.6 0.9 %shard_map.86 = f32[24,128]{1,0:T(8,128)S(1)} custom-call(f32[3,128]{1,0:T(4,128)} %points_ref.1, f32[3,128]{1,0:T(4,128)} %normals_ref.1, f32[8,128]{1,0:T(8,128)} %left_ref.1, f32[3,64]{1,0:T(4,128)} %vertices_ref.1, s32[2,128]{1,0:T(2,128)} %connect_ref.1, f32[8,128]{1,0:T(8,128)} %right_ref.1, f32[8]{0:T(128)} %weights_ref.1), custom_call_target="tpu_custom_call" | custom-call | tf_op jit(solution)/shard_map/pallas_call | solution.py:491
  1.5 3.5 %collective-permute-start = (f32[1,24,128]{2,1,0:T(8,128)S(1)}, f32[1,24,128]{2,1,0:T(8,128)S(1)}, u32[]{:S(2)}, u32[]{:S(2)}) collective-permute-start(f32[1,24,128]{2,1,0:T(8,128)S(1)} %bitcast.2), channel_id=1, source_target_pairs={{0,9},{1,8},{2,11},{3,10},{4,13},{5,12},{6,15},{7,14},{8,1},{9,0},... | collective-permute-start | bytes 36872 | tf_op jit(solution)/shard_map/ppermute | solution.py:517
  5.1 0.7 %shard_map.87 = (f32[6,128,128]{2,1,0:T(8,128)S(1)}, f32[8,64,128]{2,1,0:T(8,128)S(1)}, bf16[128,32]{1,0:T(8,128)(2,1)S(1)}, bf16[64,32]{1,0:T(8,128)(2,1)S(1)},...) custom-call(f32[1,24,128]{2,1,0:T(8,128)S(1)} %bitcast.3), custom_call_target="tpu_custom_call" | custom-call | flops 3276800 | bytes 24576 | tf_op jit(solution)/shard_map/pallas_call | solution.py:498
  5.8 0.7 %collective-permute-done = f32[1,24,128]{2,1,0:T(8,128)S(1)} collective-permute-done((f32[1,24,128]{2,1,0:T(8,128)S(1)}, f32[1,24,128]{2,1,0:T(8,128)S(1)}, u32[]{:S(2)}, u32[]{:S(2)}) %collective-permute-start) | collective-permute-done | bytes 12320 | tf_op jit(solution)/shard_map/ppermute | solution.py:517
  6.5 1.9 %collective-permute-start.1 = (f32[2,24,128]{2,1,0:T(8,128)S(1)}, f32[2,24,128]{2,1,0:T(8,128)S(1)}, u32[]{:S(2)}, u32[]{:S(2)}) collective-permute-start(f32[2,24,128]{2,1,0:T(8,128)S(1)} %pad_maximum_fusion.2), channel_id=1, source_target_pairs={{0,5},{1,4},{2,7},{3,6},{4,1},{5,0},{6,3},{7,2},{8,13},{9,12},{10,... | collective-permute-start | bytes 73736 | tf_op jit(solution)/shard_map/ppermute | solution.py:517
  8.4 1.6 %collective-permute-start.2 = (f32[2,24,128]{2,1,0:T(8,128)S(1)}, f32[2,24,128]{2,1,0:T(8,128)S(1)}, u32[]{:S(2)}, u32[]{:S(2)}) collective-permute-start(f32[2,24,128]{2,1,0:T(8,128)S(1)} %pad_maximum_fusion.2), channel_id=1, source_target_pairs={{0,3},{1,2},{2,1},{3,0},{4,7},{5,6},{6,5},{7,4},{8,11},{9,10},{10,... | collective-permute-start | bytes 73736 | tf_op jit(solution)/shard_map/ppermute | solution.py:517
  9.9 0.0 collective-permute-done.1
  9.9 0.5 %collective-permute-start.4 = (f32[4,24,128]{2,1,0:T(8,128)S(1)}, f32[4,24,128]{2,1,0:T(8,128)S(1)}, u32[]{:S(2)}, u32[]{:S(2)}) collective-permute-start(f32[4,24,128]{2,1,0:T(8,128)S(1)} %pad_maximum_fusion.1.refs_0_), channel_id=1, source_target_pairs={{0,1},{1,0},{2,3},{3,2},{4,5},{5,4},{6,7},{7,6},{8,9},{9,8},{10,11... | collective-permute-start | bytes 147464 | tf_op jit(solution)/shard_map/ppermute | solution.py:517
  10.4 1.6 %collective-permute-start.3 = (f32[2,24,128]{2,1,0:T(8,128)S(1)}, f32[2,24,128]{2,1,0:T(8,128)S(1)}, u32[]{:S(2)}, u32[]{:S(2)}) collective-permute-start(f32[2,24,128]{2,1,0:T(8,128)S(1)} %collective-permute-done.1), channel_id=1, source_target_pairs={{0,3},{1,2},{2,1},{3,0},{4,7},{5,6},{6,5},{7,4},{8,11},{9,10},{10,... | collective-permute-start | bytes 73736 | tf_op jit(solution)/shard_map/ppermute | solution.py:517
  12.0 0.0 collective-permute-done.2
  12.0 0.1 collective-permute-start.5
  12.1 0.8 %shard_map.88 = (f32[10,128,128]{2,1,0:T(8,128)S(1)}, f32[12,64,128]{2,1,0:T(8,128)S(1)}) custom-call(f32[4,24,128]{2,1,0:T(8,128)S(1)} %pad_maximum_fusion.1.refs_0_, f32[6,128,128]{2,1,0:T(8,128)S(1)} %get-tuple-element.19.refs_1_, f32[8,64,128]{2,1,0:T(8,128)S(1)} %get-tuple-element.20.refs_2_, bf16[128,32]{1,0:T(8,128)(2,1)S(1)} %get-tuple-element.21.refs_3_, ...), custom_call_target="tpu_custom_call" | custom-call | flops 6553600 | bytes 49152 | tf_op jit(solution)/shard_map/pallas_call | solution.py:520
  12.9 0.0 collective-permute-done.4.refs_0_
  12.9 0.8 %shard_map.89 = (f32[10,128,128]{2,1,0:T(8,128)S(1)}, f32[12,64,128]{2,1,0:T(8,128)S(1)}) custom-call(f32[4,24,128]{2,1,0:T(8,128)S(1)} %collective-permute-done.4.refs_0_, f32[6,128,128]{2,1,0:T(8,128)S(1)} %get-tuple-element.19.refs_1_, f32[8,64,128]{2,1,0:T(8,128)S(1)} %get-tuple-element.20.refs_2_, bf16[128,32]{1,0:T(8,128)(2,1)S(1)} %get-tuple-element.21.refs_3_, ...), custom_call_target="tpu_custom_call" | custom-call | flops 6553600 | bytes 49152 | tf_op jit(solution)/shard_map/pallas_call | solution.py:520
  13.8 0.0 collective-permute-done.3
  13.8 0.4 %collective-permute-start.6 = (f32[2,24,128]{2,1,0:T(8,128)S(1)}, f32[2,24,128]{2,1,0:T(8,128)S(1)}, u32[]{:S(2)}, u32[]{:S(2)}) collective-permute-start(f32[2,24,128]{2,1,0:T(8,128)S(1)} %collective-permute-done.3), channel_id=1, source_target_pairs={{0,1},{1,0},{2,3},{3,2},{4,5},{5,4},{6,7},{7,6},{8,9},{9,8},{10,11... | collective-permute-start | bytes 73736 | tf_op jit(solution)/shard_map/ppermute | solution.py:517
  14.2 0.0 collective-permute-done.5
  14.3 1.3 %shard_map.90 = (f32[10,128,128]{2,1,0:T(8,128)S(1)}, f32[12,64,128]{2,1,0:T(8,128)S(1)}) custom-call(f32[6,24,128]{2,1,0:T(8,128)S(1)} %pad_maximum_fusion.refs_0_, f32[6,128,128]{2,1,0:T(8,128)S(1)} %get-tuple-element.19.refs_1_, f32[8,64,128]{2,1,0:T(8,128)S(1)} %get-tuple-element.20.refs_2_, bf16[128,32]{1,0:T(8,128)(2,1)S(1)} %get-tuple-element.21.refs_3_, ...), custom_call_target="tpu_custom_call" | custom-call | flops 9830400 | bytes 73728 | tf_op jit(solution)/shard_map/pallas_call | solution.py:520
  15.6 0.0 collective-permute-done.6
  15.6 1.8 %shard_map.91 = (f32[6,128]{1,0:T(8,128)}, f32[3,64]{1,0:T(4,128)}) custom-call(f32[16,24,128]{2,1,0:T(8,128)S(1)} %constant_dynamic-update-slice_fusion.refs_0_, f32[6,128,128]{2,1,0:T(8,128)S(1)} %get-tuple-element.19.refs_1_, f32[8,64,128]{2,1,0:T(8,128)S(1)} %get-tuple-element.20.refs_2_, bf16[128,32]{1,0:T(8,128)(2,1)S(1)} %get-tuple-element.21.refs_3_, ...), custom_call_target="tpu_custom_call" | custom-call | flops 3276800 | bytes 24576 | tf_op jit(solution)/shard_map/pallas_call | solution.py:543
  (11 shorter events, 0.0 us)
Async XLA Ops:
  1.5 4.9 %collective-permute-start = (f32[1,24,128]{2,1,0:T(8,128)S(1)}, f32[1,24,128]{2,1,0:T(8,128)S(1)}, u32[]{:S(2)}, u32[]{:S(2)}) collective-permute-start(f32[1,24,128]{2,1,0:T(8,128)S(1)} %bitcast.2), channel_id=1, source_target_pairs={{0,9},{1,8},{2,11},{3,10},{4,13},{5,12},{6,15},{7,14},{8,1},{9,0},... | collective-permute-start | bytes 36872 | tf_op jit(solution)/shard_map/ppermute | solution.py:517
  6.5 3.4 %collective-permute-start.1 = (f32[2,24,128]{2,1,0:T(8,128)S(1)}, f32[2,24,128]{2,1,0:T(8,128)S(1)}, u32[]{:S(2)}, u32[]{:S(2)}) collective-permute-start(f32[2,24,128]{2,1,0:T(8,128)S(1)} %pad_maximum_fusion.2), channel_id=1, source_target_pairs={{0,5},{1,4},{2,7},{3,6},{4,1},{5,0},{6,3},{7,2},{8,13},{9,12},{10,... | collective-permute-start | bytes 73736 | tf_op jit(solution)/shard_map/ppermute | solution.py:517
  8.4 3.6 %collective-permute-start.2 = (f32[2,24,128]{2,1,0:T(8,128)S(1)}, f32[2,24,128]{2,1,0:T(8,128)S(1)}, u32[]{:S(2)}, u32[]{:S(2)}) collective-permute-start(f32[2,24,128]{2,1,0:T(8,128)S(1)} %pad_maximum_fusion.2), channel_id=1, source_target_pairs={{0,3},{1,2},{2,1},{3,0},{4,7},{5,6},{6,5},{7,4},{8,11},{9,10},{10,... | collective-permute-start | bytes 73736 | tf_op jit(solution)/shard_map/ppermute | solution.py:517
  9.9 3.0 %collective-permute-start.4 = (f32[4,24,128]{2,1,0:T(8,128)S(1)}, f32[4,24,128]{2,1,0:T(8,128)S(1)}, u32[]{:S(2)}, u32[]{:S(2)}) collective-permute-start(f32[4,24,128]{2,1,0:T(8,128)S(1)} %pad_maximum_fusion.1.refs_0_), channel_id=1, source_target_pairs={{0,1},{1,0},{2,3},{3,2},{4,5},{5,4},{6,7},{7,6},{8,9},{9,8},{10,11... | collective-permute-start | bytes 147464 | tf_op jit(solution)/shard_map/ppermute | solution.py:517
  10.4 3.4 %collective-permute-start.3 = (f32[2,24,128]{2,1,0:T(8,128)S(1)}, f32[2,24,128]{2,1,0:T(8,128)S(1)}, u32[]{:S(2)}, u32[]{:S(2)}) collective-permute-start(f32[2,24,128]{2,1,0:T(8,128)S(1)} %collective-permute-done.1), channel_id=1, source_target_pairs={{0,3},{1,2},{2,1},{3,0},{4,7},{5,6},{6,5},{7,4},{8,11},{9,10},{10,... | collective-permute-start | bytes 73736 | tf_op jit(solution)/shard_map/ppermute | solution.py:517
  12.0 2.3 %collective-permute-start.5 = (f32[2,24,128]{2,1,0:T(8,128)S(1)}, f32[2,24,128]{2,1,0:T(8,128)S(1)}, u32[]{:S(2)}, u32[]{:S(2)}) collective-permute-start(f32[2,24,128]{2,1,0:T(8,128)S(1)} %collective-permute-done.2), channel_id=1, source_target_pairs={{0,1},{1,0},{2,3},{3,2},{4,5},{5,4},{6,7},{7,6},{8,9},{9,8},{10,11... | collective-permute-start | bytes 73736 | tf_op jit(solution)/shard_map/ppermute | solution.py:517
  13.8 1.8 %collective-permute-start.6 = (f32[2,24,128]{2,1,0:T(8,128)S(1)}, f32[2,24,128]{2,1,0:T(8,128)S(1)}, u32[]{:S(2)}, u32[]{:S(2)}) collective-permute-start(f32[2,24,128]{2,1,0:T(8,128)S(1)} %collective-permute-done.3), channel_id=1, source_target_pairs={{0,1},{1,0},{2,3},{3,2},{4,5},{5,4},{6,7},{7,6},{8,9},{9,8},{10,11... | collective-permute-start | bytes 73736 | tf_op jit(solution)/shard_map/ppermute | solution.py:517

commit v13 on v10

--- a/solution.py
+++ b/solution.py
@@ -482,11 +482,11 @@
     value = jnp.concatenate([value, arrived], 0)
     beside = exchange(value, masks[-1])
     sums = add_pairs(value)
-    sums = add_pairs(beside, *sums)
+    sums = add_pairs(early, *sums)
     late, sums = lax.optimization_barrier((late, sums))
     across = jnp.concatenate([early, late], 0)
     opposite = exchange(across, masks[-1])
-    sums = add_pairs(across, *sums)
+    sums = add_pairs(jnp.concatenate([beside, late], 0), *sums)
     value = jnp.concatenate([value, across, beside, opposite], 0)
     return pl.pallas_call(
         functools.partial(last_kernel, count, own_seg),

time: 17.2 us -> 17.4 us (1.012)
  transfers between devices with their start and end apart: 6 -> 6, of which waited for: 2 -> 2; matrix products, arithmetic and copies ran while one was open for 0% -> 0% of each run, Pallas kernels for 18% -> 19%
where the time goes in v13:
time: 17.4 us; the launch traced here: 17.3 us
  starting transfers between devices  9.17 us (53%)
  Pallas kernels  6.24 us (36%)
  waiting for transfers between devices  1.1 us (6%)
  between operations  0.7 us (4%)
    ppermute x6, starting transfers between devices, exchange(): return lax.ppermute(block, 'src', [(s, s ^ mask) for s in range(count)])  9.17 us
    pallas_call x3, Pallas kernels, add_pairs(): pl.pallas_call(functools.partial(early_kernel, len(sums) > 0, own_seg), o...  2.56 us
    pallas_call x1, Pallas kernels, on_device(): pl.pallas_call(functools.partial(last_kernel, count, own_seg), out_shape=...  2.12 us
    ppermute x6, waiting for transfers between devices, exchange(): return lax.ppermute(block, 'src', [(s, s ^ mask) for s in range(count)])  1.1 us
    pallas_call x1, Pallas kernels, on_device(): pl.pallas_call(functools.partial(pack_kernel, own_seg), out_shape=pltpu.V...  0.92 us
    pallas_call x1, Pallas kernels, on_device(): pl.pallas_call(functools.partial(own_kernel, own_seg), out_shape=(pltpu.V...  0.64 us
  transfers between devices with their start and end apart: 6, of which 2 were waited for; matrix products, arithmetic and copies ran while one was open for 0% of the time, Pallas kernels for 19%

profile of v13, /device:TPU:0, one launch (start us, length us, event | category | flops | bytes accessed | tf_op | source)
XLA Modules:
  0.0 17.3 jit_solution(2894991696398819750)
XLA Ops:
  0.6 0.9 %shard_map.86 = f32[24,128]{1,0:T(8,128)S(1)} custom-call(f32[3,128]{1,0:T(4,128)} %points_ref.1, f32[3,128]{1,0:T(4,128)} %normals_ref.1, f32[8,128]{1,0:T(8,128)} %left_ref.1, f32[3,64]{1,0:T(4,128)} %vertices_ref.1, s32[2,128]{1,0:T(2,128)} %connect_ref.1, f32[8,128]{1,0:T(8,128)} %right_ref.1, f32[8]{0:T(128)} %weights_ref.1), custom_call_target="tpu_custom_call" | custom-call | tf_op jit(solution)/shard_map/pallas_call | solution.py:440
  1.5 3.5 %collective-permute-start = (f32[1,24,128]{2,1,0:T(8,128)S(1)}, f32[1,24,128]{2,1,0:T(8,128)S(1)}, u32[]{:S(2)}, u32[]{:S(2)}) collective-permute-start(f32[1,24,128]{2,1,0:T(8,128)S(1)} %bitcast.2), channel_id=1, source_target_pairs={{0,9},{1,8},{2,11},{3,10},{4,13},{5,12},{6,15},{7,14},{8,1},{9,0},... | collective-permute-start | bytes 36872 | tf_op jit(solution)/shard_map/ppermute | solution.py:464
  5.1 0.6 %shard_map.87 = (f32[6,128,128]{2,1,0:T(8,128)S(1)}, f32[8,64,128]{2,1,0:T(8,128)S(1)}, bf16[128,32]{1,0:T(8,128)(2,1)S(1)}, bf16[64,32]{1,0:T(8,128)(2,1)S(1)},...) custom-call(f32[1,24,128]{2,1,0:T(8,128)S(1)} %bitcast.3), custom_call_target="tpu_custom_call" | custom-call | flops 3276800 | bytes 24576 | tf_op jit(solution)/shard_map/pallas_call | solution.py:447
  5.7 0.8 %collective-permute-done = f32[1,24,128]{2,1,0:T(8,128)S(1)} collective-permute-done((f32[1,24,128]{2,1,0:T(8,128)S(1)}, f32[1,24,128]{2,1,0:T(8,128)S(1)}, u32[]{:S(2)}, u32[]{:S(2)}) %collective-permute-start) | collective-permute-done | bytes 12320 | tf_op jit(solution)/shard_map/ppermute | solution.py:464
  6.5 1.9 %collective-permute-start.1 = (f32[2,24,128]{2,1,0:T(8,128)S(1)}, f32[2,24,128]{2,1,0:T(8,128)S(1)}, u32[]{:S(2)}, u32[]{:S(2)}) collective-permute-start(f32[2,24,128]{2,1,0:T(8,128)S(1)} %pad_maximum_fusion.3), channel_id=1, source_target_pairs={{0,5},{1,4},{2,7},{3,6},{4,1},{5,0},{6,3},{7,2},{8,13},{9,12},{10,... | collective-permute-start | bytes 73736 | tf_op jit(solution)/shard_map/ppermute | solution.py:464
  8.4 1.6 %collective-permute-start.2 = (f32[2,24,128]{2,1,0:T(8,128)S(1)}, f32[2,24,128]{2,1,0:T(8,128)S(1)}, u32[]{:S(2)}, u32[]{:S(2)}) collective-permute-start(f32[2,24,128]{2,1,0:T(8,128)S(1)} %pad_maximum_fusion.3), channel_id=1, source_target_pairs={{0,3},{1,2},{2,1},{3,0},{4,7},{5,6},{6,5},{7,4},{8,11},{9,10},{10,... | collective-permute-start | bytes 73736 | tf_op jit(solution)/shard_map/ppermute | solution.py:464
  9.9 0.0 collective-permute-done.1
  9.9 0.5 %collective-permute-start.4 = (f32[4,24,128]{2,1,0:T(8,128)S(1)}, f32[4,24,128]{2,1,0:T(8,128)S(1)}, u32[]{:S(2)}, u32[]{:S(2)}) collective-permute-start(f32[4,24,128]{2,1,0:T(8,128)S(1)} %pad_maximum_fusion.1.refs_0_), channel_id=1, source_target_pairs={{0,1},{1,0},{2,3},{3,2},{4,5},{5,4},{6,7},{7,6},{8,9},{9,8},{10,11... | collective-permute-start | bytes 147464 | tf_op jit(solution)/shard_map/ppermute | solution.py:464
  10.4 1.6 %collective-permute-start.3 = (f32[2,24,128]{2,1,0:T(8,128)S(1)}, f32[2,24,128]{2,1,0:T(8,128)S(1)}, u32[]{:S(2)}, u32[]{:S(2)}) collective-permute-start(f32[2,24,128]{2,1,0:T(8,128)S(1)} %collective-permute-done.1), channel_id=1, source_target_pairs={{0,3},{1,2},{2,1},{3,0},{4,7},{5,6},{6,5},{7,4},{8,11},{9,10},{10,... | collective-permute-start | bytes 73736 | tf_op jit(solution)/shard_map/ppermute | solution.py:464
  12.0 0.0 collective-permute-done.2.refs_0_
  12.0 0.8 %shard_map.88 = (f32[9,128,128]{2,1,0:T(8,128)S(1)}, f32[11,64,128]{2,1,0:T(8,128)S(1)}) custom-call(f32[4,24,128]{2,1,0:T(8,128)S(1)} %pad_maximum_fusion.1.refs_0_, f32[6,128,128]{2,1,0:T(8,128)S(1)} %get-tuple-element.17.refs_1_, f32[8,64,128]{2,1,0:T(8,128)S(1)} %get-tuple-element.18.refs_2_, bf16[128,32]{1,0:T(8,128)(2,1)S(1)} %get-tuple-element.19.refs_3_, ...), custom_call_target="tpu_custom_call" | custom-call | flops 6553600 | bytes 49152 | tf_op jit(solution)/shard_map/pallas_call | solution.py:467
  12.8 0.5 %shard_map.89 = (f32[9,128,128]{2,1,0:T(8,128)S(1)}, f32[11,64,128]{2,1,0:T(8,128)S(1)}) custom-call(f32[2,24,128]{2,1,0:T(8,128)S(1)} %collective-permute-done.2.refs_0_, f32[6,128,128]{2,1,0:T(8,128)S(1)} %get-tuple-element.17.refs_1_, f32[8,64,128]{2,1,0:T(8,128)S(1)} %get-tuple-element.18.refs_2_, bf16[128,32]{1,0:T(8,128)(2,1)S(1)} %get-tuple-element.19.refs_3_, ...), custom_call_target="tpu_custom_call" | custom-call | flops 3276800 | bytes 24576 | tf_op jit(solution)/shard_map/pallas_call | solution.py:467
  13.3 0.3 %collective-permute-done.3 = f32[2,24,128]{2,1,0:T(8,128)S(1)} collective-permute-done((f32[2,24,128]{2,1,0:T(8,128)S(1)}, f32[2,24,128]{2,1,0:T(8,128)S(1)}, u32[]{:S(2)}, u32[]{:S(2)}) %collective-permute-start.3) | collective-permute-done | bytes 24608 | tf_op jit(solution)/shard_map/ppermute | solution.py:464
  13.7 0.2 %collective-permute-start.5 = (f32[4,24,128]{2,1,0:T(8,128)S(1)}, f32[4,24,128]{2,1,0:T(8,128)S(1)}, u32[]{:S(2)}, u32[]{:S(2)}) collective-permute-start(f32[4,24,128]{2,1,0:T(8,128)S(1)} %pad_maximum_fusion.2), channel_id=1, source_target_pairs={{0,1},{1,0},{2,3},{3,2},{4,5},{5,4},{6,7},{7,6},{8,9},{9,8},{10,11... | collective-permute-start | bytes 147464 | tf_op jit(solution)/shard_map/ppermute | solution.py:464
  13.8 0.0 collective-permute-done.4
  13.9 1.2 %shard_map.90 = (f32[9,128,128]{2,1,0:T(8,128)S(1)}, f32[11,64,128]{2,1,0:T(8,128)S(1)}) custom-call(f32[6,24,128]{2,1,0:T(8,128)S(1)} %pad_maximum_fusion.refs_0_, f32[6,128,128]{2,1,0:T(8,128)S(1)} %get-tuple-element.17.refs_1_, f32[8,64,128]{2,1,0:T(8,128)S(1)} %get-tuple-element.18.refs_2_, bf16[128,32]{1,0:T(8,128)(2,1)S(1)} %get-tuple-element.19.refs_3_, ...), custom_call_target="tpu_custom_call" | custom-call | flops 9830400 | bytes 73728 | tf_op jit(solution)/shard_map/pallas_call | solution.py:467
  15.1 0.0 collective-permute-done.5
  15.1 2.1 %shard_map.91 = (f32[6,128]{1,0:T(8,128)}, f32[3,64]{1,0:T(4,128)}) custom-call(f32[16,24,128]{2,1,0:T(8,128)S(1)} %constant_dynamic-update-slice_fusion.refs_0_, f32[6,128,128]{2,1,0:T(8,128)S(1)} %get-tuple-element.17.refs_1_, f32[8,64,128]{2,1,0:T(8,128)S(1)} %get-tuple-element.18.refs_2_, bf16[128,32]{1,0:T(8,128)(2,1)S(1)} %get-tuple-element.19.refs_3_, ...), custom_call_target="tpu_custom_call" | custom-call | flops 6553600 | bytes 49152 | tf_op jit(solution)/shard_map/pallas_call | solution.py:491
  (11 shorter events, 0.0 us)
Async XLA Ops:
  1.5 4.9 %collective-permute-start = (f32[1,24,128]{2,1,0:T(8,128)S(1)}, f32[1,24,128]{2,1,0:T(8,128)S(1)}, u32[]{:S(2)}, u32[]{:S(2)}) collective-permute-start(f32[1,24,128]{2,1,0:T(8,128)S(1)} %bitcast.2), channel_id=1, source_target_pairs={{0,9},{1,8},{2,11},{3,10},{4,13},{5,12},{6,15},{7,14},{8,1},{9,0},... | collective-permute-start | bytes 36872 | tf_op jit(solution)/shard_map/ppermute | solution.py:464
  6.5 3.4 %collective-permute-start.1 = (f32[2,24,128]{2,1,0:T(8,128)S(1)}, f32[2,24,128]{2,1,0:T(8,128)S(1)}, u32[]{:S(2)}, u32[]{:S(2)}) collective-permute-start(f32[2,24,128]{2,1,0:T(8,128)S(1)} %pad_maximum_fusion.3), channel_id=1, source_target_pairs={{0,5},{1,4},{2,7},{3,6},{4,1},{5,0},{6,3},{7,2},{8,13},{9,12},{10,... | collective-permute-start | bytes 73736 | tf_op jit(solution)/shard_map/ppermute | solution.py:464
  8.4 3.6 %collective-permute-start.2 = (f32[2,24,128]{2,1,0:T(8,128)S(1)}, f32[2,24,128]{2,1,0:T(8,128)S(1)}, u32[]{:S(2)}, u32[]{:S(2)}) collective-permute-start(f32[2,24,128]{2,1,0:T(8,128)S(1)} %pad_maximum_fusion.3), channel_id=1, source_target_pairs={{0,3},{1,2},{2,1},{3,0},{4,7},{5,6},{6,5},{7,4},{8,11},{9,10},{10,... | collective-permute-start | bytes 73736 | tf_op jit(solution)/shard_map/ppermute | solution.py:464
  9.9 3.9 %collective-permute-start.4 = (f32[4,24,128]{2,1,0:T(8,128)S(1)}, f32[4,24,128]{2,1,0:T(8,128)S(1)}, u32[]{:S(2)}, u32[]{:S(2)}) collective-permute-start(f32[4,24,128]{2,1,0:T(8,128)S(1)} %pad_maximum_fusion.1.refs_0_), channel_id=1, source_target_pairs={{0,1},{1,0},{2,3},{3,2},{4,5},{5,4},{6,7},{7,6},{8,9},{9,8},{10,11... | collective-permute-start | bytes 147464 | tf_op jit(solution)/shard_map/ppermute | solution.py:464
  10.4 3.3 %collective-permute-start.3 = (f32[2,24,128]{2,1,0:T(8,128)S(1)}, f32[2,24,128]{2,1,0:T(8,128)S(1)}, u32[]{:S(2)}, u32[]{:S(2)}) collective-permute-start(f32[2,24,128]{2,1,0:T(8,128)S(1)} %collective-permute-done.1), channel_id=1, source_target_pairs={{0,3},{1,2},{2,1},{3,0},{4,7},{5,6},{6,5},{7,4},{8,11},{9,10},{10,... | collective-permute-start | bytes 73736 | tf_op jit(solution)/shard_map/ppermute | solution.py:464
  13.7 1.5 %collective-permute-start.5 = (f32[4,24,128]{2,1,0:T(8,128)S(1)}, f32[4,24,128]{2,1,0:T(8,128)S(1)}, u32[]{:S(2)}, u32[]{:S(2)}) collective-permute-start(f32[4,24,128]{2,1,0:T(8,128)S(1)} %pad_maximum_fusion.2), channel_id=1, source_target_pairs={{0,1},{1,0},{2,3},{3,2},{4,5},{5,4},{6,7},{7,6},{8,9},{9,8},{10,11... | collective-permute-start | bytes 147464 | tf_op jit(solution)/shard_map/ppermute | solution.py:464

commit v14 on v10

--- a/solution.py
+++ b/solution.py
@@ -13,8 +13,8 @@
 
 LANES = 128
 ROWS = 24
-CHUNK = 64
-FINISH = 32
+CHUNK = 16
+FINISH = 16
 VMEM = pl.BlockSpec(memory_space=pltpu.VMEM)
 
 
@@ -392,8 +392,8 @@
 
     found = []
     pair_sums(
-        data_ref, own_refs, count - count // 4, count, own_seg, scratch, old1_ref, old2_ref, new1_ref, new2_ref,
-        lambda: found.extend((*edge_sums(), receiver_totals(new1_ref, own_refs[0]))))
+        data_ref, own_refs, count - count // 4, count, own_seg, scratch, old1_ref, old2_ref, new1_ref, new2_ref)
+    found.extend((*edge_sums(), receiver_totals(new1_ref, own_refs[0])))
     edge_point, edge_normal, arriving, leaving, totals = found
     for axis in range(3):
         value = totals[axis : axis + 1] + edge_point[axis]

time: 17.2 us -> 17.2 us (level)
  no operation moved by 1% of the time
where the time goes in v14:
time: 17.2 us; the launch traced here: 17.1 us
  starting transfers between devices  9.2 us (53%)
  Pallas kernels  6.11 us (36%)
  waiting for transfers between devices  1.01 us (6%)
  between operations  0.69 us (4%)
    ppermute x6, starting transfers between devices, exchange(): return lax.ppermute(block, 'src', [(s, s ^ mask) for s in range(count)])  9.2 us
    pallas_call x3, Pallas kernels, add_pairs(): pl.pallas_call(functools.partial(early_kernel, len(sums) > 0, own_seg), o...  2.46 us
    pallas_call x1, Pallas kernels, on_device(): pl.pallas_call(functools.partial(last_kernel, count, own_seg), out_shape=...  2.09 us
    ppermute x6, waiting for transfers between devices, exchange(): return lax.ppermute(block, 'src', [(s, s ^ mask) for s in range(count)])  1.01 us
    pallas_call x1, Pallas kernels, on_device(): pl.pallas_call(functools.partial(pack_kernel, own_seg), out_shape=pltpu.V...  0.92 us
    pallas_call x1, Pallas kernels, on_device(): pl.pallas_call(functools.partial(own_kernel, own_seg), out_shape=(pltpu.V...  0.64 us
  transfers between devices with their start and end apart: 6, of which 2 were waited for; matrix products, arithmetic and copies ran while one was open for 0% of the time, Pallas kernels for 18%

profile of v14, /device:TPU:0, one launch (start us, length us, event | category | flops | bytes accessed | tf_op | source)
XLA Modules:
  0.0 17.1 jit_solution(11777563006502133785)
XLA Ops:
  0.6 0.9 %shard_map.86 = f32[24,128]{1,0:T(8,128)S(1)} custom-call(f32[3,128]{1,0:T(4,128)} %points_ref.1, f32[3,128]{1,0:T(4,128)} %normals_ref.1, f32[8,128]{1,0:T(8,128)} %left_ref.1, f32[3,64]{1,0:T(4,128)} %vertices_ref.1, s32[2,128]{1,0:T(2,128)} %connect_ref.1, f32[8,128]{1,0:T(8,128)} %right_ref.1, f32[8]{0:T(128)} %weights_ref.1), custom_call_target="tpu_custom_call" | custom-call | tf_op jit(solution)/shard_map/pallas_call | solution.py:440
  1.5 3.5 %collective-permute-start = (f32[1,24,128]{2,1,0:T(8,128)S(1)}, f32[1,24,128]{2,1,0:T(8,128)S(1)}, u32[]{:S(2)}, u32[]{:S(2)}) collective-permute-start(f32[1,24,128]{2,1,0:T(8,128)S(1)} %bitcast.2), channel_id=1, source_target_pairs={{0,9},{1,8},{2,11},{3,10},{4,13},{5,12},{6,15},{7,14},{8,1},{9,0},... | collective-permute-start | bytes 36872 | tf_op jit(solution)/shard_map/ppermute | solution.py:464
  5.1 0.6 %shard_map.87 = (f32[6,128,128]{2,1,0:T(8,128)S(1)}, f32[8,64,128]{2,1,0:T(8,128)S(1)}, bf16[128,32]{1,0:T(8,128)(2,1)S(1)}, bf16[64,32]{1,0:T(8,128)(2,1)S(1)},...) custom-call(f32[1,24,128]{2,1,0:T(8,128)S(1)} %bitcast.3), custom_call_target="tpu_custom_call" | custom-call | flops 3276800 | bytes 24576 | tf_op jit(solution)/shard_map/pallas_call | solution.py:447
  5.7 0.8 %collective-permute-done = f32[1,24,128]{2,1,0:T(8,128)S(1)} collective-permute-done((f32[1,24,128]{2,1,0:T(8,128)S(1)}, f32[1,24,128]{2,1,0:T(8,128)S(1)}, u32[]{:S(2)}, u32[]{:S(2)}) %collective-permute-start) | collective-permute-done | bytes 12320 | tf_op jit(solution)/shard_map/ppermute | solution.py:464
  6.5 1.9 %collective-permute-start.1 = (f32[2,24,128]{2,1,0:T(8,128)S(1)}, f32[2,24,128]{2,1,0:T(8,128)S(1)}, u32[]{:S(2)}, u32[]{:S(2)}) collective-permute-start(f32[2,24,128]{2,1,0:T(8,128)S(1)} %pad_maximum_fusion.1), channel_id=1, source_target_pairs={{0,5},{1,4},{2,7},{3,6},{4,1},{5,0},{6,3},{7,2},{8,13},{9,12},{10,... | collective-permute-start | bytes 73736 | tf_op jit(solution)/shard_map/ppermute | solution.py:464
  8.4 1.6 %collective-permute-start.2 = (f32[2,24,128]{2,1,0:T(8,128)S(1)}, f32[2,24,128]{2,1,0:T(8,128)S(1)}, u32[]{:S(2)}, u32[]{:S(2)}) collective-permute-start(f32[2,24,128]{2,1,0:T(8,128)S(1)} %pad_maximum_fusion.1), channel_id=1, source_target_pairs={{0,3},{1,2},{2,1},{3,0},{4,7},{5,6},{6,5},{7,4},{8,11},{9,10},{10,... | collective-permute-start | bytes 73736 | tf_op jit(solution)/shard_map/ppermute | solution.py:464
  9.9 0.0 collective-permute-done.1
  9.9 0.5 %collective-permute-start.4 = (f32[4,24,128]{2,1,0:T(8,128)S(1)}, f32[4,24,128]{2,1,0:T(8,128)S(1)}, u32[]{:S(2)}, u32[]{:S(2)}) collective-permute-start(f32[4,24,128]{2,1,0:T(8,128)S(1)} %pad_maximum_fusion.refs_0_), channel_id=1, source_target_pairs={{0,1},{1,0},{2,3},{3,2},{4,5},{5,4},{6,7},{7,6},{8,9},{9,8},{10,11... | collective-permute-start | bytes 147464 | tf_op jit(solution)/shard_map/ppermute | solution.py:464
  10.4 1.6 %collective-permute-start.3 = (f32[2,24,128]{2,1,0:T(8,128)S(1)}, f32[2,24,128]{2,1,0:T(8,128)S(1)}, u32[]{:S(2)}, u32[]{:S(2)}) collective-permute-start(f32[2,24,128]{2,1,0:T(8,128)S(1)} %collective-permute-done.1), channel_id=1, source_target_pairs={{0,3},{1,2},{2,1},{3,0},{4,7},{5,6},{6,5},{7,4},{8,11},{9,10},{10,... | collective-permute-start | bytes 73736 | tf_op jit(solution)/shard_map/ppermute | solution.py:464
  12.0 0.0 collective-permute-done.2
  12.0 0.8 %shard_map.88 = (f32[9,128,128]{2,1,0:T(8,128)S(1)}, f32[11,64,128]{2,1,0:T(8,128)S(1)}) custom-call(f32[4,24,128]{2,1,0:T(8,128)S(1)} %pad_maximum_fusion.refs_0_, f32[6,128,128]{2,1,0:T(8,128)S(1)} %get-tuple-element.17.refs_1_, f32[8,64,128]{2,1,0:T(8,128)S(1)} %get-tuple-element.18.refs_2_, bf16[128,32]{1,0:T(8,128)(2,1)S(1)} %get-tuple-element.19.refs_3_, ...), custom_call_target="tpu_custom_call" | custom-call | flops 6553600 | bytes 49152 | tf_op jit(solution)/shard_map/pallas_call | solution.py:467
  12.8 0.0 collective-permute-done.4.refs_0_
  12.8 0.8 %shard_map.89 = (f32[9,128,128]{2,1,0:T(8,128)S(1)}, f32[11,64,128]{2,1,0:T(8,128)S(1)}) custom-call(f32[4,24,128]{2,1,0:T(8,128)S(1)} %collective-permute-done.4.refs_0_, f32[6,128,128]{2,1,0:T(8,128)S(1)} %get-tuple-element.17.refs_1_, f32[8,64,128]{2,1,0:T(8,128)S(1)} %get-tuple-element.18.refs_2_, bf16[128,32]{1,0:T(8,128)(2,1)S(1)} %get-tuple-element.19.refs_3_, ...), custom_call_target="tpu_custom_call" | custom-call | flops 6553600 | bytes 49152 | tf_op jit(solution)/shard_map/pallas_call | solution.py:467
  13.6 0.0 collective-permute-done.3
  13.7 0.2 %collective-permute-start.5 = (f32[4,24,128]{2,1,0:T(8,128)S(1)}, f32[4,24,128]{2,1,0:T(8,128)S(1)}, u32[]{:S(2)}, u32[]{:S(2)}) collective-permute-start(f32[4,24,128]{2,1,0:T(8,128)S(1)} %get-tuple-element.32.refs_0_), channel_id=1, source_target_pairs={{0,1},{1,0},{2,3},{3,2},{4,5},{5,4},{6,7},{7,6},{8,9},{9,8},{10,11... | collective-permute-start | bytes 147464 | tf_op jit(solution)/shard_map/ppermute | solution.py:464
  13.9 0.8 %shard_map.90 = (f32[9,128,128]{2,1,0:T(8,128)S(1)}, f32[11,64,128]{2,1,0:T(8,128)S(1)}) custom-call(f32[4,24,128]{2,1,0:T(8,128)S(1)} %get-tuple-element.32.refs_0_, f32[6,128,128]{2,1,0:T(8,128)S(1)} %get-tuple-element.17.refs_1_, f32[8,64,128]{2,1,0:T(8,128)S(1)} %get-tuple-element.18.refs_2_, bf16[128,32]{1,0:T(8,128)(2,1)S(1)} %get-tuple-element.19.refs_3_, ...), custom_call_target="tpu_custom_call" | custom-call | flops 6553600 | bytes 49152 | tf_op jit(solution)/shard_map/pallas_call | solution.py:467
  14.7 0.2 %collective-permute-done.5 = f32[4,24,128]{2,1,0:T(8,128)S(1)} collective-permute-done((f32[4,24,128]{2,1,0:T(8,128)S(1)}, f32[4,24,128]{2,1,0:T(8,128)S(1)}, u32[]{:S(2)}, u32[]{:S(2)}) %collective-permute-start.5) | collective-permute-done | bytes 49184 | tf_op jit(solution)/shard_map/ppermute | solution.py:464
  15.0 2.1 %shard_map.91 = (f32[6,128]{1,0:T(8,128)}, f32[3,64]{1,0:T(4,128)}) custom-call(f32[16,24,128]{2,1,0:T(8,128)S(1)} %constant_dynamic-update-slice_fusion.2.refs_0_, f32[6,128,128]{2,1,0:T(8,128)S(1)} %get-tuple-element.17.refs_1_, f32[8,64,128]{2,1,0:T(8,128)S(1)} %get-tuple-element.18.refs_2_, bf16[128,32]{1,0:T(8,128)(2,1)S(1)} %get-tuple-element.19.refs_3_, ...), custom_call_target="tpu_custom_call" | custom-call | flops 6553600 | bytes 49152 | tf_op jit(solution)/shard_map/pallas_call | solution.py:491
  (9 shorter events, 0.0 us)
Async XLA Ops:
  1.5 4.9 %collective-permute-start = (f32[1,24,128]{2,1,0:T(8,128)S(1)}, f32[1,24,128]{2,1,0:T(8,128)S(1)}, u32[]{:S(2)}, u32[]{:S(2)}) collective-permute-start(f32[1,24,128]{2,1,0:T(8,128)S(1)} %bitcast.2), channel_id=1, source_target_pairs={{0,9},{1,8},{2,11},{3,10},{4,13},{5,12},{6,15},{7,14},{8,1},{9,0},... | collective-permute-start | bytes 36872 | tf_op jit(solution)/shard_map/ppermute | solution.py:464
  6.5 3.4 %collective-permute-start.1 = (f32[2,24,128]{2,1,0:T(8,128)S(1)}, f32[2,24,128]{2,1,0:T(8,128)S(1)}, u32[]{:S(2)}, u32[]{:S(2)}) collective-permute-start(f32[2,24,128]{2,1,0:T(8,128)S(1)} %pad_maximum_fusion.1), channel_id=1, source_target_pairs={{0,5},{1,4},{2,7},{3,6},{4,1},{5,0},{6,3},{7,2},{8,13},{9,12},{10,... | collective-permute-start | bytes 73736 | tf_op jit(solution)/shard_map/ppermute | solution.py:464
  8.4 3.6 %collective-permute-start.2 = (f32[2,24,128]{2,1,0:T(8,128)S(1)}, f32[2,24,128]{2,1,0:T(8,128)S(1)}, u32[]{:S(2)}, u32[]{:S(2)}) collective-permute-start(f32[2,24,128]{2,1,0:T(8,128)S(1)} %pad_maximum_fusion.1), channel_id=1, source_target_pairs={{0,3},{1,2},{2,1},{3,0},{4,7},{5,6},{6,5},{7,4},{8,11},{9,10},{10,... | collective-permute-start | bytes 73736 | tf_op jit(solution)/shard_map/ppermute | solution.py:464
  9.9 2.8 %collective-permute-start.4 = (f32[4,24,128]{2,1,0:T(8,128)S(1)}, f32[4,24,128]{2,1,0:T(8,128)S(1)}, u32[]{:S(2)}, u32[]{:S(2)}) collective-permute-start(f32[4,24,128]{2,1,0:T(8,128)S(1)} %pad_maximum_fusion.refs_0_), channel_id=1, source_target_pairs={{0,1},{1,0},{2,3},{3,2},{4,5},{5,4},{6,7},{7,6},{8,9},{9,8},{10,11... | collective-permute-start | bytes 147464 | tf_op jit(solution)/shard_map/ppermute | solution.py:464
  10.4 3.3 %collective-permute-start.3 = (f32[2,24,128]{2,1,0:T(8,128)S(1)}, f32[2,24,128]{2,1,0:T(8,128)S(1)}, u32[]{:S(2)}, u32[]{:S(2)}) collective-permute-start(f32[2,24,128]{2,1,0:T(8,128)S(1)} %collective-permute-done.1), channel_id=1, source_target_pairs={{0,3},{1,2},{2,1},{3,0},{4,7},{5,6},{6,5},{7,4},{8,11},{9,10},{10,... | collective-permute-start | bytes 73736 | tf_op jit(solution)/shard_map/ppermute | solution.py:464
  13.7 1.3 %collective-permute-start.5 = (f32[4,24,128]{2,1,0:T(8,128)S(1)}, f32[4,24,128]{2,1,0:T(8,128)S(1)}, u32[]{:S(2)}, u32[]{:S(2)}) collective-permute-start(f32[4,24,128]{2,1,0:T(8,128)S(1)} %get-tuple-element.32.refs_0_), channel_id=1, source_target_pairs={{0,1},{1,0},{2,3},{3,2},{4,5},{5,4},{6,7},{7,6},{8,9},{9,8},{10,11... | collective-permute-start | bytes 147464 | tf_op jit(solution)/shard_map/ppermute | solution.py:464

commit v15 on v10

--- a/solution.py
+++ b/solution.py
@@ -24,7 +24,7 @@
     while step > 1:
         masks.append(step + 1)
         step //= 2
-    return masks + [1]
+    return masks[:-2] + [masks[-1], masks[-2], 1]
 
 
 def mask_at(place, masks):

time: 17.2 us -> 17.3 us (level)
  no operation moved by 1% of the time
where the time goes in v15:
time: 17.3 us; the launch traced here: 17.1 us
  starting transfers between devices  9.26 us (54%)
  Pallas kernels  6.1 us (35%)
  waiting for transfers between devices  1.01 us (6%)
  between operations  0.7 us (4%)
    ppermute x6, starting transfers between devices, exchange(): return lax.ppermute(block, 'src', [(s, s ^ mask) for s in range(count)])  9.26 us
    pallas_call x3, Pallas kernels, add_pairs(): pl.pallas_call(functools.partial(early_kernel, len(sums) > 0, own_seg), o...  2.44 us
    pallas_call x1, Pallas kernels, on_device(): pl.pallas_call(functools.partial(last_kernel, count, own_seg), out_shape=...  2.09 us
    ppermute x6, waiting for transfers between devices, exchange(): return lax.ppermute(block, 'src', [(s, s ^ mask) for s in range(count)])  1.01 us
    pallas_call x1, Pallas kernels, on_device(): pl.pallas_call(functools.partial(pack_kernel, own_seg), out_shape=pltpu.V...  0.92 us
    pallas_call x1, Pallas kernels, on_device(): pl.pallas_call(functools.partial(own_kernel, own_seg), out_shape=(pltpu.V...  0.64 us
  transfers between devices with their start and end apart: 6, of which 2 were waited for; matrix products, arithmetic and copies ran while one was open for 0% of the time, Pallas kernels for 18%

profile of v15, /device:TPU:0, one launch (start us, length us, event | category | flops | bytes accessed | tf_op | source)
XLA Modules:
  0.0 17.1 jit_solution(8003787219681779415)
XLA Ops:
  0.6 0.9 %shard_map.86 = f32[24,128]{1,0:T(8,128)S(1)} custom-call(f32[3,128]{1,0:T(4,128)} %points_ref.1, f32[3,128]{1,0:T(4,128)} %normals_ref.1, f32[8,128]{1,0:T(8,128)} %left_ref.1, f32[3,64]{1,0:T(4,128)} %vertices_ref.1, s32[2,128]{1,0:T(2,128)} %connect_ref.1, f32[8,128]{1,0:T(8,128)} %right_ref.1, f32[8]{0:T(128)} %weights_ref.1), custom_call_target="tpu_custom_call" | custom-call | tf_op jit(solution)/shard_map/pallas_call | solution.py:440
  1.5 3.5 %collective-permute-start = (f32[1,24,128]{2,1,0:T(8,128)S(1)}, f32[1,24,128]{2,1,0:T(8,128)S(1)}, u32[]{:S(2)}, u32[]{:S(2)}) collective-permute-start(f32[1,24,128]{2,1,0:T(8,128)S(1)} %bitcast.2), channel_id=1, source_target_pairs={{0,9},{1,8},{2,11},{3,10},{4,13},{5,12},{6,15},{7,14},{8,1},{9,0},... | collective-permute-start | bytes 36872 | tf_op jit(solution)/shard_map/ppermute | solution.py:464
  5.1 0.6 %shard_map.87 = (f32[6,128,128]{2,1,0:T(8,128)S(1)}, f32[8,64,128]{2,1,0:T(8,128)S(1)}, bf16[128,32]{1,0:T(8,128)(2,1)S(1)}, bf16[64,32]{1,0:T(8,128)(2,1)S(1)},...) custom-call(f32[1,24,128]{2,1,0:T(8,128)S(1)} %bitcast.3), custom_call_target="tpu_custom_call" | custom-call | flops 3276800 | bytes 24576 | tf_op jit(solution)/shard_map/pallas_call | solution.py:447
  5.7 0.8 %collective-permute-done = f32[1,24,128]{2,1,0:T(8,128)S(1)} collective-permute-done((f32[1,24,128]{2,1,0:T(8,128)S(1)}, f32[1,24,128]{2,1,0:T(8,128)S(1)}, u32[]{:S(2)}, u32[]{:S(2)}) %collective-permute-start) | collective-permute-done | bytes 12320 | tf_op jit(solution)/shard_map/ppermute | solution.py:464
  6.5 1.8 %collective-permute-start.1 = (f32[2,24,128]{2,1,0:T(8,128)S(1)}, f32[2,24,128]{2,1,0:T(8,128)S(1)}, u32[]{:S(2)}, u32[]{:S(2)}) collective-permute-start(f32[2,24,128]{2,1,0:T(8,128)S(1)} %pad_maximum_fusion.1), channel_id=1, source_target_pairs={{0,3},{1,2},{2,1},{3,0},{4,7},{5,6},{6,5},{7,4},{8,11},{9,10},{10,... | collective-permute-start | bytes 73736 | tf_op jit(solution)/shard_map/ppermute | solution.py:464
  8.3 1.6 %collective-permute-start.2 = (f32[2,24,128]{2,1,0:T(8,128)S(1)}, f32[2,24,128]{2,1,0:T(8,128)S(1)}, u32[]{:S(2)}, u32[]{:S(2)}) collective-permute-start(f32[2,24,128]{2,1,0:T(8,128)S(1)} %pad_maximum_fusion.1), channel_id=1, source_target_pairs={{0,5},{1,4},{2,7},{3,6},{4,1},{5,0},{6,3},{7,2},{8,13},{9,12},{10,... | collective-permute-start | bytes 73736 | tf_op jit(solution)/shard_map/ppermute | solution.py:464
  9.9 0.0 collective-permute-done.1
  9.9 0.5 %collective-permute-start.4 = (f32[4,24,128]{2,1,0:T(8,128)S(1)}, f32[4,24,128]{2,1,0:T(8,128)S(1)}, u32[]{:S(2)}, u32[]{:S(2)}) collective-permute-start(f32[4,24,128]{2,1,0:T(8,128)S(1)} %pad_maximum_fusion.refs_0_), channel_id=1, source_target_pairs={{0,1},{1,0},{2,3},{3,2},{4,5},{5,4},{6,7},{7,6},{8,9},{9,8},{10,11... | collective-permute-start | bytes 147464 | tf_op jit(solution)/shard_map/ppermute | solution.py:464
  10.4 1.6 %collective-permute-start.3 = (f32[2,24,128]{2,1,0:T(8,128)S(1)}, f32[2,24,128]{2,1,0:T(8,128)S(1)}, u32[]{:S(2)}, u32[]{:S(2)}) collective-permute-start(f32[2,24,128]{2,1,0:T(8,128)S(1)} %collective-permute-done.1), channel_id=1, source_target_pairs={{0,5},{1,4},{2,7},{3,6},{4,1},{5,0},{6,3},{7,2},{8,13},{9,12},{10,... | collective-permute-start | bytes 73736 | tf_op jit(solution)/shard_map/ppermute | solution.py:464
  12.0 0.0 collective-permute-done.2
  12.0 0.8 %shard_map.88 = (f32[9,128,128]{2,1,0:T(8,128)S(1)}, f32[11,64,128]{2,1,0:T(8,128)S(1)}) custom-call(f32[4,24,128]{2,1,0:T(8,128)S(1)} %pad_maximum_fusion.refs_0_, f32[6,128,128]{2,1,0:T(8,128)S(1)} %get-tuple-element.17.refs_1_, f32[8,64,128]{2,1,0:T(8,128)S(1)} %get-tuple-element.18.refs_2_, bf16[128,32]{1,0:T(8,128)(2,1)S(1)} %get-tuple-element.19.refs_3_, ...), custom_call_target="tpu_custom_call" | custom-call | flops 6553600 | bytes 49152 | tf_op jit(solution)/shard_map/pallas_call | solution.py:467
  12.8 0.0 collective-permute-done.4.refs_0_
  12.8 0.8 %shard_map.89 = (f32[9,128,128]{2,1,0:T(8,128)S(1)}, f32[11,64,128]{2,1,0:T(8,128)S(1)}) custom-call(f32[4,24,128]{2,1,0:T(8,128)S(1)} %collective-permute-done.4.refs_0_, f32[6,128,128]{2,1,0:T(8,128)S(1)} %get-tuple-element.17.refs_1_, f32[8,64,128]{2,1,0:T(8,128)S(1)} %get-tuple-element.18.refs_2_, bf16[128,32]{1,0:T(8,128)(2,1)S(1)} %get-tuple-element.19.refs_3_, ...), custom_call_target="tpu_custom_call" | custom-call | flops 6553600 | bytes 49152 | tf_op jit(solution)/shard_map/pallas_call | solution.py:467
  13.7 0.0 collective-permute-done.3
  13.7 0.2 %collective-permute-start.5 = (f32[4,24,128]{2,1,0:T(8,128)S(1)}, f32[4,24,128]{2,1,0:T(8,128)S(1)}, u32[]{:S(2)}, u32[]{:S(2)}) collective-permute-start(f32[4,24,128]{2,1,0:T(8,128)S(1)} %get-tuple-element.32.refs_0_), channel_id=1, source_target_pairs={{0,1},{1,0},{2,3},{3,2},{4,5},{5,4},{6,7},{7,6},{8,9},{9,8},{10,11... | collective-permute-start | bytes 147464 | tf_op jit(solution)/shard_map/ppermute | solution.py:464
  13.9 0.8 %shard_map.90 = (f32[9,128,128]{2,1,0:T(8,128)S(1)}, f32[11,64,128]{2,1,0:T(8,128)S(1)}) custom-call(f32[4,24,128]{2,1,0:T(8,128)S(1)} %get-tuple-element.32.refs_0_, f32[6,128,128]{2,1,0:T(8,128)S(1)} %get-tuple-element.17.refs_1_, f32[8,64,128]{2,1,0:T(8,128)S(1)} %get-tuple-element.18.refs_2_, bf16[128,32]{1,0:T(8,128)(2,1)S(1)} %get-tuple-element.19.refs_3_, ...), custom_call_target="tpu_custom_call" | custom-call | flops 6553600 | bytes 49152 | tf_op jit(solution)/shard_map/pallas_call | solution.py:467
  14.8 0.2 %collective-permute-done.5 = f32[4,24,128]{2,1,0:T(8,128)S(1)} collective-permute-done((f32[4,24,128]{2,1,0:T(8,128)S(1)}, f32[4,24,128]{2,1,0:T(8,128)S(1)}, u32[]{:S(2)}, u32[]{:S(2)}) %collective-permute-start.5) | collective-permute-done | bytes 49184 | tf_op jit(solution)/shard_map/ppermute | solution.py:464
  15.0 2.1 %shard_map.91 = (f32[6,128]{1,0:T(8,128)}, f32[3,64]{1,0:T(4,128)}) custom-call(f32[16,24,128]{2,1,0:T(8,128)S(1)} %constant_dynamic-update-slice_fusion.2.refs_0_, f32[6,128,128]{2,1,0:T(8,128)S(1)} %get-tuple-element.17.refs_1_, f32[8,64,128]{2,1,0:T(8,128)S(1)} %get-tuple-element.18.refs_2_, bf16[128,32]{1,0:T(8,128)(2,1)S(1)} %get-tuple-element.19.refs_3_, ...), custom_call_target="tpu_custom_call" | custom-call | flops 6553600 | bytes 49152 | tf_op jit(solution)/shard_map/pallas_call | solution.py:491
  (9 shorter events, 0.0 us)
Async XLA Ops:
  1.5 4.9 %collective-permute-start = (f32[1,24,128]{2,1,0:T(8,128)S(1)}, f32[1,24,128]{2,1,0:T(8,128)S(1)}, u32[]{:S(2)}, u32[]{:S(2)}) collective-permute-start(f32[1,24,128]{2,1,0:T(8,128)S(1)} %bitcast.2), channel_id=1, source_target_pairs={{0,9},{1,8},{2,11},{3,10},{4,13},{5,12},{6,15},{7,14},{8,1},{9,0},... | collective-permute-start | bytes 36872 | tf_op jit(solution)/shard_map/ppermute | solution.py:464
  6.5 3.4 %collective-permute-start.1 = (f32[2,24,128]{2,1,0:T(8,128)S(1)}, f32[2,24,128]{2,1,0:T(8,128)S(1)}, u32[]{:S(2)}, u32[]{:S(2)}) collective-permute-start(f32[2,24,128]{2,1,0:T(8,128)S(1)} %pad_maximum_fusion.1), channel_id=1, source_target_pairs={{0,3},{1,2},{2,1},{3,0},{4,7},{5,6},{6,5},{7,4},{8,11},{9,10},{10,... | collective-permute-start | bytes 73736 | tf_op jit(solution)/shard_map/ppermute | solution.py:464
  8.3 3.7 %collective-permute-start.2 = (f32[2,24,128]{2,1,0:T(8,128)S(1)}, f32[2,24,128]{2,1,0:T(8,128)S(1)}, u32[]{:S(2)}, u32[]{:S(2)}) collective-permute-start(f32[2,24,128]{2,1,0:T(8,128)S(1)} %pad_maximum_fusion.1), channel_id=1, source_target_pairs={{0,5},{1,4},{2,7},{3,6},{4,1},{5,0},{6,3},{7,2},{8,13},{9,12},{10,... | collective-permute-start | bytes 73736 | tf_op jit(solution)/shard_map/ppermute | solution.py:464
  9.9 2.9 %collective-permute-start.4 = (f32[4,24,128]{2,1,0:T(8,128)S(1)}, f32[4,24,128]{2,1,0:T(8,128)S(1)}, u32[]{:S(2)}, u32[]{:S(2)}) collective-permute-start(f32[4,24,128]{2,1,0:T(8,128)S(1)} %pad_maximum_fusion.refs_0_), channel_id=1, source_target_pairs={{0,1},{1,0},{2,3},{3,2},{4,5},{5,4},{6,7},{7,6},{8,9},{9,8},{10,11... | collective-permute-start | bytes 147464 | tf_op jit(solution)/shard_map/ppermute | solution.py:464
  10.4 3.3 %collective-permute-start.3 = (f32[2,24,128]{2,1,0:T(8,128)S(1)}, f32[2,24,128]{2,1,0:T(8,128)S(1)}, u32[]{:S(2)}, u32[]{:S(2)}) collective-permute-start(f32[2,24,128]{2,1,0:T(8,128)S(1)} %collective-permute-done.1), channel_id=1, source_target_pairs={{0,5},{1,4},{2,7},{3,6},{4,1},{5,0},{6,3},{7,2},{8,13},{9,12},{10,... | collective-permute-start | bytes 73736 | tf_op jit(solution)/shard_map/ppermute | solution.py:464
  13.7 1.3 %collective-permute-start.5 = (f32[4,24,128]{2,1,0:T(8,128)S(1)}, f32[4,24,128]{2,1,0:T(8,128)S(1)}, u32[]{:S(2)}, u32[]{:S(2)}) collective-permute-start(f32[4,24,128]{2,1,0:T(8,128)S(1)} %get-tuple-element.32.refs_0_), channel_id=1, source_target_pairs={{0,1},{1,0},{2,3},{3,2},{4,5},{5,4},{6,7},{7,6},{8,9},{9,8},{10,11... | collective-permute-start | bytes 147464 | tf_op jit(solution)/shard_map/ppermute | solution.py:464
